TPU v7x, 32 devices: a whole 2x2x4 slice. The times are simulated.
32 devices in a mesh: ctx: 16 (over z, y, x), head: 2 (over core).
Axes of the slice: x: 2, y: 2, z: 4, core: 2. Of those that a mesh axis runs over, the one named last changes fastest.
Arguments:
- queries: bfloat16 [6144, 4096], P('ctx', 'head'), may hold values from -6 to 6
- key_heads: bfloat16 [6144, 1024], P('ctx', 'head'), may hold values from -5 to 5
- value_heads: bfloat16 [6144, 1024], P('ctx', 'head'), may hold values from -6 to 6
- doc_units: int32 [6], replicated, may hold values from 1 to 24, as said below
- w_out: bfloat16 [4096, 4096], P('head'), may hold values from -0.09375 to 0.09375
Outputs:
- layer_out: bfloat16 [6144, 4096], P(('ctx', 'head'))
Inputs may be any that keep to these rules, and one draw needn't show every extreme that they name: `doc_units`: the lengths, in units of 128 tokens, of the 6 documents laid end to end; they sum to 48; exactly one document has 24 units, it covers token 3072, and every other one has at most 12.
All inputs are finite; a program needn't handle non-finite values.
Results may differ from a plain program's by a relative error of at most 0.018.
Values may be sent and summed in bfloat16 or wider, within the bound.
No kernel may reach another device: no remote copies, remote signals or barrier semaphores. Data moves between devices by JAX's collectives and lax.ppermute only.
A program may use at most 64 MiB of HBM per device.

v0:
```python
from functools import partial
import math

import jax
import jax.numpy as jnp
from jax import lax
from jax.experimental import pallas as pl
from jax.experimental.pallas import tpu as pltpu
from jax.sharding import PartitionSpec as P

HD = 128
UNIT = 128
CHUNK_UNITS = 4
LOW = -1e30
LARGE = 2.0**90
VMEM_LIMIT = 24 * 1024 * 1024
HBM = pl.BlockSpec(memory_space=pl.ANY)
SMEM = pl.BlockSpec(memory_space=pltpu.SMEM)
VMEM = pl.BlockSpec(memory_space=pltpu.VMEM)


def params():
    return pltpu.CompilerParams(vmem_limit_bytes=VMEM_LIMIT)


def run_copies(copies):
    for copy in copies:
        copy.start()
    for copy in copies:
        copy.wait()


def attention_kernel(mode, steps, group, planes, heads, docs, *refs):
    refs = list(refs)

    def take(number):
        taken = refs[:number]
        del refs[:number]
        return taken

    pieces = len(steps)
    early, late = mode == "early", mode == "late"
    (docs_ref,) = take(1)
    queries = take(pieces)
    keys = take(planes)
    if early:
        (w_from,) = take(1)
    if late:
        (state,) = take(1)
        take(pieces)
    outs = take(pieces)
    if early:
        state, w_to = take(2)
    q_buf, kv_buf, o_buf, shift, total, in_sem, out_sem = refs
    tokens = queries[0].shape[0]
    units = tokens // UNIT
    plane_rows = keys[0].shape[0]
    plane_units = plane_rows // UNIT
    pad_units = CHUNK_UNITS - 1
    pad = pad_units * UNIT
    chunk = CHUNK_UNITS * UNIT
    rank = lax.axis_index("ctx")
    member = lax.rem(rank, group)
    first_unit = (rank - member) * units - (planes - 1) * plane_units
    unseen = pad_units + max(planes - 2, 0) * plane_units
    scale = math.log2(math.e) / math.sqrt(HD)

    def place(piece):
        here = (rank ^ (steps[0] - piece)) * units
        starts = []
        for unit in range(units):
            doc_first = jnp.int32(0)
            end = jnp.int32(0)
            for doc in range(docs):
                end = end + docs_ref[doc]
                doc_first = jnp.where(end <= here + unit, end, doc_first)
            starts.append(doc_first - first_unit + pad_units)
        return here - first_unit + pad_units, starts

    def load():
        copies = []
        for number in range(planes):
            for step in range(group):
                to = pl.multiple_of(pad + number * plane_rows + (member ^ step) * tokens, UNIT)
                copies.append(
                    pltpu.make_async_copy(
                        keys[number].at[pl.ds(step * tokens, tokens), :],
                        kv_buf.at[pl.ds(to, tokens), :],
                        in_sem.at[number * group + step],
                    )
                )
        for piece in range(pieces):
            copies.append(
                pltpu.make_async_copy(queries[piece], q_buf.at[piece], in_sem.at[planes * group + piece])
            )
        for copy in copies:
            copy.start()
        kv_buf[pl.ds(0, pad), :] = jnp.zeros((pad, 2 * HD), jnp.bfloat16)
        for copy in copies:
            copy.wait()

    def one_piece(piece):
        ones = jnp.ones((chunk, HD), jnp.bfloat16)
        square = jnp.ones((HD, HD), jnp.bfloat16)
        first_row, starts = place(piece)
        lows = [jnp.maximum(start, pad_units) for start in starts]
        low, high = lows[0], lows[-1]
        stop = jnp.int32(unseen) if late else first_row + units
        count = (stop - low + CHUNK_UNITS - 1) // CHUNK_UNITS
        whole = jnp.maximum((stop - high) // CHUNK_UNITS, 0 if late else 1)
        query = jnp.concatenate([q_buf[piece, :, head * HD:(head + 1) * HD] for head in range(heads)], axis=0)

        def scores_of(end, number, masked):
            begin_unit = end - (number + 1) * CHUNK_UNITS
            begin = pl.multiple_of(begin_unit * UNIT, UNIT)
            key = kv_buf[pl.ds(begin, chunk), :HD]
            value = jnp.concatenate([kv_buf[pl.ds(begin, chunk), HD:], ones], axis=1)
            scores = lax.dot_general(query, key, (((1,), (1,)), ((), ())), preferred_element_type=jnp.float32)
            if masked:
                column = lax.broadcasted_iota(jnp.int32, (UNIT, chunk), 1)
                ahead = column - lax.broadcasted_iota(jnp.int32, (UNIT, chunk), 0)
                allowed = [
                    (column >= (lows[unit] - begin_unit) * UNIT) & (ahead <= (first_row + unit - begin_unit) * UNIT)
                    for unit in range(units)
                ]
                scores = jnp.concatenate([
                    jnp.where(allowed[number % units], scores[number * UNIT:(number + 1) * UNIT], LOW)
                    for number in range(heads * units)
                ], axis=0)
            return scores, value

        own_key = kv_buf[pl.ds(pl.multiple_of(first_row * UNIT, UNIT), tokens), :HD]
        own = query * jnp.concatenate([own_key] * heads, axis=0)
        shift[...] = jnp.dot(own, square, preferred_element_type=jnp.float32) * scale

        def visit(number, masked, fresh=False):
            scores, value = scores_of(stop, number, masked)
            shifts = jnp.concatenate([shift[...]] * CHUNK_UNITS, axis=1)
            weights = jnp.exp2(scores * scale - shifts).astype(jnp.bfloat16)
            update = jnp.dot(weights, value, preferred_element_type=jnp.float32)
            if fresh:
                total[...] = update
            else:
                total[...] += update

        def masked_visit(number, inner):
            visit(number, True)
            return inner

        def plain_visit(number, inner):
            visit(number, False)
            return inner

        if late:
            total[...] = state[piece]
        else:
            visit(0, True, True)
        lax.fori_loop(0 if late else 1, whole, plain_visit, 0)
        lax.fori_loop(whole, count, masked_visit, 0)

        overflow = jnp.logical_not(jnp.max(total[:, HD:]) < LARGE)
        if early:
            unfinished = starts[0] < pad_units
            overflow = overflow & jnp.logical_not(unfinished)

            @pl.when(unfinished)
            def _():
                state[piece] = total[...]

        @pl.when(overflow)
        def _():
            shift[...] = jnp.full(shift.shape, LOW, jnp.float32)
            total[...] = jnp.zeros(total.shape, jnp.float32)

            def careful(number, inner):
                scores, value = scores_of(first_row + units, number, True)
                old = shift[...]
                new = jnp.maximum(old, jnp.max(scores, axis=1, keepdims=True))
                weights = jnp.exp2((scores - new[:, :1]) * scale).astype(jnp.bfloat16)
                shrink = jnp.exp2((old - new) * scale)
                update = jnp.dot(weights, value, preferred_element_type=jnp.float32)
                total[...] = total[...] * jnp.concatenate([shrink] * 2, axis=1) + update
                shift[...] = new
                return inner

            lax.fori_loop(0, (first_row + units - low + CHUNK_UNITS - 1) // CHUNK_UNITS, careful, 0)

        result = (total[:, :HD] / total[:, HD:]).astype(jnp.bfloat16)
        for head in range(heads):
            o_buf[piece, :, head * HD:(head + 1) * HD] = result[head * tokens:(head + 1) * tokens]

    if late:
        needed = [place(jnp.int32(piece))[1][0] < unseen for piece in range(pieces)]

        @pl.when(sum(need.astype(jnp.int32) for need in needed) > 0)
        def _():
            load()
            for piece in range(pieces):

                @pl.when(needed[piece])
                def _():
                    one_piece(piece)
                    copy = pltpu.make_async_copy(o_buf.at[piece], outs[piece], out_sem.at[piece])
                    copy.start()
                    copy.wait()
    else:
        if early:
            w_copy = pltpu.make_async_copy(w_from, w_to, out_sem.at[pieces])
            w_copy.start()
        load()

        def always(piece, carry):
            one_piece(piece)
            return carry

        lax.fori_loop(0, pieces, always, 0)
        run_copies([
            pltpu.make_async_copy(o_buf.at[piece], outs[piece], out_sem.at[piece]) for piece in range(pieces)
        ])
        if early:
            w_copy.wait()


def attend(mode, steps, doc_units, queries, planes, w_out=None, state=None, outs=None):
    pieces = len(steps)
    group = planes[0].shape[0] // queries[0].shape[0]
    tokens, width = queries[0].shape
    heads = width // HD
    plane_rows = planes[0].shape[0]
    rows = heads * tokens
    pad = (CHUNK_UNITS - 1) * UNIT
    scores = tokens * pieces * heads * plane_rows * (1 if mode == "late" else len(planes)) // 2
    operands = [doc_units, *queries, *planes]
    in_specs = [SMEM] + [HBM] * (len(operands) - 1)
    out_shape = [jax.ShapeDtypeStruct((tokens, width), jnp.bfloat16)] * pieces
    out_specs = [HBM] * pieces
    aliases = {}
    moved = 4 * tokens * pieces * width
    if mode == "early":
        operands += [w_out]
        in_specs += [HBM]
        out_shape += [pltpu.VMEM((pieces, rows, 2 * HD), jnp.float32), pltpu.VMEM(w_out.shape, w_out.dtype)]
        out_specs += [VMEM, VMEM]
        moved += 2 * w_out.size
    if mode == "late":
        aliases = {len(operands) + 1 + piece: piece for piece in range(pieces)}
        operands += [pltpu.with_memory_space_constraint(state, pltpu.VMEM), *outs]
        in_specs += [VMEM] + [HBM] * pieces
    return pl.pallas_call(
        partial(attention_kernel, mode, steps, group, len(planes), heads, doc_units.shape[0]),
        out_shape=out_shape,
        in_specs=in_specs,
        out_specs=out_specs,
        scratch_shapes=[
            pltpu.VMEM((pieces, tokens, width), jnp.bfloat16),
            pltpu.VMEM((pad + plane_rows * len(planes), 2 * HD), jnp.bfloat16),
            pltpu.VMEM((pieces, tokens, width), jnp.bfloat16),
            pltpu.VMEM((rows, HD), jnp.float32),
            pltpu.VMEM((rows, 2 * HD), jnp.float32),
            pltpu.SemaphoreType.DMA((pieces + group * len(planes),)),
            pltpu.SemaphoreType.DMA((pieces + 1,)),
        ],
        input_output_aliases=aliases,
        compiler_params=params(),
        cost_estimate=pl.CostEstimate(flops=4 * HD * scores, transcendentals=scores, bytes_accessed=moved),
    )(*operands)


def project_kernel(group, first, tile, *refs):
    pieces = refs[:group]
    w_ref, give_ref, keep_ref, a_buf, sem = refs[group:]
    width = pieces[0].shape[1]
    member = lax.rem(lax.axis_index("ctx"), group)

    @pl.when(pl.program_id(0) == 0)
    def _():
        copies = []
        for step in range(group):
            start = pl.multiple_of((member ^ step) * width, width)
            copies.append(
                pltpu.make_async_copy(pieces[step], a_buf.at[:, pl.ds(start, width)], sem.at[step])
            )
        run_copies(copies)

    start = pl.multiple_of(first + pl.program_id(0) * tile, tile)
    product = jnp.dot(a_buf[...], w_ref[:, pl.ds(start, tile)], preferred_element_type=jnp.float32)
    product = product.astype(jnp.bfloat16)
    block = product.shape[0] // 2
    low_first = lax.axis_index("head") == 0
    keep_ref[...] = jnp.where(low_first, product[:block], product[block:])
    give_ref[...] = jnp.where(low_first, product[block:], product[:block])


def project(pieces, w_out, first, columns, tile):
    group = len(pieces)
    rows, width = pieces[0].shape
    depth = w_out.shape[0]
    half = jax.ShapeDtypeStruct((rows // 2, columns), jnp.bfloat16)
    spec = pl.BlockSpec((rows // 2, tile), lambda step: (0, step))
    return pl.pallas_call(
        partial(project_kernel, group, first, tile),
        out_shape=[half, half],
        grid=(columns // tile,),
        in_specs=[HBM] * group + [pl.BlockSpec(memory_space=pltpu.VMEM)],
        out_specs=[spec, spec],
        scratch_shapes=[pltpu.VMEM((rows, depth), jnp.bfloat16), pltpu.SemaphoreType.DMA((group,))],
        compiler_params=params(),
        cost_estimate=pl.CostEstimate(
            flops=2 * rows * depth * columns, transcendentals=0, bytes_accessed=4 * rows * columns
        ),
    )(*pieces, w_out)


def sum_kernel(*refs):
    out_ref = refs[-1]
    halves = (len(refs) - 1) // 2
    columns = refs[0].shape[1]
    for half in range(halves):
        summed = refs[half][...].astype(jnp.float32) + refs[halves + half][...].astype(jnp.float32)
        out_ref[:, half * columns:(half + 1) * columns] = summed.astype(jnp.bfloat16)


def shards(queries, key_heads, value_heads, doc_units, w_out):
    count = lax.axis_size("ctx")
    group = key_heads.shape[1] // HD
    hops = min(16, count // 2) // group
    tokens, depth = queries.shape
    width = depth // group
    rank = lax.axis_index("ctx")
    member = lax.rem(rank, group)

    def column_block(value, step, size):
        return lax.dynamic_slice(value, (0, (member ^ step) * size), (tokens, size))

    def swap(value, step):
        if step == 0:
            return value
        return lax.ppermute(value, "ctx", [(source, source ^ step) for source in range(count)])

    def next_plane(value):
        return lax.ppermute(value, "ctx", [(source, source + group) for source in range(count - group)])

    kv_pieces = [
        swap(
            jnp.concatenate([column_block(key_heads, step, HD), column_block(value_heads, step, HD)], axis=1), step
        )
        for step in range(group)
    ]
    planes = [jnp.concatenate(kv_pieces, axis=0)]
    queries, planes = lax.optimization_barrier((queries, planes))
    query_pieces = [swap(column_block(queries, step, width), step) for step in range(group)]
    planes = [next_plane(planes[0])] + planes
    planes, query_pieces = lax.optimization_barrier((planes, query_pieces))
    for hop in range(hops - 1):
        planes = [next_plane(planes[0])] + planes
    w_here = w_out
    attention = [None] * group
    far = tuple(range(group - 1, 1, -1))
    if far:
        far_queries = [query_pieces[step] for step in far]
        *partials, state, w_here = attend("early", far, doc_units, far_queries, planes[-2:], w_out=w_out)
        finals = attend("late", far, doc_units, far_queries, planes, state=state, outs=partials)
        for step, final in zip(far, finals):
            attention[step] = swap(final, step)
        query_pieces, finals = lax.optimization_barrier((query_pieces, finals))
    for step in range(min(group, 2) - 1, -1, -1):
        (final,) = attend("full", (step,), doc_units, [query_pieces[step]], planes)
        attention[step] = swap(final, step)
        query_pieces, final = lax.optimization_barrier((query_pieces, final))
    columns = w_out.shape[1]
    if lax.axis_size("head") == 2:
        w_here = pltpu.with_memory_space_constraint(w_here, pltpu.VMEM)
        size = columns // 2
        keeps, gots = [], []
        for half in range(2):
            give, keep = project(attention, w_here, half * size, size, 512)
            keeps.append(keep)
            gots.append(lax.ppermute(give, "head", [(0, 1), (1, 0)]))
        return pl.pallas_call(
            sum_kernel,
            out_shape=jax.ShapeDtypeStruct((tokens // 2, columns), jnp.bfloat16),
            compiler_params=params(),
        )(*keeps, *gots)
    product = sum(
        jnp.dot(
            attention[step],
            lax.dynamic_slice(w_out, ((member ^ step) * width, 0), (width, columns)),
            preferred_element_type=jnp.float32,
        )
        for step in range(group)
    )
    return lax.psum_scatter(product.astype(jnp.bfloat16), "head", scatter_dimension=0, tiled=True)


def solution(mesh):
    in_specs = (P("ctx", "head"), P("ctx", "head"), P("ctx", "head"), P(), P("head", None))
    out_specs = P(("ctx", "head"), None)
    return jax.shard_map(shards, mesh=mesh, in_specs=in_specs, out_specs=out_specs, check_vma=False)
```

profile of v0, /device:TPU:25, one launch (start us, length us, event | category | flops | bytes accessed | tf_op | source)
XLA Modules:
  0.0 108.9 jit_solution(2924532049236144019)
XLA Ops:
  0.0 1.3 %constant_dynamic-slice_fusion.10 = (bf16[384,128]{1,0:T(8,128)(2,1)S(1)}, bf16[384,128]{1,0:T(8,128)(2,1)S(1)}, bf16[384,128]{1,0:T(8,128)(2,1)S(1)}, bf16[384,...) fusion(bf16[384,512]{1,0:T(8,128)(2,1)} %param.7, ...), kind=kLoop, calls=%fused_computation.14 | loop fusion | bytes 1572880 | tf_op jit(solution)/shard_map/dynamic_slice | solution.py:333
  1.3 0.0 copy-start.1
  1.3 1.3 %collective-permute-start.1 = (bf16[384,256]{1,0:T(8,128)(2,1)S(1)}, bf16[384,256]{1,0:T(8,128)(2,1)S(1)}, u32[]{:S(2)}, u32[]{:S(2)}) collective-permute-start(bf16[384,256]{1,0:T(8,128)(2,1)S(1)} %pad_maximum_fusion.2), channel_id=1, source_target_pairs={{0,4},{2,6},{4,0},{6,2},{8,12},{10,14},{12,8},{14,10},{16,20},{18,... | collective-permute-start | bytes 589832 | tf_op jit(solution)/shard_map/ppermute | solution.py:338
  2.7 1.2 %collective-permute-start.2 = (bf16[384,256]{1,0:T(8,128)(2,1)S(1)}, bf16[384,256]{1,0:T(8,128)(2,1)S(1)}, u32[]{:S(2)}, u32[]{:S(2)}) collective-permute-start(bf16[384,256]{1,0:T(8,128)(2,1)S(1)} %pad_maximum_fusion.3), channel_id=1, source_target_pairs={{0,6},{2,4},{4,2},{6,0},{8,14},{10,12},{12,10},{14,8},{16,22},{18,... | collective-permute-start | bytes 589832 | tf_op jit(solution)/shard_map/ppermute | solution.py:338
  3.9 0.3 collective-permute-start
  4.2 6.5 %collective-permute-done.1 = bf16[384,256]{1,0:T(8,128)(2,1)S(1)} collective-permute-done((bf16[384,256]{1,0:T(8,128)(2,1)S(1)}, bf16[384,256]{1,0:T(8,128)(2,1)S(1)}, u32[]{:S(2)}, u32[]{:S(2)}) %collective-permute-start.1) | collective-permute-done | bytes 196640 | tf_op jit(solution)/shard_map/ppermute | solution.py:338
  10.7 0.0 collective-permute-done.2
  10.7 1.7 %collective-permute-done = bf16[384,256]{1,0:T(8,128)(2,1)S(1)} collective-permute-done((bf16[384,256]{1,0:T(8,128)(2,1)S(1)}, bf16[384,256]{1,0:T(8,128)(2,1)S(1)}, u32[]{:S(2)}, u32[]{:S(2)}) %collective-permute-start) | collective-permute-done | bytes 196640 | tf_op jit(solution)/shard_map/ppermute | solution.py:338
  12.4 0.1 pad_maximum_fusion.refs_4_.refs_5_
  12.5 1.3 %collective-permute-start.3 = (bf16[1536,256]{1,0:T(8,128)(2,1)S(1)}, bf16[1536,256]{1,0:T(8,128)(2,1)S(1)}, u32[]{:S(2)}, u32[]{:S(2)}) collective-permute-start(bf16[1536,256]{1,0:T(8,128)(2,1)S(1)} %pad_maximum_fusion.refs_4_.refs_5_), channel_id=1, source_target_pairs={{0,8},{2,10},{4,12},{6,14},{8,16},{10,18},{12,20},{14,22},{16,24},... | collective-permute-start | bytes 2359304 | tf_op jit(solution)/shard_map/ppermute | solution.py:341
  13.8 0.0 copy-done.1
  13.8 0.0 copy-start
  13.8 0.2 constant_dynamic-slice_fusion
  14.0 2.2 %collective-permute-start.6 = (bf16[384,512]{1,0:T(8,128)(2,1)S(1)}, bf16[384,512]{1,0:T(8,128)(2,1)S(1)}, u32[]{:S(2)}, u32[]{:S(2)}) collective-permute-start(bf16[384,512]{1,0:T(8,128)(2,1)S(1)} %get-tuple-element.47), channel_id=1, source_target_pairs={{0,6},{2,4},{4,2},{6,0},{8,14},{10,12},{12,10},{14,8},{16,22},{18,... | collective-permute-start | bytes 1179656 | tf_op jit(solution)/shard_map/ppermute | solution.py:338
  16.3 0.2 collective-permute-start.5
  16.5 0.3 collective-permute-start.4
  16.7 7.1 %collective-permute-done.6.refs_1_ = bf16[384,512]{1,0:T(8,128)(2,1)S(1)} collective-permute-done((bf16[384,512]{1,0:T(8,128)(2,1)S(1)}, bf16[384,512]{1,0:T(8,128)(2,1)S(1)}, u32[]{:S(2)}, u32[]{:S(2)}) %collective-permute-start.6) | collective-permute-done | bytes 393248 | tf_op jit(solution)/shard_map/ppermute | solution.py:338
  23.8 10.6 %collective-permute-done.5.refs_2_ = bf16[384,512]{1,0:T(8,128)(2,1)S(1)} collective-permute-done((bf16[384,512]{1,0:T(8,128)(2,1)S(1)}, bf16[384,512]{1,0:T(8,128)(2,1)S(1)}, u32[]{:S(2)}, u32[]{:S(2)}) %collective-permute-start.5) | collective-permute-done | bytes 393248 | tf_op jit(solution)/shard_map/ppermute | solution.py:338
  34.5 0.0 collective-permute-done.4.refs_1_
  34.5 0.0 collective-permute-done.3.refs_3_.refs_4_
  34.5 1.3 %collective-permute-start.7 = (bf16[1536,256]{1,0:T(8,128)(2,1)S(1)}, bf16[1536,256]{1,0:T(8,128)(2,1)S(1)}, u32[]{:S(2)}, u32[]{:S(2)}) collective-permute-start(bf16[1536,256]{1,0:T(8,128)(2,1)S(1)} %collective-permute-done.3.refs_3_.refs_4_), channel_id=1, source_target_pairs={{0,8},{2,10},{4,12},{6,14},{8,16},{10,18},{12,20},{14,22},{16,24},... | collective-permute-start | bytes 2359304 | tf_op jit(solution)/shard_map/ppermute | solution.py:341
  35.7 0.0 copy-done
  35.8 9.2 %shard_map.55 = (bf16[384,512]{1,0:T(8,128)(2,1)S(1)}, bf16[384,512]{1,0:T(8,128)(2,1)S(1)}, f32[2,1536,256]{2,1,0:T(8,128)S(1)}, bf16[2048,4096]{1,0:T(8,128)(2,1)S(1)}) custom-call(s32[6]{0:T(128)S(1)} %copy-done, bf16[384,512]{1,0:T(8,128)(2,1)S(1)} %collective-permute-done.6.refs_1_, bf16[384,512]{1,0:T(8,128)(2,1)S(1)} %collective-permute-done.5.refs_2_, ...), custom_call_target="tpu_custom_call" | custom-call | flops 2415919104 | bytes 18350080 | tf_op jit(solution)/shard_map/pallas_call | solution.py:249
  45.0 10.8 %collective-permute-done.7.refs_3_.refs_2_ = bf16[1536,256]{1,0:T(8,128)(2,1)S(1)} collective-permute-done((bf16[1536,256]{1,0:T(8,128)(2,1)S(1)}, bf16[1536,256]{1,0:T(8,128)(2,1)S(1)}, u32[]{:S(2)}, u32[]{:S(2)}) %collective-permute-start.7) | collective-permute-done | bytes 786464 | tf_op jit(solution)/shard_map/ppermute | solution.py:341
  55.8 0.9 shard_map.56
  56.7 12.5 %shard_map.57 = bf16[384,512]{1,0:T(8,128)(2,1)S(1)} custom-call(s32[6]{0:T(128)S(1)} %copy-done, bf16[384,512]{1,0:T(8,128)(2,1)S(1)} %collective-permute-done.4.refs_1_, bf16[1536,256]{1,0:T(8,128)(2,1)S(1)} %collective-permute-done.7.refs_3_.refs_2_, bf16[1536,256]{1,0:T(8,128)(2,1)S(1)} %collective-permute-done.3.refs_3_.refs_4_, ...), custom_call_target="tpu_custom_call" | custom-call | flops 1811939328 | bytes 786432 | tf_op jit(solution)/shard_map/pallas_call | solution.py:249
  69.3 0.2 collective-permute-start.8
  69.4 7.0 %collective-permute-start.10 = (bf16[384,512]{1,0:T(8,128)(2,1)S(1)}, bf16[384,512]{1,0:T(8,128)(2,1)S(1)}, u32[]{:S(2)}, u32[]{:S(2)}) collective-permute-start(bf16[384,512]{1,0:T(8,128)(2,1)S(1)} %get-tuple-element.37), channel_id=1, source_target_pairs={{0,6},{2,4},{4,2},{6,0},{8,14},{10,12},{12,10},{14,8},{16,22},{18,... | collective-permute-start | bytes 1179656 | tf_op jit(solution)/shard_map/ppermute | solution.py:338
  76.4 0.0 collective-permute-start.9
  76.4 11.4 %shard_map.58.refs_0_ = bf16[384,512]{1,0:T(8,128)(2,1)S(1)} custom-call(s32[6]{0:T(128)S(1)} %copy-done, bf16[384,512]{1,0:T(8,128)(2,1)S(1)} %get-tuple-element.41.refs_1_, bf16[1536,256]{1,0:T(8,128)(2,1)S(1)} %collective-permute-done.7.refs_3_.refs_2_, bf16[1536,256]{1,0:T(8,128)(2,1)S(1)} %collective-permute-done.3.refs_3_.refs_4_, ...), custom_call_target="tpu_custom_call" | custom-call | flops 1811939328 | bytes 786432 | tf_op jit(solution)/shard_map/pallas_call | solution.py:249
  87.8 0.0 collective-permute-done.8.refs_1_
  87.8 5.2 %collective-permute-done.10.refs_3_ = bf16[384,512]{1,0:T(8,128)(2,1)S(1)} collective-permute-done((bf16[384,512]{1,0:T(8,128)(2,1)S(1)}, bf16[384,512]{1,0:T(8,128)(2,1)S(1)}, u32[]{:S(2)}, u32[]{:S(2)}) %collective-permute-start.10) | collective-permute-done | bytes 393248 | tf_op jit(solution)/shard_map/ppermute | solution.py:338
  93.0 0.0 collective-permute-done.9.refs_2_
  93.0 4.3 %shard_map.60 = (bf16[192,2048]{1,0:T(8,128)(2,1)S(1)}, bf16[192,2048]{1,0:T(8,128)(2,1)S(1)}) custom-call(bf16[384,512]{1,0:T(8,128)(2,1)S(1)} %shard_map.58.refs_0_, bf16[384,512]{1,0:T(8,128)(2,1)S(1)} %collective-permute-done.8.refs_1_, bf16[384,512]{1,0:T(8,128)(2,1)S(1)} %collective-permute-done.9.refs_2_, ...), custom_call_target="tpu_custom_call" | custom-call | flops 3221225472 | bytes 3145728 | tf_op jit(solution)/shard_map/pallas_call | solution.py:300
  97.3 3.4 %collective-permute-start.12 = (bf16[192,2048]{1,0:T(8,128)(2,1)S(1)}, bf16[192,2048]{1,0:T(8,128)(2,1)S(1)}, u32[]{:S(2)}, u32[]{:S(2)}) collective-permute-start(bf16[192,2048]{1,0:T(8,128)(2,1)S(1)} %get-tuple-element.46), channel_id=1, source_target_pairs={{0,1},{1,0},{2,3},{3,2},{4,5},{5,4},{6,7},{7,6},{8,9},{9,8},{10,11... | collective-permute-start | bytes 2359304 | tf_op jit(solution)/shard_map/ppermute | solution.py:378
  100.7 4.3 %shard_map.59 = (bf16[192,2048]{1,0:T(8,128)(2,1)S(1)}, bf16[192,2048]{1,0:T(8,128)(2,1)S(1)}) custom-call(bf16[384,512]{1,0:T(8,128)(2,1)S(1)} %shard_map.58.refs_0_, bf16[384,512]{1,0:T(8,128)(2,1)S(1)} %collective-permute-done.8.refs_1_, bf16[384,512]{1,0:T(8,128)(2,1)S(1)} %collective-permute-done.9.refs_2_, ...), custom_call_target="tpu_custom_call" | custom-call | flops 3221225472 | bytes 3145728 | tf_op jit(solution)/shard_map/pallas_call | solution.py:300
  105.0 0.1 collective-permute-start.11
  105.2 0.0 collective-permute-done.12.refs_3_
  105.2 2.2 %collective-permute-done.11.refs_2_ = bf16[192,2048]{1,0:T(8,128)(2,1)S(1)} collective-permute-done((bf16[192,2048]{1,0:T(8,128)(2,1)S(1)}, bf16[192,2048]{1,0:T(8,128)(2,1)S(1)}, u32[]{:S(2)}, u32[]{:S(2)}) %collective-permute-start.11) | collective-permute-done | bytes 786464 | tf_op jit(solution)/shard_map/ppermute | solution.py:378
  107.4 1.5 %shard_map.61 = bf16[192,4096]{1,0:T(8,128)(2,1)} custom-call(bf16[192,2048]{1,0:T(8,128)(2,1)S(1)} %get-tuple-element.43.refs_0_, bf16[192,2048]{1,0:T(8,128)(2,1)S(1)} %get-tuple-element.44.refs_1_, bf16[192,2048]{1,0:T(8,128)(2,1)S(1)} %collective-permute-done.11.refs_2_, bf16[192,2048]{1,0:T(8,128)(2,1)S(1)} %collective-permute-done.12.refs_3_), custom_call_target="tpu_custom_call" | custom-call | tf_op jit(solution)/shard_map/pallas_call | solution.py:379
  (3 shorter events, 0.1 us)
Async XLA Ops:
  1.3 12.5 %copy-start.1 = (bf16[384,2048]{1,0:T(8,128)(2,1)S(1)}, bf16[384,2048]{1,0:T(8,128)(2,1)}, u32[]{:S(2)}) copy-start(bf16[384,2048]{1,0:T(8,128)(2,1)} %param.5) | copy-start | bytes 4718596
  1.3 9.4 %collective-permute-start.1 = (bf16[384,256]{1,0:T(8,128)(2,1)S(1)}, bf16[384,256]{1,0:T(8,128)(2,1)S(1)}, u32[]{:S(2)}, u32[]{:S(2)}) collective-permute-start(bf16[384,256]{1,0:T(8,128)(2,1)S(1)} %pad_maximum_fusion.2), channel_id=1, source_target_pairs={{0,4},{2,6},{4,0},{6,2},{8,12},{10,14},{12,8},{14,10},{16,20},{18,... | collective-permute-start | bytes 589832 | tf_op jit(solution)/shard_map/ppermute | solution.py:338
  2.7 8.1 %collective-permute-start.2 = (bf16[384,256]{1,0:T(8,128)(2,1)S(1)}, bf16[384,256]{1,0:T(8,128)(2,1)S(1)}, u32[]{:S(2)}, u32[]{:S(2)}) collective-permute-start(bf16[384,256]{1,0:T(8,128)(2,1)S(1)} %pad_maximum_fusion.3), channel_id=1, source_target_pairs={{0,6},{2,4},{4,2},{6,0},{8,14},{10,12},{12,10},{14,8},{16,22},{18,... | collective-permute-start | bytes 589832 | tf_op jit(solution)/shard_map/ppermute | solution.py:338
  3.9 8.5 %collective-permute-start = (bf16[384,256]{1,0:T(8,128)(2,1)S(1)}, bf16[384,256]{1,0:T(8,128)(2,1)S(1)}, u32[]{:S(2)}, u32[]{:S(2)}) collective-permute-start(bf16[384,256]{1,0:T(8,128)(2,1)S(1)} %pad_maximum_fusion.1), channel_id=1, source_target_pairs={{0,2},{2,0},{4,6},{6,4},{8,10},{10,8},{12,14},{14,12},{16,18},{18,... | collective-permute-start | bytes 589832 | tf_op jit(solution)/shard_map/ppermute | solution.py:338
  12.5 22.0 %collective-permute-start.3 = (bf16[1536,256]{1,0:T(8,128)(2,1)S(1)}, bf16[1536,256]{1,0:T(8,128)(2,1)S(1)}, u32[]{:S(2)}, u32[]{:S(2)}) collective-permute-start(bf16[1536,256]{1,0:T(8,128)(2,1)S(1)} %pad_maximum_fusion.refs_4_.refs_5_), channel_id=1, source_target_pairs={{0,8},{2,10},{4,12},{6,14},{8,16},{10,18},{12,20},{14,22},{16,24},... | collective-permute-start | bytes 2359304 | tf_op jit(solution)/shard_map/ppermute | solution.py:341
  13.8 21.9 %copy-start = (s32[6]{0:T(128)S(1)}, s32[6]{0:T(128)}, u32[]{:S(2)}) copy-start(s32[6]{0:T(128)} %refs_0_.7) | copy-start | bytes 76
  14.0 9.8 %collective-permute-start.6 = (bf16[384,512]{1,0:T(8,128)(2,1)S(1)}, bf16[384,512]{1,0:T(8,128)(2,1)S(1)}, u32[]{:S(2)}, u32[]{:S(2)}) collective-permute-start(bf16[384,512]{1,0:T(8,128)(2,1)S(1)} %get-tuple-element.47), channel_id=1, source_target_pairs={{0,6},{2,4},{4,2},{6,0},{8,14},{10,12},{12,10},{14,8},{16,22},{18,... | collective-permute-start | bytes 1179656 | tf_op jit(solution)/shard_map/ppermute | solution.py:338
  16.3 18.2 %collective-permute-start.5 = (bf16[384,512]{1,0:T(8,128)(2,1)S(1)}, bf16[384,512]{1,0:T(8,128)(2,1)S(1)}, u32[]{:S(2)}, u32[]{:S(2)}) collective-permute-start(bf16[384,512]{1,0:T(8,128)(2,1)S(1)} %get-tuple-element.48), channel_id=1, source_target_pairs={{0,4},{2,6},{4,0},{6,2},{8,12},{10,14},{12,8},{14,10},{16,20},{18,... | collective-permute-start | bytes 1179656 | tf_op jit(solution)/shard_map/ppermute | solution.py:338
  16.5 18.0 %collective-permute-start.4 = (bf16[384,512]{1,0:T(8,128)(2,1)S(1)}, bf16[384,512]{1,0:T(8,128)(2,1)S(1)}, u32[]{:S(2)}, u32[]{:S(2)}) collective-permute-start(bf16[384,512]{1,0:T(8,128)(2,1)S(1)} %get-tuple-element.49), channel_id=1, source_target_pairs={{0,2},{2,0},{4,6},{6,4},{8,10},{10,8},{12,14},{14,12},{16,18},{18,... | collective-permute-start | bytes 1179656 | tf_op jit(solution)/shard_map/ppermute | solution.py:338
  34.5 21.3 %collective-permute-start.7 = (bf16[1536,256]{1,0:T(8,128)(2,1)S(1)}, bf16[1536,256]{1,0:T(8,128)(2,1)S(1)}, u32[]{:S(2)}, u32[]{:S(2)}) collective-permute-start(bf16[1536,256]{1,0:T(8,128)(2,1)S(1)} %collective-permute-done.3.refs_3_.refs_4_), channel_id=1, source_target_pairs={{0,8},{2,10},{4,12},{6,14},{8,16},{10,18},{12,20},{14,22},{16,24},... | collective-permute-start | bytes 2359304 | tf_op jit(solution)/shard_map/ppermute | solution.py:341
  69.3 18.5 %collective-permute-start.8 = (bf16[384,512]{1,0:T(8,128)(2,1)S(1)}, bf16[384,512]{1,0:T(8,128)(2,1)S(1)}, u32[]{:S(2)}, u32[]{:S(2)}) collective-permute-start(bf16[384,512]{1,0:T(8,128)(2,1)S(1)} %shard_map.57), channel_id=1, source_target_pairs={{0,2},{2,0},{4,6},{6,4},{8,10},{10,8},{12,14},{14,12},{16,18},{18,... | collective-permute-start | bytes 1179656 | tf_op jit(solution)/shard_map/ppermute | solution.py:338
  69.4 23.5 %collective-permute-start.10 = (bf16[384,512]{1,0:T(8,128)(2,1)S(1)}, bf16[384,512]{1,0:T(8,128)(2,1)S(1)}, u32[]{:S(2)}, u32[]{:S(2)}) collective-permute-start(bf16[384,512]{1,0:T(8,128)(2,1)S(1)} %get-tuple-element.37), channel_id=1, source_target_pairs={{0,6},{2,4},{4,2},{6,0},{8,14},{10,12},{12,10},{14,8},{16,22},{18,... | collective-permute-start | bytes 1179656 | tf_op jit(solution)/shard_map/ppermute | solution.py:338
  76.4 16.6 %collective-permute-start.9 = (bf16[384,512]{1,0:T(8,128)(2,1)S(1)}, bf16[384,512]{1,0:T(8,128)(2,1)S(1)}, u32[]{:S(2)}, u32[]{:S(2)}) collective-permute-start(bf16[384,512]{1,0:T(8,128)(2,1)S(1)} %get-tuple-element.38), channel_id=1, source_target_pairs={{0,4},{2,6},{4,0},{6,2},{8,12},{10,14},{12,8},{14,10},{16,20},{18,... | collective-permute-start | bytes 1179656 | tf_op jit(solution)/shard_map/ppermute | solution.py:338
  97.3 7.9 %collective-permute-start.12 = (bf16[192,2048]{1,0:T(8,128)(2,1)S(1)}, bf16[192,2048]{1,0:T(8,128)(2,1)S(1)}, u32[]{:S(2)}, u32[]{:S(2)}) collective-permute-start(bf16[192,2048]{1,0:T(8,128)(2,1)S(1)} %get-tuple-element.46), channel_id=1, source_target_pairs={{0,1},{1,0},{2,3},{3,2},{4,5},{5,4},{6,7},{7,6},{8,9},{9,8},{10,11... | collective-permute-start | bytes 2359304 | tf_op jit(solution)/shard_map/ppermute | solution.py:378
  105.0 2.4 %collective-permute-start.11 = (bf16[192,2048]{1,0:T(8,128)(2,1)S(1)}, bf16[192,2048]{1,0:T(8,128)(2,1)S(1)}, u32[]{:S(2)}, u32[]{:S(2)}) collective-permute-start(bf16[192,2048]{1,0:T(8,128)(2,1)S(1)} %get-tuple-element.45), channel_id=1, source_target_pairs={{0,1},{1,0},{2,3},{3,2},{4,5},{5,4},{6,7},{7,6},{8,9},{9,8},{10,11... | collective-permute-start | bytes 2359304 | tf_op jit(solution)/shard_map/ppermute | solution.py:378
where the time goes:
time: 109 us
  Pallas kernels  44.2 us (41%)
  waiting for transfers between devices  44.1 us (40%)
  starting transfers between devices  18.8 us (17%)
  local copies, waits for them, and re-layouts  1.48 us (1%)
    pallas_call x4, Pallas kernels, attend(): pl.pallas_call(partial(attention_kernel, mode, steps, group, len(planes),...  34.1 us
    ppermute x9, waiting for transfers between devices, swap(): lax.ppermute(value, 'ctx', [(source, source ^ step) for source in range(c...  31.1 us
    ppermute x9, starting transfers between devices, swap(): lax.ppermute(value, 'ctx', [(source, source ^ step) for source in range(c...  12.7 us
    ppermute x2, waiting for transfers between devices, next_plane(): lax.ppermute(value, 'ctx', [(source, source + group) for source in range(...  10.8 us
    pallas_call x2, Pallas kernels, project(): pl.pallas_call(partial(project_kernel, group, first, tile), out_shape=[ha...  8.63 us
    ppermute x2, starting transfers between devices, shards(): gots.append(lax.ppermute(give, 'head', [(0, 1), (1, 0)]))  3.54 us
    ppermute x2, starting transfers between devices, next_plane(): lax.ppermute(value, 'ctx', [(source, source + group) for source in range(...  2.57 us
    ppermute x2, waiting for transfers between devices, shards(): gots.append(lax.ppermute(give, 'head', [(0, 1), (1, 0)]))  2.23 us
  transfers between devices with their start and end apart: 13, of which 7 were waited for; matrix products, arithmetic and copies ran while one was open for 0% of the time, Pallas kernels for 23%

commit v1 on v0

--- a/solution.py
+++ b/solution.py
@@ -43,6 +43,7 @@
     (docs_ref,) = take(1)
     queries = take(pieces)
     keys = take(planes)
+    values = take(planes)
     if early:
         (w_from,) = take(1)
     if late:
@@ -51,7 +52,7 @@
     outs = take(pieces)
     if early:
         state, w_to = take(2)
-    q_buf, kv_buf, o_buf, shift, total, in_sem, out_sem = refs
+    q_buf, k_buf, v_buf, o_buf, shift, total, in_sem, out_sem = refs
     tokens = queries[0].shape[0]
     units = tokens // UNIT
     plane_rows = keys[0].shape[0]
@@ -82,20 +83,22 @@
         for number in range(planes):
             for step in range(group):
                 to = pl.multiple_of(pad + number * plane_rows + (member ^ step) * tokens, UNIT)
-                copies.append(
-                    pltpu.make_async_copy(
-                        keys[number].at[pl.ds(step * tokens, tokens), :],
-                        kv_buf.at[pl.ds(to, tokens), :],
-                        in_sem.at[number * group + step],
+                for part, (source, target) in enumerate(((keys, k_buf), (values, v_buf))):
+                    copies.append(
+                        pltpu.make_async_copy(
+                            source[number].at[pl.ds(step * tokens, tokens), :],
+                            target.at[pl.ds(to, tokens), :],
+                            in_sem.at[2 * (number * group + step) + part],
+                        )
                     )
-                )
         for piece in range(pieces):
             copies.append(
-                pltpu.make_async_copy(queries[piece], q_buf.at[piece], in_sem.at[planes * group + piece])
+                pltpu.make_async_copy(queries[piece], q_buf.at[piece], in_sem.at[2 * planes * group + piece])
             )
         for copy in copies:
             copy.start()
-        kv_buf[pl.ds(0, pad), :] = jnp.zeros((pad, 2 * HD), jnp.bfloat16)
+        k_buf[pl.ds(0, pad), :] = jnp.zeros((pad, HD), jnp.bfloat16)
+        v_buf[pl.ds(0, pad), :] = jnp.zeros((pad, HD), jnp.bfloat16)
         for copy in copies:
             copy.wait()
 
@@ -113,8 +116,8 @@
         def scores_of(end, number, masked):
             begin_unit = end - (number + 1) * CHUNK_UNITS
             begin = pl.multiple_of(begin_unit * UNIT, UNIT)
-            key = kv_buf[pl.ds(begin, chunk), :HD]
-            value = jnp.concatenate([kv_buf[pl.ds(begin, chunk), HD:], ones], axis=1)
+            key = k_buf[pl.ds(begin, chunk), :]
+            value = jnp.concatenate([v_buf[pl.ds(begin, chunk), :], ones], axis=1)
             scores = lax.dot_general(query, key, (((1,), (1,)), ((), ())), preferred_element_type=jnp.float32)
             if masked:
                 column = lax.broadcasted_iota(jnp.int32, (UNIT, chunk), 1)
@@ -129,7 +132,7 @@
                 ], axis=0)
             return scores, value
 
-        own_key = kv_buf[pl.ds(pl.multiple_of(first_row * UNIT, UNIT), tokens), :HD]
+        own_key = k_buf[pl.ds(pl.multiple_of(first_row * UNIT, UNIT), tokens), :]
         own = query * jnp.concatenate([own_key] * heads, axis=0)
         shift[...] = jnp.dot(own, square, preferred_element_type=jnp.float32) * scale
 
@@ -221,16 +224,17 @@
             w_copy.wait()
 
 
-def attend(mode, steps, doc_units, queries, planes, w_out=None, state=None, outs=None):
+def attend(mode, steps, doc_units, queries, keys, values, w_out=None, state=None, outs=None):
     pieces = len(steps)
-    group = planes[0].shape[0] // queries[0].shape[0]
+    planes = len(keys)
+    group = keys[0].shape[0] // queries[0].shape[0]
     tokens, width = queries[0].shape
     heads = width // HD
-    plane_rows = planes[0].shape[0]
+    plane_rows = keys[0].shape[0]
     rows = heads * tokens
     pad = (CHUNK_UNITS - 1) * UNIT
-    scores = tokens * pieces * heads * plane_rows * (1 if mode == "late" else len(planes)) // 2
-    operands = [doc_units, *queries, *planes]
+    scores = tokens * pieces * heads * plane_rows * (1 if mode == "late" else planes) // 2
+    operands = [doc_units, *queries, *keys, *values]
     in_specs = [SMEM] + [HBM] * (len(operands) - 1)
     out_shape = [jax.ShapeDtypeStruct((tokens, width), jnp.bfloat16)] * pieces
     out_specs = [HBM] * pieces
@@ -247,17 +251,18 @@
         operands += [pltpu.with_memory_space_constraint(state, pltpu.VMEM), *outs]
         in_specs += [VMEM] + [HBM] * pieces
     return pl.pallas_call(
-        partial(attention_kernel, mode, steps, group, len(planes), heads, doc_units.shape[0]),
+        partial(attention_kernel, mode, steps, group, planes, heads, doc_units.shape[0]),
         out_shape=out_shape,
         in_specs=in_specs,
         out_specs=out_specs,
         scratch_shapes=[
             pltpu.VMEM((pieces, tokens, width), jnp.bfloat16),
-            pltpu.VMEM((pad + plane_rows * len(planes), 2 * HD), jnp.bfloat16),
+            pltpu.VMEM((pad + plane_rows * planes, HD), jnp.bfloat16),
+            pltpu.VMEM((pad + plane_rows * planes, HD), jnp.bfloat16),
             pltpu.VMEM((pieces, tokens, width), jnp.bfloat16),
             pltpu.VMEM((rows, HD), jnp.float32),
             pltpu.VMEM((rows, 2 * HD), jnp.float32),
-            pltpu.SemaphoreType.DMA((pieces + group * len(planes),)),
+            pltpu.SemaphoreType.DMA((pieces + 2 * group * planes,)),
             pltpu.SemaphoreType.DMA((pieces + 1,)),
         ],
         input_output_aliases=aliases,
@@ -340,33 +345,31 @@
     def next_plane(value):
         return lax.ppermute(value, "ctx", [(source, source + group) for source in range(count - group)])
 
-    kv_pieces = [
-        swap(
-            jnp.concatenate([column_block(key_heads, step, HD), column_block(value_heads, step, HD)], axis=1), step
-        )
-        for step in range(group)
-    ]
-    planes = [jnp.concatenate(kv_pieces, axis=0)]
-    queries, planes = lax.optimization_barrier((queries, planes))
+    def own_plane(value):
+        return jnp.concatenate([swap(column_block(value, step, HD), step) for step in range(group)], axis=0)
+
+    keys, values = [own_plane(key_heads)], [own_plane(value_heads)]
+    queries = lax.optimization_barrier((queries, keys, values))[0]
     query_pieces = [swap(column_block(queries, step, width), step) for step in range(group)]
-    planes = [next_plane(planes[0])] + planes
-    planes, query_pieces = lax.optimization_barrier((planes, query_pieces))
+    keys = [next_plane(keys[0])] + keys
+    values = [next_plane(values[0])] + values
+    if group > 1:
+        keys, query_pieces[:-1] = lax.optimization_barrier((keys, query_pieces[:-1]))
+        values, query_pieces[-1:] = lax.optimization_barrier((values, query_pieces[-1:]))
     for hop in range(hops - 1):
-        planes = [next_plane(planes[0])] + planes
+        keys = [next_plane(keys[0])] + keys
+        values = [next_plane(values[0])] + values
     w_here = w_out
     attention = [None] * group
-    far = tuple(range(group - 1, 1, -1))
+    far = tuple(range(group - 1, 0, -1))
     if far:
         far_queries = [query_pieces[step] for step in far]
-        *partials, state, w_here = attend("early", far, doc_units, far_queries, planes[-2:], w_out=w_out)
-        finals = attend("late", far, doc_units, far_queries, planes, state=state, outs=partials)
+        *partials, state, w_here = attend("early", far, doc_units, far_queries, keys[-2:], values[-2:], w_out=w_out)
+        finals = attend("late", far, doc_units, far_queries, keys, values, state=state, outs=partials)
         for step, final in zip(far, finals):
             attention[step] = swap(final, step)
         query_pieces, finals = lax.optimization_barrier((query_pieces, finals))
-    for step in range(min(group, 2) - 1, -1, -1):
-        (final,) = attend("full", (step,), doc_units, [query_pieces[step]], planes)
-        attention[step] = swap(final, step)
-        query_pieces, final = lax.optimization_barrier((query_pieces, final))
+    (attention[0],) = attend("full", (0,), doc_units, query_pieces[:1], keys, values)
     columns = w_out.shape[1]
     if lax.axis_size("head") == 2:
         w_here = pltpu.with_memory_space_constraint(w_here, pltpu.VMEM)

time: 109 us -> 98.9 us (0.907)
  waiting for transfers between devices: 44.1 us -> 27.9 us
  starting transfers between devices: 18.8 us -> 21 us
  local copies, waits for them, and re-layouts: 1.48 us -> 3.63 us
  Pallas kernels: 44.2 us -> 45.8 us
    ppermute x9 -> x12, waiting for transfers between devices: 31.1 us -> 22.6 us  [swap(): lax.ppermute(value, 'ctx', [(source, source ^ step) for source in range(c...]
    ppermute x2 -> x4, waiting for transfers between devices: 10.8 us -> 3.14 us  [next_plane(): lax.ppermute(value, 'ctx', [(source, source + group) for source in range(...]
    ppermute x2, starting transfers between devices: 3.54 us -> 0.67 us  [shards(): gots.append(lax.ppermute(give, 'head', [(0, 1), (1, 0)]))]
    ppermute x2 -> x4, starting transfers between devices: 2.57 us -> 5.13 us  [next_plane(): lax.ppermute(value, 'ctx', [(source, source + group) for source in range(...]
    ppermute x9 -> x12, starting transfers between devices: 12.7 us -> 15.2 us  [swap(): lax.ppermute(value, 'ctx', [(source, source ^ step) for source in range(c...]
    dynamic_slice x2 -> x3, local copies, waits for them, and re-layouts: 1.47 us -> 3.63 us  [column_block(): return lax.dynamic_slice(value, (0, (member ^ step) * size), (tokens, size))]
    pallas_call x4 -> x3, Pallas kernels: 34.1 us -> 35.7 us  [attend(): pl.pallas_call(partial(attention_kernel, mode, steps, group, planes, head...]
  transfers between devices with their start and end apart: 13 -> 18, of which waited for: 7 -> 10; matrix products, arithmetic and copies ran while one was open for 0% -> 3% of each run, Pallas kernels for 23% -> 32%
where the time goes in v1:
time: 98.9 us; the launch traced here: 98.6 us
  Pallas kernels  45.8 us (46%)
  waiting for transfers between devices  27.9 us (28%)
  starting transfers between devices  21 us (21%)
  local copies, waits for them, and re-layouts  3.63 us (4%)
    pallas_call x3, Pallas kernels, attend(): pl.pallas_call(partial(attention_kernel, mode, steps, group, planes, head...  35.7 us
    ppermute x12, waiting for transfers between devices, swap(): lax.ppermute(value, 'ctx', [(source, source ^ step) for source in range(c...  22.6 us
    ppermute x12, starting transfers between devices, swap(): lax.ppermute(value, 'ctx', [(source, source ^ step) for source in range(c...  15.2 us
    pallas_call x2, Pallas kernels, project(): pl.pallas_call(partial(project_kernel, group, first, tile), out_shape=[ha...  8.63 us
    ppermute x4, starting transfers between devices, next_plane(): lax.ppermute(value, 'ctx', [(source, source + group) for source in range(...  5.13 us
    dynamic_slice x3, local copies, waits for them, and re-layouts, column_block(): return lax.dynamic_slice(value, (0, (member ^ step) * size), (tokens, size))  3.63 us
    ppermute x4, waiting for transfers between devices, next_plane(): lax.ppermute(value, 'ctx', [(source, source + group) for source in range(...  3.14 us
    ppermute x2, waiting for transfers between devices, shards(): gots.append(lax.ppermute(give, 'head', [(0, 1), (1, 0)]))  2.23 us
  transfers between devices with their start and end apart: 18, of which 10 were waited for; matrix products, arithmetic and copies ran while one was open for 3% of the time, Pallas kernels for 32%

profile of v1, /device:TPU:25, one launch (start us, length us, event | category | flops | bytes accessed | tf_op | source)
XLA Modules:
  0.0 98.6 jit_solution(11292160551877430886)
XLA Ops:
  0.0 0.0 copy-start
  0.0 1.1 %constant_dynamic-slice_fusion.7 = (bf16[384,128]{1,0:T(8,128)(2,1)S(1)}, bf16[384,128]{1,0:T(8,128)(2,1)S(1)}, bf16[384,128]{1,0:T(8,128)(2,1)S(1)}, bf16[384,128]{1,0:T(8,128)(2,1)S(1)}) fusion(bf16[384,512]{1,0:T(8,128)(2,1)} %param.7, s32[]{:T(128)S(6)} %select_n.28, s32[]{:T(128)S(6)} %select_n.29, s32[]{:T(128)S(6)} %select_n.31, s32[]{:T(128)S(6)} %select_n.30), kind=kLoop, calls=%fused_computation.9 | loop fusion | bytes 786448 | tf_op jit(solution)/shard_map/dynamic_slice | solution.py:338
  1.1 1.3 %collective-permute-start.4 = (bf16[384,128]{1,0:T(8,128)(2,1)S(1)}, bf16[384,128]{1,0:T(8,128)(2,1)S(1)}, u32[]{:S(2)}, u32[]{:S(2)}) collective-permute-start(bf16[384,128]{1,0:T(8,128)(2,1)S(1)} %get-tuple-element.54), channel_id=1, source_target_pairs={{0,2},{2,0},{4,6},{6,4},{8,10},{10,8},{12,14},{14,12},{16,18},{18,... | collective-permute-start | bytes 294920 | tf_op jit(solution)/shard_map/ppermute | solution.py:343
  2.4 1.2 %collective-permute-start.6 = (bf16[384,128]{1,0:T(8,128)(2,1)S(1)}, bf16[384,128]{1,0:T(8,128)(2,1)S(1)}, u32[]{:S(2)}, u32[]{:S(2)}) collective-permute-start(bf16[384,128]{1,0:T(8,128)(2,1)S(1)} %get-tuple-element.55), channel_id=1, source_target_pairs={{0,6},{2,4},{4,2},{6,0},{8,14},{10,12},{12,10},{14,8},{16,22},{18,... | collective-permute-start | bytes 294920 | tf_op jit(solution)/shard_map/ppermute | solution.py:343
  3.6 0.2 collective-permute-start.5
  3.8 1.1 %constant_dynamic-slice_fusion.11 = (bf16[384,128]{1,0:T(8,128)(2,1)S(1)}, bf16[384,128]{1,0:T(8,128)(2,1)S(1)}, bf16[384,128]{1,0:T(8,128)(2,1)S(1)}, bf16[384,128]{1,0:T(8,128)(2,1)S(1)}) fusion(bf16[384,512]{1,0:T(8,128)(2,1)} %param.6, s32[]{:T(128)S(6)} %select_n.28, s32[]{:T(128)S(6)} %select_n.29, s32[]{:T(128)S(6)} %select_n.31, s32[]{:T(128)S(6)} %select_n.30), kind=kLoop, calls=%fused_computation.13 | loop fusion | bytes 786448 | tf_op jit(solution)/shard_map/dynamic_slice | solution.py:338
  4.9 1.3 %collective-permute-start = (bf16[384,128]{1,0:T(8,128)(2,1)S(1)}, bf16[384,128]{1,0:T(8,128)(2,1)S(1)}, u32[]{:S(2)}, u32[]{:S(2)}) collective-permute-start(bf16[384,128]{1,0:T(8,128)(2,1)S(1)} %get-tuple-element.58), channel_id=1, source_target_pairs={{0,2},{2,0},{4,6},{6,4},{8,10},{10,8},{12,14},{14,12},{16,18},{18,... | collective-permute-start | bytes 294920 | tf_op jit(solution)/shard_map/ppermute | solution.py:343
  6.2 1.2 %collective-permute-start.2 = (bf16[384,128]{1,0:T(8,128)(2,1)S(1)}, bf16[384,128]{1,0:T(8,128)(2,1)S(1)}, u32[]{:S(2)}, u32[]{:S(2)}) collective-permute-start(bf16[384,128]{1,0:T(8,128)(2,1)S(1)} %get-tuple-element.59), channel_id=1, source_target_pairs={{0,6},{2,4},{4,2},{6,0},{8,14},{10,12},{12,10},{14,8},{16,22},{18,... | collective-permute-start | bytes 294920 | tf_op jit(solution)/shard_map/ppermute | solution.py:343
  7.4 0.0 collective-permute-done.4
  7.4 0.2 collective-permute-start.1
  7.6 0.5 collective-permute-done.6
  8.1 1.2 %collective-permute-done.5 = bf16[384,128]{1,0:T(8,128)(2,1)S(1)} collective-permute-done((bf16[384,128]{1,0:T(8,128)(2,1)S(1)}, bf16[384,128]{1,0:T(8,128)(2,1)S(1)}, u32[]{:S(2)}, u32[]{:S(2)}) %collective-permute-start.5) | collective-permute-done | bytes 98336 | tf_op jit(solution)/shard_map/ppermute | solution.py:343
  9.3 1.3 %collective-permute-start.9 = (bf16[1536,128]{1,0:T(8,128)(2,1)S(1)}, bf16[1536,128]{1,0:T(8,128)(2,1)S(1)}, u32[]{:S(2)}, u32[]{:S(2)}) collective-permute-start(bf16[1536,128]{1,0:T(8,128)(2,1)S(1)} %pad_maximum_fusion.1.refs_7_.refs_9_), channel_id=1, source_target_pairs={{0,8},{2,10},{4,12},{6,14},{8,16},{10,18},{12,20},{14,22},{16,24},... | collective-permute-start | bytes 1179656 | tf_op jit(solution)/shard_map/ppermute | solution.py:346
  10.6 0.0 collective-permute-done
  10.6 0.9 collective-permute-done.2
  11.5 2.0 %collective-permute-done.1 = bf16[384,128]{1,0:T(8,128)(2,1)S(1)} collective-permute-done((bf16[384,128]{1,0:T(8,128)(2,1)S(1)}, bf16[384,128]{1,0:T(8,128)(2,1)S(1)}, u32[]{:S(2)}, u32[]{:S(2)}) %collective-permute-start.1) | collective-permute-done | bytes 98336 | tf_op jit(solution)/shard_map/ppermute | solution.py:343
  13.5 1.5 %constant_dynamic-slice_fusion = (bf16[384,512]{1,0:T(8,128)(2,1)S(1)}, bf16[384,512]{1,0:T(8,128)(2,1)S(1)}, bf16[384,512]{1,0:T(8,128)(2,1)S(1)}, bf16[384,512]{1,0:T(8,128)(2,1)S(1)}) fusion(bf16[384,2048]{1,0:T(8,128)(2,1)} %param.5, s32[]{:T(128)S(6)} %select_n.35, s32[]{:T(128)S(6)} %select_n.34, s32[]{:T(128)S(6)} %select_n.33, s32[]{:T(128)S(6)} %select_n.32), kind=kLoop, calls=%fused_computation.2 | loop fusion | bytes 3145744 | tf_op jit(solution)/shard_map/dynamic_slice | solution.py:338
  15.0 1.3 %collective-permute-start.10 = (bf16[384,512]{1,0:T(8,128)(2,1)S(1)}, bf16[384,512]{1,0:T(8,128)(2,1)S(1)}, u32[]{:S(2)}, u32[]{:S(2)}) collective-permute-start(bf16[384,512]{1,0:T(8,128)(2,1)S(1)} %get-tuple-element.49), channel_id=1, source_target_pairs={{0,6},{2,4},{4,2},{6,0},{8,14},{10,12},{12,10},{14,8},{16,22},{18,... | collective-permute-start | bytes 1179656 | tf_op jit(solution)/shard_map/ppermute | solution.py:343
  16.3 1.3 %collective-permute-start.3 = (bf16[1536,128]{1,0:T(8,128)(2,1)S(1)}, bf16[1536,128]{1,0:T(8,128)(2,1)S(1)}, u32[]{:S(2)}, u32[]{:S(2)}) collective-permute-start(bf16[1536,128]{1,0:T(8,128)(2,1)S(1)} %pad_maximum_fusion.refs_5_.refs_6_.refs_4_), channel_id=1, source_target_pairs={{0,8},{2,10},{4,12},{6,14},{8,16},{10,18},{12,20},{14,22},{16,24},... | collective-permute-start | bytes 1179656 | tf_op jit(solution)/shard_map/ppermute | solution.py:346
  17.6 1.0 %collective-permute-start.8 = (bf16[384,512]{1,0:T(8,128)(2,1)S(1)}, bf16[384,512]{1,0:T(8,128)(2,1)S(1)}, u32[]{:S(2)}, u32[]{:S(2)}) collective-permute-start(bf16[384,512]{1,0:T(8,128)(2,1)S(1)} %get-tuple-element.50), channel_id=1, source_target_pairs={{0,4},{2,6},{4,0},{6,2},{8,12},{10,14},{12,8},{14,10},{16,20},{18,... | collective-permute-start | bytes 1179656 | tf_op jit(solution)/shard_map/ppermute | solution.py:343
  18.6 0.5 collective-permute-start.7
  19.1 0.2 collective-permute-done.9.refs_6_.refs_8_
  19.3 5.9 %collective-permute-done.10.refs_1_ = bf16[384,512]{1,0:T(8,128)(2,1)S(1)} collective-permute-done((bf16[384,512]{1,0:T(8,128)(2,1)S(1)}, bf16[384,512]{1,0:T(8,128)(2,1)S(1)}, u32[]{:S(2)}, u32[]{:S(2)}) %collective-permute-start.10) | collective-permute-done | bytes 393248 | tf_op jit(solution)/shard_map/ppermute | solution.py:343
  25.2 1.3 %collective-permute-start.12 = (bf16[1536,128]{1,0:T(8,128)(2,1)S(1)}, bf16[1536,128]{1,0:T(8,128)(2,1)S(1)}, u32[]{:S(2)}, u32[]{:S(2)}) collective-permute-start(bf16[1536,128]{1,0:T(8,128)(2,1)S(1)} %collective-permute-done.9.refs_6_.refs_8_), channel_id=1, source_target_pairs={{0,8},{2,10},{4,12},{6,14},{8,16},{10,18},{12,20},{14,22},{16,24},... | collective-permute-start | bytes 1179656 | tf_op jit(solution)/shard_map/ppermute | solution.py:346
  26.5 2.9 %collective-permute-done.3.refs_4_.refs_5_.refs_3_ = bf16[1536,128]{1,0:T(8,128)(2,1)S(1)} collective-permute-done((bf16[1536,128]{1,0:T(8,128)(2,1)S(1)}, bf16[1536,128]{1,0:T(8,128)(2,1)S(1)}, u32[]{:S(2)}, u32[]{:S(2)}) %collective-permute-start.3) | collective-permute-done | bytes 393248 | tf_op jit(solution)/shard_map/ppermute | solution.py:346
  29.4 6.1 %collective-permute-done.8.refs_2_ = bf16[384,512]{1,0:T(8,128)(2,1)S(1)} collective-permute-done((bf16[384,512]{1,0:T(8,128)(2,1)S(1)}, bf16[384,512]{1,0:T(8,128)(2,1)S(1)}, u32[]{:S(2)}, u32[]{:S(2)}) %collective-permute-start.8) | collective-permute-done | bytes 393248 | tf_op jit(solution)/shard_map/ppermute | solution.py:343
  35.5 0.0 collective-permute-done.7.refs_3_
  35.5 1.3 %collective-permute-start.11 = (bf16[1536,128]{1,0:T(8,128)(2,1)S(1)}, bf16[1536,128]{1,0:T(8,128)(2,1)S(1)}, u32[]{:S(2)}, u32[]{:S(2)}) collective-permute-start(bf16[1536,128]{1,0:T(8,128)(2,1)S(1)} %collective-permute-done.3.refs_4_.refs_5_.refs_3_), channel_id=1, source_target_pairs={{0,8},{2,10},{4,12},{6,14},{8,16},{10,18},{12,20},{14,22},{16,24},... | collective-permute-start | bytes 1179656 | tf_op jit(solution)/shard_map/ppermute | solution.py:346
  36.7 0.0 copy-done
  36.8 15.9 %shard_map.55 = (bf16[384,512]{1,0:T(8,128)(2,1)S(1)}, bf16[384,512]{1,0:T(8,128)(2,1)S(1)}, bf16[384,512]{1,0:T(8,128)(2,1)S(1)}, f32[3,1536,256]{2,1,0:T(8,128)S(1)}, bf16[2048,4096]{1,0:T(8,128)(2,1)S(1)}) custom-call(s32[6]{0:T(128)S(1)} %copy-done, bf16[384,512]{1,0:T(8,128)(2,1)S(1)} %collective-permute-done.10.refs_1_, ...), custom_call_target="tpu_custom_call" | custom-call | flops 3623878656 | bytes 19136512 | tf_op jit(solution)/shard_map/pallas_call | solution.py:253
  52.7 0.0 collective-permute-done.12.refs_7_.refs_5_
  52.7 0.0 collective-permute-done.11.refs_4_.refs_2_
  52.7 8.2 %shard_map.56 = (bf16[384,512]{1,0:T(8,128)(2,1)S(1)}, bf16[384,512]{1,0:T(8,128)(2,1)S(1)}, bf16[384,512]{1,0:T(8,128)(2,1)S(1)}) custom-call(s32[6]{0:T(128)S(1)} %copy-done, bf16[384,512]{1,0:T(8,128)(2,1)S(1)} %collective-permute-done.10.refs_1_, ...), custom_call_target="tpu_custom_call", output_to_operand_aliasing={{0}: (11, {}), {1}: (12, {}), {2}: (13, {})} | custom-call | flops 1811939328 | bytes 2359296 | tf_op jit(solution)/shard_map/pallas_call | solution.py:253
  60.9 6.7 %collective-permute-start.15 = (bf16[384,512]{1,0:T(8,128)(2,1)S(1)}, bf16[384,512]{1,0:T(8,128)(2,1)S(1)}, u32[]{:S(2)}, u32[]{:S(2)}) collective-permute-start(bf16[384,512]{1,0:T(8,128)(2,1)S(1)} %get-tuple-element.40), channel_id=1, source_target_pairs={{0,6},{2,4},{4,2},{6,0},{8,14},{10,12},{12,10},{14,8},{16,22},{18,... | collective-permute-start | bytes 1179656 | tf_op jit(solution)/shard_map/ppermute | solution.py:343
  67.5 0.0 collective-permute-start.14
  67.5 0.4 collective-permute-start.13
  67.9 11.6 %shard_map.57.refs_0_ = bf16[384,512]{1,0:T(8,128)(2,1)S(1)} custom-call(s32[6]{0:T(128)S(1)} %copy-done, bf16[384,512]{1,0:T(8,128)(2,1)S(1)} %get-tuple-element.43.refs_1_, bf16[1536,128]{1,0:T(8,128)(2,1)S(1)} %collective-permute-done.11.refs_4_.refs_2_, bf16[1536,128]{1,0:T(8,128)(2,1)S(1)} %collective-permute-done.3.refs_4_.refs_5_.refs_3_, ...), custom_call_target="tpu_custom_call" | custom-call | flops 1811939328 | bytes 786432 | tf_op jit(solution)/shard_map/pallas_call | solution.py:253
  79.5 0.0 collective-permute-done.15.refs_3_
  79.5 6.0 %collective-permute-done.14.refs_2_ = bf16[384,512]{1,0:T(8,128)(2,1)S(1)} collective-permute-done((bf16[384,512]{1,0:T(8,128)(2,1)S(1)}, bf16[384,512]{1,0:T(8,128)(2,1)S(1)}, u32[]{:S(2)}, u32[]{:S(2)}) %collective-permute-start.14) | collective-permute-done | bytes 393248 | tf_op jit(solution)/shard_map/ppermute | solution.py:343
  85.5 0.0 collective-permute-done.13.refs_1_
  85.5 4.3 %shard_map.59 = (bf16[192,2048]{1,0:T(8,128)(2,1)S(1)}, bf16[192,2048]{1,0:T(8,128)(2,1)S(1)}) custom-call(bf16[384,512]{1,0:T(8,128)(2,1)S(1)} %shard_map.57.refs_0_, bf16[384,512]{1,0:T(8,128)(2,1)S(1)} %collective-permute-done.13.refs_1_, bf16[384,512]{1,0:T(8,128)(2,1)S(1)} %collective-permute-done.14.refs_2_, ...), custom_call_target="tpu_custom_call" | custom-call | flops 3221225472 | bytes 3145728 | tf_op jit(solution)/shard_map/pallas_call | solution.py:305
  89.9 0.6 collective-permute-start.17
  90.4 4.3 %shard_map.58 = (bf16[192,2048]{1,0:T(8,128)(2,1)S(1)}, bf16[192,2048]{1,0:T(8,128)(2,1)S(1)}) custom-call(bf16[384,512]{1,0:T(8,128)(2,1)S(1)} %shard_map.57.refs_0_, bf16[384,512]{1,0:T(8,128)(2,1)S(1)} %collective-permute-done.13.refs_1_, bf16[384,512]{1,0:T(8,128)(2,1)S(1)} %collective-permute-done.14.refs_2_, ...), custom_call_target="tpu_custom_call" | custom-call | flops 3221225472 | bytes 3145728 | tf_op jit(solution)/shard_map/pallas_call | solution.py:305
  94.7 0.1 collective-permute-start.16
  94.9 0.0 collective-permute-done.17.refs_3_
  94.9 2.2 %collective-permute-done.16.refs_2_ = bf16[192,2048]{1,0:T(8,128)(2,1)S(1)} collective-permute-done((bf16[192,2048]{1,0:T(8,128)(2,1)S(1)}, bf16[192,2048]{1,0:T(8,128)(2,1)S(1)}, u32[]{:S(2)}, u32[]{:S(2)}) %collective-permute-start.16) | collective-permute-done | bytes 786464 | tf_op jit(solution)/shard_map/ppermute | solution.py:381
  97.1 1.5 %shard_map.60 = bf16[192,4096]{1,0:T(8,128)(2,1)} custom-call(bf16[192,2048]{1,0:T(8,128)(2,1)S(1)} %get-tuple-element.45.refs_0_, bf16[192,2048]{1,0:T(8,128)(2,1)S(1)} %get-tuple-element.46.refs_1_, bf16[192,2048]{1,0:T(8,128)(2,1)S(1)} %collective-permute-done.16.refs_2_, bf16[192,2048]{1,0:T(8,128)(2,1)S(1)} %collective-permute-done.17.refs_3_), custom_call_target="tpu_custom_call" | custom-call | tf_op jit(solution)/shard_map/pallas_call | solution.py:382
  (2 shorter events, 0.1 us)
Async XLA Ops:
  0.0 36.7 %copy-start = (s32[6]{0:T(128)S(1)}, s32[6]{0:T(128)}, u32[]{:S(2)}) copy-start(s32[6]{0:T(128)} %refs_0_.5) | copy-start | bytes 76
  1.1 6.3 %collective-permute-start.4 = (bf16[384,128]{1,0:T(8,128)(2,1)S(1)}, bf16[384,128]{1,0:T(8,128)(2,1)S(1)}, u32[]{:S(2)}, u32[]{:S(2)}) collective-permute-start(bf16[384,128]{1,0:T(8,128)(2,1)S(1)} %get-tuple-element.54), channel_id=1, source_target_pairs={{0,2},{2,0},{4,6},{6,4},{8,10},{10,8},{12,14},{14,12},{16,18},{18,... | collective-permute-start | bytes 294920 | tf_op jit(solution)/shard_map/ppermute | solution.py:343
  2.4 5.7 %collective-permute-start.6 = (bf16[384,128]{1,0:T(8,128)(2,1)S(1)}, bf16[384,128]{1,0:T(8,128)(2,1)S(1)}, u32[]{:S(2)}, u32[]{:S(2)}) collective-permute-start(bf16[384,128]{1,0:T(8,128)(2,1)S(1)} %get-tuple-element.55), channel_id=1, source_target_pairs={{0,6},{2,4},{4,2},{6,0},{8,14},{10,12},{12,10},{14,8},{16,22},{18,... | collective-permute-start | bytes 294920 | tf_op jit(solution)/shard_map/ppermute | solution.py:343
  3.6 5.7 %collective-permute-start.5 = (bf16[384,128]{1,0:T(8,128)(2,1)S(1)}, bf16[384,128]{1,0:T(8,128)(2,1)S(1)}, u32[]{:S(2)}, u32[]{:S(2)}) collective-permute-start(bf16[384,128]{1,0:T(8,128)(2,1)S(1)} %get-tuple-element.56), channel_id=1, source_target_pairs={{0,4},{2,6},{4,0},{6,2},{8,12},{10,14},{12,8},{14,10},{16,20},{18,... | collective-permute-start | bytes 294920 | tf_op jit(solution)/shard_map/ppermute | solution.py:343
  4.9 5.7 %collective-permute-start = (bf16[384,128]{1,0:T(8,128)(2,1)S(1)}, bf16[384,128]{1,0:T(8,128)(2,1)S(1)}, u32[]{:S(2)}, u32[]{:S(2)}) collective-permute-start(bf16[384,128]{1,0:T(8,128)(2,1)S(1)} %get-tuple-element.58), channel_id=1, source_target_pairs={{0,2},{2,0},{4,6},{6,4},{8,10},{10,8},{12,14},{14,12},{16,18},{18,... | collective-permute-start | bytes 294920 | tf_op jit(solution)/shard_map/ppermute | solution.py:343
  6.2 5.3 %collective-permute-start.2 = (bf16[384,128]{1,0:T(8,128)(2,1)S(1)}, bf16[384,128]{1,0:T(8,128)(2,1)S(1)}, u32[]{:S(2)}, u32[]{:S(2)}) collective-permute-start(bf16[384,128]{1,0:T(8,128)(2,1)S(1)} %get-tuple-element.59), channel_id=1, source_target_pairs={{0,6},{2,4},{4,2},{6,0},{8,14},{10,12},{12,10},{14,8},{16,22},{18,... | collective-permute-start | bytes 294920 | tf_op jit(solution)/shard_map/ppermute | solution.py:343
  7.4 6.1 %collective-permute-start.1 = (bf16[384,128]{1,0:T(8,128)(2,1)S(1)}, bf16[384,128]{1,0:T(8,128)(2,1)S(1)}, u32[]{:S(2)}, u32[]{:S(2)}) collective-permute-start(bf16[384,128]{1,0:T(8,128)(2,1)S(1)} %get-tuple-element.60), channel_id=1, source_target_pairs={{0,4},{2,6},{4,0},{6,2},{8,12},{10,14},{12,8},{14,10},{16,20},{18,... | collective-permute-start | bytes 294920 | tf_op jit(solution)/shard_map/ppermute | solution.py:343
  9.3 10.0 %collective-permute-start.9 = (bf16[1536,128]{1,0:T(8,128)(2,1)S(1)}, bf16[1536,128]{1,0:T(8,128)(2,1)S(1)}, u32[]{:S(2)}, u32[]{:S(2)}) collective-permute-start(bf16[1536,128]{1,0:T(8,128)(2,1)S(1)} %pad_maximum_fusion.1.refs_7_.refs_9_), channel_id=1, source_target_pairs={{0,8},{2,10},{4,12},{6,14},{8,16},{10,18},{12,20},{14,22},{16,24},... | collective-permute-start | bytes 1179656 | tf_op jit(solution)/shard_map/ppermute | solution.py:346
  15.0 10.2 %collective-permute-start.10 = (bf16[384,512]{1,0:T(8,128)(2,1)S(1)}, bf16[384,512]{1,0:T(8,128)(2,1)S(1)}, u32[]{:S(2)}, u32[]{:S(2)}) collective-permute-start(bf16[384,512]{1,0:T(8,128)(2,1)S(1)} %get-tuple-element.49), channel_id=1, source_target_pairs={{0,6},{2,4},{4,2},{6,0},{8,14},{10,12},{12,10},{14,8},{16,22},{18,... | collective-permute-start | bytes 1179656 | tf_op jit(solution)/shard_map/ppermute | solution.py:343
  16.3 13.1 %collective-permute-start.3 = (bf16[1536,128]{1,0:T(8,128)(2,1)S(1)}, bf16[1536,128]{1,0:T(8,128)(2,1)S(1)}, u32[]{:S(2)}, u32[]{:S(2)}) collective-permute-start(bf16[1536,128]{1,0:T(8,128)(2,1)S(1)} %pad_maximum_fusion.refs_5_.refs_6_.refs_4_), channel_id=1, source_target_pairs={{0,8},{2,10},{4,12},{6,14},{8,16},{10,18},{12,20},{14,22},{16,24},... | collective-permute-start | bytes 1179656 | tf_op jit(solution)/shard_map/ppermute | solution.py:346
  17.6 17.9 %collective-permute-start.8 = (bf16[384,512]{1,0:T(8,128)(2,1)S(1)}, bf16[384,512]{1,0:T(8,128)(2,1)S(1)}, u32[]{:S(2)}, u32[]{:S(2)}) collective-permute-start(bf16[384,512]{1,0:T(8,128)(2,1)S(1)} %get-tuple-element.50), channel_id=1, source_target_pairs={{0,4},{2,6},{4,0},{6,2},{8,12},{10,14},{12,8},{14,10},{16,20},{18,... | collective-permute-start | bytes 1179656 | tf_op jit(solution)/shard_map/ppermute | solution.py:343
  18.6 16.8 %collective-permute-start.7 = (bf16[384,512]{1,0:T(8,128)(2,1)S(1)}, bf16[384,512]{1,0:T(8,128)(2,1)S(1)}, u32[]{:S(2)}, u32[]{:S(2)}) collective-permute-start(bf16[384,512]{1,0:T(8,128)(2,1)S(1)} %get-tuple-element.51), channel_id=1, source_target_pairs={{0,2},{2,0},{4,6},{6,4},{8,10},{10,8},{12,14},{14,12},{16,18},{18,... | collective-permute-start | bytes 1179656 | tf_op jit(solution)/shard_map/ppermute | solution.py:343
  25.2 27.5 %collective-permute-start.12 = (bf16[1536,128]{1,0:T(8,128)(2,1)S(1)}, bf16[1536,128]{1,0:T(8,128)(2,1)S(1)}, u32[]{:S(2)}, u32[]{:S(2)}) collective-permute-start(bf16[1536,128]{1,0:T(8,128)(2,1)S(1)} %collective-permute-done.9.refs_6_.refs_8_), channel_id=1, source_target_pairs={{0,8},{2,10},{4,12},{6,14},{8,16},{10,18},{12,20},{14,22},{16,24},... | collective-permute-start | bytes 1179656 | tf_op jit(solution)/shard_map/ppermute | solution.py:346
  35.5 17.2 %collective-permute-start.11 = (bf16[1536,128]{1,0:T(8,128)(2,1)S(1)}, bf16[1536,128]{1,0:T(8,128)(2,1)S(1)}, u32[]{:S(2)}, u32[]{:S(2)}) collective-permute-start(bf16[1536,128]{1,0:T(8,128)(2,1)S(1)} %collective-permute-done.3.refs_4_.refs_5_.refs_3_), channel_id=1, source_target_pairs={{0,8},{2,10},{4,12},{6,14},{8,16},{10,18},{12,20},{14,22},{16,24},... | collective-permute-start | bytes 1179656 | tf_op jit(solution)/shard_map/ppermute | solution.py:346
  60.9 18.6 %collective-permute-start.15 = (bf16[384,512]{1,0:T(8,128)(2,1)S(1)}, bf16[384,512]{1,0:T(8,128)(2,1)S(1)}, u32[]{:S(2)}, u32[]{:S(2)}) collective-permute-start(bf16[384,512]{1,0:T(8,128)(2,1)S(1)} %get-tuple-element.40), channel_id=1, source_target_pairs={{0,6},{2,4},{4,2},{6,0},{8,14},{10,12},{12,10},{14,8},{16,22},{18,... | collective-permute-start | bytes 1179656 | tf_op jit(solution)/shard_map/ppermute | solution.py:343
  67.5 18.0 %collective-permute-start.14 = (bf16[384,512]{1,0:T(8,128)(2,1)S(1)}, bf16[384,512]{1,0:T(8,128)(2,1)S(1)}, u32[]{:S(2)}, u32[]{:S(2)}) collective-permute-start(bf16[384,512]{1,0:T(8,128)(2,1)S(1)} %get-tuple-element.41), channel_id=1, source_target_pairs={{0,4},{2,6},{4,0},{6,2},{8,12},{10,14},{12,8},{14,10},{16,20},{18,... | collective-permute-start | bytes 1179656 | tf_op jit(solution)/shard_map/ppermute | solution.py:343
  67.5 18.0 %collective-permute-start.13 = (bf16[384,512]{1,0:T(8,128)(2,1)S(1)}, bf16[384,512]{1,0:T(8,128)(2,1)S(1)}, u32[]{:S(2)}, u32[]{:S(2)}) collective-permute-start(bf16[384,512]{1,0:T(8,128)(2,1)S(1)} %get-tuple-element.42), channel_id=1, source_target_pairs={{0,2},{2,0},{4,6},{6,4},{8,10},{10,8},{12,14},{14,12},{16,18},{18,... | collective-permute-start | bytes 1179656 | tf_op jit(solution)/shard_map/ppermute | solution.py:343
  89.9 5.0 %collective-permute-start.17 = (bf16[192,2048]{1,0:T(8,128)(2,1)S(1)}, bf16[192,2048]{1,0:T(8,128)(2,1)S(1)}, u32[]{:S(2)}, u32[]{:S(2)}) collective-permute-start(bf16[192,2048]{1,0:T(8,128)(2,1)S(1)} %get-tuple-element.48), channel_id=1, source_target_pairs={{0,1},{1,0},{2,3},{3,2},{4,5},{5,4},{6,7},{7,6},{8,9},{9,8},{10,11... | collective-permute-start | bytes 2359304 | tf_op jit(solution)/shard_map/ppermute | solution.py:381
  94.7 2.4 %collective-permute-start.16 = (bf16[192,2048]{1,0:T(8,128)(2,1)S(1)}, bf16[192,2048]{1,0:T(8,128)(2,1)S(1)}, u32[]{:S(2)}, u32[]{:S(2)}) collective-permute-start(bf16[192,2048]{1,0:T(8,128)(2,1)S(1)} %get-tuple-element.47), channel_id=1, source_target_pairs={{0,1},{1,0},{2,3},{3,2},{4,5},{5,4},{6,7},{7,6},{8,9},{9,8},{10,11... | collective-permute-start | bytes 2359304 | tf_op jit(solution)/shard_map/ppermute | solution.py:381

commit v2 on v1

v2 whole, which is shorter than its diff:
```python
from functools import partial
import math

import jax
import jax.numpy as jnp
from jax import lax
from jax.experimental import pallas as pl
from jax.experimental.pallas import tpu as pltpu
from jax.sharding import PartitionSpec as P

HD = 128
UNIT = 128
CHUNK_UNITS = 4
LOW = -1e30
LARGE = 2.0**90
VMEM_LIMIT = 24 * 1024 * 1024
HBM = pl.BlockSpec(memory_space=pl.ANY)
SMEM = pl.BlockSpec(memory_space=pltpu.SMEM)
VMEM = pl.BlockSpec(memory_space=pltpu.VMEM)


def params():
    return pltpu.CompilerParams(vmem_limit_bytes=VMEM_LIMIT)


def run_copies(copies):
    for copy in copies:
        copy.start()
    for copy in copies:
        copy.wait()


def pack_kernel(group, *refs):
    packed = refs[group]
    rows = refs[0].shape[0]
    member = lax.rem(lax.axis_index("ctx"), group)
    for step in range(group):
        packed[pl.ds(pl.multiple_of((member ^ step) * rows, rows), rows), :] = refs[step][...]


def pack_rows(pieces):
    group = len(pieces)
    rows, columns = pieces[0].shape
    return pl.pallas_call(
        partial(pack_kernel, group),
        out_shape=jax.ShapeDtypeStruct((rows * group, columns), pieces[0].dtype),
        compiler_params=params(),
    )(*pieces)


def attention_kernel(mode, steps, group, regions, heads, docs, *refs):
    refs = list(refs)

    def take(number):
        taken = refs[:number]
        del refs[:number]
        return taken

    pieces = len(steps)
    early, late = mode == "early", mode == "late"
    (docs_ref,) = take(1)
    queries = take(pieces)
    keys = take(regions)
    values = take(regions)
    if early:
        (w_from,) = take(1)
    if late:
        (state,) = take(1)
        take(pieces)
    outs = take(pieces)
    if early:
        state, w_to = take(2)
    q_buf, o_buf, shift, total, in_sem, out_sem = refs
    tokens = queries[0].shape[0]
    units = tokens // UNIT
    sizes = [key.shape[0] // UNIT for key in keys]
    bases = [sum(sizes[:region]) for region in range(regions)]
    chunk_units = CHUNK_UNITS if sizes[0] % CHUNK_UNITS == 0 else units
    chunk = chunk_units * UNIT
    rank = lax.axis_index("ctx")
    member = lax.rem(rank, group)
    first_unit = (rank - member + group) * units - sum(sizes)
    unseen = 0 if early else bases[1] if late else None
    visited = keys[:1] if late else keys
    scale = math.log2(math.e) / math.sqrt(HD)

    def place(piece):
        here = (rank ^ (steps[0] - piece)) * units
        starts = []
        for unit in range(units):
            doc_first = jnp.int32(0)
            end = jnp.int32(0)
            for doc in range(docs):
                end = end + docs_ref[doc]
                doc_first = jnp.where(end <= here + unit, end, doc_first)
            starts.append(doc_first - first_unit)
        return here - first_unit, starts

    def load():
        run_copies([
            pltpu.make_async_copy(queries[piece], q_buf.at[piece], in_sem.at[piece]) for piece in range(pieces)
        ])

    def one_piece(piece):
        ones = jnp.ones((chunk, HD), jnp.bfloat16)
        square = jnp.ones((HD, HD), jnp.bfloat16)
        first_row, starts = place(piece)
        lows = [jnp.maximum(start, 0) for start in starts]
        low, high, stop = lows[0], lows[-1], first_row + units
        query = jnp.concatenate([q_buf[piece, :, head * HD:(head + 1) * HD] for head in range(heads)], axis=0)

        def scores_of(region, number, masked, query):
            begin_unit = bases[region] + number * chunk_units
            begin = pl.multiple_of(number * chunk, chunk)
            key = keys[region][pl.ds(begin, chunk), :]
            value = jnp.concatenate([values[region][pl.ds(begin, chunk), :], ones], axis=1)
            scores = lax.dot_general(query, key, (((1,), (1,)), ((), ())), preferred_element_type=jnp.float32)
            if masked:
                column = lax.broadcasted_iota(jnp.int32, (UNIT, chunk), 1)
                ahead = column - lax.broadcasted_iota(jnp.int32, (UNIT, chunk), 0)
                allowed = [
                    (column >= (lows[unit] - begin_unit) * UNIT) & (ahead <= (first_row + unit - begin_unit) * UNIT)
                    for unit in range(units)
                ]
                scores = jnp.concatenate([
                    jnp.where(allowed[part % units], scores[part * UNIT:(part + 1) * UNIT], LOW)
                    for part in range(query.shape[0] // UNIT)
                ], axis=0)
            return scores, value

        own_start = pl.multiple_of((first_row - bases[-1]) * UNIT, UNIT)
        own = query * jnp.concatenate([keys[-1][pl.ds(own_start, tokens), :]] * heads, axis=0)
        shift[...] = jnp.dot(own, square, preferred_element_type=jnp.float32) * scale
        if late:
            total[...] = state[piece]
        else:
            total[...] = jnp.zeros(total.shape, jnp.float32)

        def visit(region, number, masked):
            scores, value = scores_of(region, number, masked, query)
            shifts = jnp.concatenate([shift[...]] * chunk_units, axis=1)
            weights = jnp.exp2(scores * scale - shifts).astype(jnp.bfloat16)
            total[...] += jnp.dot(weights, value, preferred_element_type=jnp.float32)

        def span(region):
            count = sizes[region] // chunk_units
            first = jnp.clip((low - bases[region]) // chunk_units, 0, count)
            last = jnp.clip((stop - bases[region] + chunk_units - 1) // chunk_units, 0, count)
            return first, jnp.maximum(first, last)

        for region in range(len(visited)):
            first, last = span(region)
            inner = jnp.clip((high - bases[region] + chunk_units - 1) // chunk_units, first, last)
            outer = jnp.clip((first_row - bases[region]) // chunk_units, inner, last)

            def masked_visit(number, carry, region=region, first=first, inner=inner, outer=outer):
                at = first + number
                visit(region, jnp.where(at < inner, at, at - inner + outer), True)
                return carry

            def plain_visit(number, carry, region=region):
                visit(region, number, False)
                return carry

            lax.fori_loop(0, inner - first + last - outer, masked_visit, 0)
            lax.fori_loop(inner, outer, plain_visit, 0)

        overflow = jnp.logical_not(jnp.max(total[:, HD:]) < LARGE)
        if early:
            unfinished = starts[0] < unseen
            overflow = overflow & jnp.logical_not(unfinished)

            @pl.when(unfinished)
            def _():
                state[piece] = total[...]

        @pl.when(overflow)
        def _():
            shift[...] = jnp.full(shift.shape, LOW, jnp.float32)
            total[...] = jnp.zeros(total.shape, jnp.float32)

            for region in reversed(range(regions)):
                first, last = span(region)

                def careful(number, carry, region=region, first=first):
                    head = lax.rem(number, heads)
                    some = pl.ds(pl.multiple_of(head * tokens, tokens), tokens)
                    query = q_buf[piece, :, pl.ds(pl.multiple_of(head * HD, HD), HD)]
                    scores, value = scores_of(region, first + number // heads, True, query)
                    old = shift[some, :]
                    new = jnp.maximum(old, jnp.max(scores, axis=1, keepdims=True))
                    weights = jnp.exp2((scores - new[:, :1]) * scale).astype(jnp.bfloat16)
                    shrink = jnp.exp2((old - new) * scale)
                    update = jnp.dot(weights, value, preferred_element_type=jnp.float32)
                    total[some, :] = total[some, :] * jnp.concatenate([shrink] * 2, axis=1) + update
                    shift[some, :] = new
                    return carry

                lax.fori_loop(0, (last - first) * heads, careful, 0)

        result = (total[:, :HD] / total[:, HD:]).astype(jnp.bfloat16)
        for head in range(heads):
            o_buf[piece, :, head * HD:(head + 1) * HD] = result[head * tokens:(head + 1) * tokens]

    if late:
        def needs(piece):
            return place(piece)[1][0] < unseen

        @pl.when(sum(needs(jnp.int32(piece)).astype(jnp.int32) for piece in range(pieces)) > 0)
        def _():
            load()

            def maybe(piece, carry):
                @pl.when(needs(piece))
                def _():
                    one_piece(piece)

                return carry

            lax.fori_loop(0, pieces, maybe, 0)
            for piece in range(pieces):

                @pl.when(needs(jnp.int32(piece)))
                def _():
                    run_copies([pltpu.make_async_copy(o_buf.at[piece], outs[piece], out_sem.at[piece])])
    else:
        if early:
            w_copy = pltpu.make_async_copy(w_from, w_to, out_sem.at[pieces])
            w_copy.start()
        load()

        def always(piece, carry):
            one_piece(piece)
            return carry

        lax.fori_loop(0, pieces, always, 0)
        run_copies([
            pltpu.make_async_copy(o_buf.at[piece], outs[piece], out_sem.at[piece]) for piece in range(pieces)
        ])
        if early:
            w_copy.wait()


def attend(mode, steps, group, doc_units, queries, keys, values, w_out=None, state=None, outs=None):
    pieces = len(steps)
    regions = len(keys)
    tokens, width = queries[0].shape
    heads = width // HD
    rows = heads * tokens
    seen = sum(key.shape[0] for key in (keys[:1] if mode == "late" else keys))
    scores = rows * pieces * seen // 2
    operands = [doc_units, *queries, *keys, *values]
    in_specs = [SMEM] + [HBM] * pieces + [VMEM] * (2 * regions)
    out_shape = [jax.ShapeDtypeStruct((tokens, width), jnp.bfloat16)] * pieces
    out_specs = [HBM] * pieces
    aliases = {}
    moved = 4 * tokens * pieces * width
    if mode == "early":
        operands += [w_out]
        in_specs += [HBM]
        out_shape += [pltpu.VMEM((pieces, rows, 2 * HD), jnp.float32), pltpu.VMEM(w_out.shape, w_out.dtype)]
        out_specs += [VMEM, VMEM]
        moved += 2 * w_out.size
    if mode == "late":
        aliases = {len(operands) + 1 + piece: piece for piece in range(pieces)}
        operands += [pltpu.with_memory_space_constraint(state, pltpu.VMEM), *outs]
        in_specs += [VMEM] + [HBM] * pieces
    return pl.pallas_call(
        partial(attention_kernel, mode, steps, group, regions, heads, doc_units.shape[0]),
        out_shape=out_shape,
        in_specs=in_specs,
        out_specs=out_specs,
        scratch_shapes=[
            pltpu.VMEM((pieces, tokens, width), jnp.bfloat16),
            pltpu.VMEM((pieces, tokens, width), jnp.bfloat16),
            pltpu.VMEM((rows, HD), jnp.float32),
            pltpu.VMEM((rows, 2 * HD), jnp.float32),
            pltpu.SemaphoreType.DMA((pieces,)),
            pltpu.SemaphoreType.DMA((pieces + 1,)),
        ],
        input_output_aliases=aliases,
        compiler_params=params(),
        cost_estimate=pl.CostEstimate(flops=4 * HD * scores, transcendentals=scores, bytes_accessed=moved),
    )(*operands)


def project_kernel(group, first, tile, *refs):
    pieces = refs[:group]
    w_ref, give_ref, keep_ref, a_buf, sem = refs[group:]
    width = pieces[0].shape[1]
    member = lax.rem(lax.axis_index("ctx"), group)

    @pl.when(pl.program_id(0) == 0)
    def _():
        copies = []
        for step in range(group):
            start = pl.multiple_of((member ^ step) * width, width)
            copies.append(
                pltpu.make_async_copy(pieces[step], a_buf.at[:, pl.ds(start, width)], sem.at[step])
            )
        run_copies(copies)

    start = pl.multiple_of(first + pl.program_id(0) * tile, tile)
    product = jnp.dot(a_buf[...], w_ref[:, pl.ds(start, tile)], preferred_element_type=jnp.float32)
    product = product.astype(jnp.bfloat16)
    block = product.shape[0] // 2
    low_first = lax.axis_index("head") == 0
    keep_ref[...] = jnp.where(low_first, product[:block], product[block:])
    give_ref[...] = jnp.where(low_first, product[block:], product[:block])


def project(pieces, w_out, first, columns, tile):
    group = len(pieces)
    rows, width = pieces[0].shape
    depth = w_out.shape[0]
    half = jax.ShapeDtypeStruct((rows // 2, columns), jnp.bfloat16)
    spec = pl.BlockSpec((rows // 2, tile), lambda step: (0, step))
    return pl.pallas_call(
        partial(project_kernel, group, first, tile),
        out_shape=[half, half],
        grid=(columns // tile,),
        in_specs=[HBM] * group + [pl.BlockSpec(memory_space=pltpu.VMEM)],
        out_specs=[spec, spec],
        scratch_shapes=[pltpu.VMEM((rows, depth), jnp.bfloat16), pltpu.SemaphoreType.DMA((group,))],
        compiler_params=params(),
        cost_estimate=pl.CostEstimate(
            flops=2 * rows * depth * columns, transcendentals=0, bytes_accessed=4 * rows * columns
        ),
    )(*pieces, w_out)


def sum_kernel(*refs):
    out_ref = refs[-1]
    halves = (len(refs) - 1) // 2
    columns = refs[0].shape[1]
    for half in range(halves):
        summed = refs[half][...].astype(jnp.float32) + refs[halves + half][...].astype(jnp.float32)
        out_ref[:, half * columns:(half + 1) * columns] = summed.astype(jnp.bfloat16)


def shards(queries, key_heads, value_heads, doc_units, w_out):
    count = lax.axis_size("ctx")
    group = key_heads.shape[1] // HD
    hops = min(16, count // 2) // group
    tokens, depth = queries.shape
    width = depth // group
    rank = lax.axis_index("ctx")
    member = lax.rem(rank, group)

    def column_block(value, step, size):
        return lax.dynamic_slice(value, (0, (member ^ step) * size), (tokens, size))

    def swap(value, step):
        if step == 0:
            return value
        return lax.ppermute(value, "ctx", [(source, source ^ step) for source in range(count)])

    def next_plane(value):
        return lax.ppermute(value, "ctx", [(source, source + group) for source in range(count - group)])

    def own_plane(value):
        pieces = [swap(column_block(value, step, HD), step) for step in range(group)]
        return pack_rows(pieces) if group > 1 else pieces[0]

    keys, values = [own_plane(key_heads)], [own_plane(value_heads)]
    queries = lax.optimization_barrier((queries, keys, values))[0]
    query_pieces = [swap(column_block(queries, step, width), step) for step in range(group)]
    keys = [next_plane(keys[0])] + keys
    values = [next_plane(values[0])] + values
    if group > 1:
        keys, values, query_pieces[-1] = lax.optimization_barrier((keys, values, query_pieces[-1]))
    for hop in range(hops - 1):
        keys = [next_plane(keys[0])] + keys
        values = [next_plane(values[0])] + values
    if group == 1:
        keys, values = [jnp.concatenate(keys, axis=0)], [jnp.concatenate(values, axis=0)]

    def place_in_vmem(arrays):
        return [pltpu.with_memory_space_constraint(array, pltpu.VMEM) for array in arrays]

    keys, values = place_in_vmem(keys), place_in_vmem(values)
    w_here = w_out
    attention = [None] * group
    far = tuple(range(group - 1, 0, -1))
    if far:
        far_queries = [query_pieces[step] for step in far]
        *partials, state, w_here = attend("early", far, group, doc_units, far_queries, keys[-2:], values[-2:], w_out=w_out)
        finals = attend("late", far, group, doc_units, far_queries, keys, values, state=state, outs=partials)
        for step, final in zip(far, finals):
            attention[step] = swap(final, step)
        query_pieces, finals = lax.optimization_barrier((query_pieces, finals))
    (attention[0],) = attend("full", (0,), group, doc_units, query_pieces[:1], keys, values)
    columns = w_out.shape[1]
    if lax.axis_size("head") == 2:
        w_here = pltpu.with_memory_space_constraint(w_here, pltpu.VMEM)
        size = columns // 2
        keeps, gots = [], []
        for half in range(2):
            give, keep = project(attention, w_here, half * size, size, 512)
            keeps.append(keep)
            gots.append(lax.ppermute(give, "head", [(0, 1), (1, 0)]))
        return pl.pallas_call(
            sum_kernel,
            out_shape=jax.ShapeDtypeStruct((tokens // 2, columns), jnp.bfloat16),
            compiler_params=params(),
        )(*keeps, *gots)
    product = sum(
        jnp.dot(
            attention[step],
            lax.dynamic_slice(w_out, ((member ^ step) * width, 0), (width, columns)),
            preferred_element_type=jnp.float32,
        )
        for step in range(group)
    )
    return lax.psum_scatter(product.astype(jnp.bfloat16), "head", scatter_dimension=0, tiled=True)


def solution(mesh):
    in_specs = (P("ctx", "head"), P("ctx", "head"), P("ctx", "head"), P(), P("head", None))
    out_specs = P(("ctx", "head"), None)
    return jax.shard_map(shards, mesh=mesh, in_specs=in_specs, out_specs=out_specs, check_vma=False)
```

time: 98.9 us -> 94.3 us (0.953)
  the two profiles are of different devices: /device:TPU:25 before, /device:TPU:19 now
where the time goes in v2:
time: 94.3 us; the launch traced here: 92.7 us
  Pallas kernels  40.1 us (43%)
  waiting for transfers between devices  24.7 us (26%)
  starting transfers between devices  24.1 us (26%)
  local copies, waits for them, and re-layouts  3.63 us (4%)
    pallas_call x3, Pallas kernels, attend(): pl.pallas_call(partial(attention_kernel, mode, steps, group, regions, hea...  29.9 us
    ppermute x12, waiting for transfers between devices, swap(): lax.ppermute(value, 'ctx', [(source, source ^ step) for source in range(c...  15.6 us
    ppermute x12, starting transfers between devices, swap(): lax.ppermute(value, 'ctx', [(source, source ^ step) for source in range(c...  11.9 us
    ppermute x4, starting transfers between devices, next_plane(): lax.ppermute(value, 'ctx', [(source, source + group) for source in range(...  11.4 us
    pallas_call x2, Pallas kernels, project(): pl.pallas_call(partial(project_kernel, group, first, tile), out_shape=[ha...  8.63 us
    ppermute x4, waiting for transfers between devices, next_plane(): lax.ppermute(value, 'ctx', [(source, source + group) for source in range(...  6.93 us
    dynamic_slice x3, local copies, waits for them, and re-layouts, column_block(): return lax.dynamic_slice(value, (0, (member ^ step) * size), (tokens, size))  3.63 us
    ppermute x2, waiting for transfers between devices, shards(): gots.append(lax.ppermute(give, 'head', [(0, 1), (1, 0)]))  2.23 us
  transfers between devices with their start and end apart: 18, of which 8 were waited for; matrix products, arithmetic and copies ran while one was open for 3% of the time, Pallas kernels for 36%

profile of v2, /device:TPU:19, one launch (start us, length us, event | category | flops | bytes accessed | tf_op | source)
XLA Modules:
  0.0 92.7 jit_solution(5802053183163881563)
XLA Ops:
  0.0 0.0 copy-start
  0.0 1.1 %constant_dynamic-slice_fusion.4 = (bf16[384,128]{1,0:T(8,128)(2,1)S(1)}, bf16[384,128]{1,0:T(8,128)(2,1)S(1)}, bf16[384,128]{1,0:T(8,128)(2,1)S(1)}, bf16[384,128]{1,0:T(8,128)(2,1)S(1)}) fusion(bf16[384,512]{1,0:T(8,128)(2,1)} %param.7, s32[]{:T(128)S(6)} %select_n.31, s32[]{:T(128)S(6)} %select_n.29, s32[]{:T(128)S(6)} %select_n.28, s32[]{:T(128)S(6)} %select_n.30), kind=kLoop, calls=%fused_computation.4 | loop fusion | bytes 786448 | tf_op jit(solution)/shard_map/dynamic_slice | solution.py:351
  1.1 1.3 %collective-permute-start.5 = (bf16[384,128]{1,0:T(8,128)(2,1)S(1)}, bf16[384,128]{1,0:T(8,128)(2,1)S(1)}, u32[]{:S(2)}, u32[]{:S(2)}) collective-permute-start(bf16[384,128]{1,0:T(8,128)(2,1)S(1)} %get-tuple-element.47), channel_id=1, source_target_pairs={{0,6},{2,4},{4,2},{6,0},{8,14},{10,12},{12,10},{14,8},{16,22},{18,... | collective-permute-start | bytes 294920 | tf_op jit(solution)/shard_map/ppermute | solution.py:356
  2.4 1.2 %collective-permute-start.3 = (bf16[384,128]{1,0:T(8,128)(2,1)S(1)}, bf16[384,128]{1,0:T(8,128)(2,1)S(1)}, u32[]{:S(2)}, u32[]{:S(2)}) collective-permute-start(bf16[384,128]{1,0:T(8,128)(2,1)S(1)} %get-tuple-element.48), channel_id=1, source_target_pairs={{0,2},{2,0},{4,6},{6,4},{8,10},{10,8},{12,14},{14,12},{16,18},{18,... | collective-permute-start | bytes 294920 | tf_op jit(solution)/shard_map/ppermute | solution.py:356
  3.6 0.2 collective-permute-start.4
  3.8 1.1 %constant_dynamic-slice_fusion.8 = (bf16[384,128]{1,0:T(8,128)(2,1)S(1)}, bf16[384,128]{1,0:T(8,128)(2,1)S(1)}, bf16[384,128]{1,0:T(8,128)(2,1)S(1)}, bf16[384,128]{1,0:T(8,128)(2,1)S(1)}) fusion(bf16[384,512]{1,0:T(8,128)(2,1)} %param.6, s32[]{:T(128)S(6)} %select_n.31, s32[]{:T(128)S(6)} %select_n.29, s32[]{:T(128)S(6)} %select_n.28, s32[]{:T(128)S(6)} %select_n.30), kind=kLoop, calls=%fused_computation.8 | loop fusion | bytes 786448 | tf_op jit(solution)/shard_map/dynamic_slice | solution.py:351
  4.9 1.3 %collective-permute-start.2 = (bf16[384,128]{1,0:T(8,128)(2,1)S(1)}, bf16[384,128]{1,0:T(8,128)(2,1)S(1)}, u32[]{:S(2)}, u32[]{:S(2)}) collective-permute-start(bf16[384,128]{1,0:T(8,128)(2,1)S(1)} %get-tuple-element.51), channel_id=1, source_target_pairs={{0,6},{2,4},{4,2},{6,0},{8,14},{10,12},{12,10},{14,8},{16,22},{18,... | collective-permute-start | bytes 294920 | tf_op jit(solution)/shard_map/ppermute | solution.py:356
  6.2 1.2 %collective-permute-start = (bf16[384,128]{1,0:T(8,128)(2,1)S(1)}, bf16[384,128]{1,0:T(8,128)(2,1)S(1)}, u32[]{:S(2)}, u32[]{:S(2)}) collective-permute-start(bf16[384,128]{1,0:T(8,128)(2,1)S(1)} %get-tuple-element.52), channel_id=1, source_target_pairs={{0,2},{2,0},{4,6},{6,4},{8,10},{10,8},{12,14},{14,12},{16,18},{18,... | collective-permute-start | bytes 294920 | tf_op jit(solution)/shard_map/ppermute | solution.py:356
  7.4 0.0 collective-permute-done.5.refs_3_
  7.4 0.2 collective-permute-start.1
  7.6 0.3 collective-permute-done.3.refs_1_
  7.9 0.4 collective-permute-done.4.refs_2_
  8.4 3.2 %collective-permute-start.9 = (bf16[1536,128]{1,0:T(8,128)(2,1)S(1)}, bf16[1536,128]{1,0:T(8,128)(2,1)S(1)}, u32[]{:S(2)}, u32[]{:S(2)}) collective-permute-start(bf16[1536,128]{1,0:T(8,128)(2,1)S(1)} %shard_map.56.refs_7_.refs_9_), channel_id=1, source_target_pairs={{0,8},{2,10},{4,12},{6,14},{8,16},{10,18},{12,20},{14,22},{16,24},... | collective-permute-start | bytes 1179656 | tf_op jit(solution)/shard_map/ppermute | solution.py:359
  11.6 0.0 collective-permute-done.2.refs_3_
  11.6 0.0 collective-permute-done.refs_1_
  11.6 0.8 collective-permute-done.1.refs_2_
  12.5 3.2 %collective-permute-start.8 = (bf16[1536,128]{1,0:T(8,128)(2,1)S(1)}, bf16[1536,128]{1,0:T(8,128)(2,1)S(1)}, u32[]{:S(2)}, u32[]{:S(2)}) collective-permute-start(bf16[1536,128]{1,0:T(8,128)(2,1)S(1)} %shard_map.55.refs_5_.refs_6_.refs_4_), channel_id=1, source_target_pairs={{0,8},{2,10},{4,12},{6,14},{8,16},{10,18},{12,20},{14,22},{16,24},... | collective-permute-start | bytes 1179656 | tf_op jit(solution)/shard_map/ppermute | solution.py:359
  15.7 1.5 %constant_dynamic-slice_fusion = (bf16[384,512]{1,0:T(8,128)(2,1)S(1)}, bf16[384,512]{1,0:T(8,128)(2,1)S(1)}, bf16[384,512]{1,0:T(8,128)(2,1)S(1)}, bf16[384,512]{1,0:T(8,128)(2,1)S(1)}) fusion(bf16[384,2048]{1,0:T(8,128)(2,1)} %param.5, s32[]{:T(128)S(6)} %select_n.35, s32[]{:T(128)S(6)} %select_n.34, s32[]{:T(128)S(6)} %select_n.33, s32[]{:T(128)S(6)} %select_n.32), kind=kLoop, calls=%fused_computation | loop fusion | bytes 3145744 | tf_op jit(solution)/shard_map/dynamic_slice | solution.py:351
  17.2 0.4 collective-permute-start.10
  17.6 1.0 %collective-permute-start.7 = (bf16[384,512]{1,0:T(8,128)(2,1)S(1)}, bf16[384,512]{1,0:T(8,128)(2,1)S(1)}, u32[]{:S(2)}, u32[]{:S(2)}) collective-permute-start(bf16[384,512]{1,0:T(8,128)(2,1)S(1)} %get-tuple-element.44), channel_id=1, source_target_pairs={{0,4},{2,6},{4,0},{6,2},{8,12},{10,14},{12,8},{14,10},{16,20},{18,... | collective-permute-start | bytes 1179656 | tf_op jit(solution)/shard_map/ppermute | solution.py:356
  18.6 1.3 %collective-permute-start.6 = (bf16[384,512]{1,0:T(8,128)(2,1)S(1)}, bf16[384,512]{1,0:T(8,128)(2,1)S(1)}, u32[]{:S(2)}, u32[]{:S(2)}) collective-permute-start(bf16[384,512]{1,0:T(8,128)(2,1)S(1)} %get-tuple-element.45), channel_id=1, source_target_pairs={{0,2},{2,0},{4,6},{6,4},{8,10},{10,8},{12,14},{14,12},{16,18},{18,... | collective-permute-start | bytes 1179656 | tf_op jit(solution)/shard_map/ppermute | solution.py:356
  19.9 0.0 collective-permute-done.9.refs_6_.refs_8_
  19.9 6.9 %collective-permute-done.8.refs_4_.refs_5_.refs_3_ = bf16[1536,128]{1,0:T(8,128)(2,1)S(1)} collective-permute-done((bf16[1536,128]{1,0:T(8,128)(2,1)S(1)}, bf16[1536,128]{1,0:T(8,128)(2,1)S(1)}, u32[]{:S(2)}, u32[]{:S(2)}) %collective-permute-start.8) | collective-permute-done | bytes 393248 | tf_op jit(solution)/shard_map/ppermute | solution.py:359
  26.8 0.1 collective-permute-done.10.refs_1_
  26.9 3.1 %collective-permute-start.11 = (bf16[1536,128]{1,0:T(8,128)(2,1)S(1)}, bf16[1536,128]{1,0:T(8,128)(2,1)S(1)}, u32[]{:S(2)}, u32[]{:S(2)}) collective-permute-start(bf16[1536,128]{1,0:T(8,128)(2,1)S(1)} %collective-permute-done.8.refs_4_.refs_5_.refs_3_), channel_id=1, source_target_pairs={{0,8},{2,10},{4,12},{6,14},{8,16},{10,18},{12,20},{14,22},{16,24},... | collective-permute-start | bytes 1179656 | tf_op jit(solution)/shard_map/ppermute | solution.py:359
  30.0 1.9 %collective-permute-start.12 = (bf16[1536,128]{1,0:T(8,128)(2,1)S(1)}, bf16[1536,128]{1,0:T(8,128)(2,1)S(1)}, u32[]{:S(2)}, u32[]{:S(2)}) collective-permute-start(bf16[1536,128]{1,0:T(8,128)(2,1)S(1)} %collective-permute-done.9.refs_6_.refs_8_), channel_id=1, source_target_pairs={{0,8},{2,10},{4,12},{6,14},{8,16},{10,18},{12,20},{14,22},{16,24},... | collective-permute-start | bytes 1179656 | tf_op jit(solution)/shard_map/ppermute | solution.py:359
  31.9 4.5 %collective-permute-done.7.refs_2_ = bf16[384,512]{1,0:T(8,128)(2,1)S(1)} collective-permute-done((bf16[384,512]{1,0:T(8,128)(2,1)S(1)}, bf16[384,512]{1,0:T(8,128)(2,1)S(1)}, u32[]{:S(2)}, u32[]{:S(2)}) %collective-permute-start.7) | collective-permute-done | bytes 393248 | tf_op jit(solution)/shard_map/ppermute | solution.py:356
  36.4 0.0 collective-permute-done.6.refs_3_
  36.4 0.0 copy-done
  36.5 21.7 %shard_map.57 = (bf16[384,512]{1,0:T(8,128)(2,1)S(1)}, bf16[384,512]{1,0:T(8,128)(2,1)S(1)}, bf16[384,512]{1,0:T(8,128)(2,1)S(1)}, f32[3,1536,256]{2,1,0:T(8,128)S(1)}, bf16[2048,4096]{1,0:T(8,128)(2,1)S(1)}) custom-call(s32[6]{0:T(128)S(1)} %copy-done, bf16[384,512]{1,0:T(8,128)(2,1)S(1)} %collective-permute-done.10.refs_1_, ...), custom_call_target="tpu_custom_call" | custom-call | flops 3623878656 | bytes 19136512 | tf_op jit(solution)/shard_map/pallas_call | solution.py:268
  58.2 0.0 collective-permute-done.11.refs_4_.refs_2_
  58.2 0.0 collective-permute-done.12.refs_7_.refs_5_
  58.2 0.9 shard_map.58
  59.1 0.5 collective-permute-start.15
  59.6 3.2 %collective-permute-start.14 = (bf16[384,512]{1,0:T(8,128)(2,1)S(1)}, bf16[384,512]{1,0:T(8,128)(2,1)S(1)}, u32[]{:S(2)}, u32[]{:S(2)}) collective-permute-start(bf16[384,512]{1,0:T(8,128)(2,1)S(1)} %get-tuple-element.35), channel_id=1, source_target_pairs={{0,4},{2,6},{4,0},{6,2},{8,12},{10,14},{12,8},{14,10},{16,20},{18,... | collective-permute-start | bytes 1179656 | tf_op jit(solution)/shard_map/ppermute | solution.py:356
  62.8 0.0 collective-permute-start.13
  62.8 7.3 %shard_map.59.refs_0_ = bf16[384,512]{1,0:T(8,128)(2,1)S(1)} custom-call(s32[6]{0:T(128)S(1)} %copy-done, bf16[384,512]{1,0:T(8,128)(2,1)S(1)} %get-tuple-element.37.refs_1_, bf16[1536,128]{1,0:T(8,128)(2,1)S(1)} %collective-permute-done.11.refs_4_.refs_2_, bf16[1536,128]{1,0:T(8,128)(2,1)S(1)} %collective-permute-done.8.refs_4_.refs_5_.refs_3_, ...), custom_call_target="tpu_custom_call" | custom-call | flops 1811939328 | bytes 786432 | tf_op jit(solution)/shard_map/pallas_call | solution.py:268
  70.1 0.0 collective-permute-done.15.refs_3_
  70.1 9.4 %collective-permute-done.14.refs_2_ = bf16[384,512]{1,0:T(8,128)(2,1)S(1)} collective-permute-done((bf16[384,512]{1,0:T(8,128)(2,1)S(1)}, bf16[384,512]{1,0:T(8,128)(2,1)S(1)}, u32[]{:S(2)}, u32[]{:S(2)}) %collective-permute-start.14) | collective-permute-done | bytes 393248 | tf_op jit(solution)/shard_map/ppermute | solution.py:356
  79.5 0.0 collective-permute-done.13.refs_1_
  79.5 4.3 %shard_map.61 = (bf16[192,2048]{1,0:T(8,128)(2,1)S(1)}, bf16[192,2048]{1,0:T(8,128)(2,1)S(1)}) custom-call(bf16[384,512]{1,0:T(8,128)(2,1)S(1)} %shard_map.59.refs_0_, bf16[384,512]{1,0:T(8,128)(2,1)S(1)} %collective-permute-done.13.refs_1_, bf16[384,512]{1,0:T(8,128)(2,1)S(1)} %collective-permute-done.14.refs_2_, ...), custom_call_target="tpu_custom_call" | custom-call | flops 3221225472 | bytes 3145728 | tf_op jit(solution)/shard_map/pallas_call | solution.py:318
  83.8 0.7 collective-permute-start.17
  84.6 4.3 %shard_map.60 = (bf16[192,2048]{1,0:T(8,128)(2,1)S(1)}, bf16[192,2048]{1,0:T(8,128)(2,1)S(1)}) custom-call(bf16[384,512]{1,0:T(8,128)(2,1)S(1)} %shard_map.59.refs_0_, bf16[384,512]{1,0:T(8,128)(2,1)S(1)} %collective-permute-done.13.refs_1_, bf16[384,512]{1,0:T(8,128)(2,1)S(1)} %collective-permute-done.14.refs_2_, ...), custom_call_target="tpu_custom_call" | custom-call | flops 3221225472 | bytes 3145728 | tf_op jit(solution)/shard_map/pallas_call | solution.py:318
  88.9 0.1 collective-permute-start.16
  89.0 0.0 collective-permute-done.17.refs_3_
  89.0 2.2 %collective-permute-done.16.refs_2_ = bf16[192,2048]{1,0:T(8,128)(2,1)S(1)} collective-permute-done((bf16[192,2048]{1,0:T(8,128)(2,1)S(1)}, bf16[192,2048]{1,0:T(8,128)(2,1)S(1)}, u32[]{:S(2)}, u32[]{:S(2)}) %collective-permute-start.16) | collective-permute-done | bytes 786464 | tf_op jit(solution)/shard_map/ppermute | solution.py:401
  91.2 1.5 %shard_map.62 = bf16[192,4096]{1,0:T(8,128)(2,1)} custom-call(bf16[192,2048]{1,0:T(8,128)(2,1)S(1)} %get-tuple-element.39.refs_0_, bf16[192,2048]{1,0:T(8,128)(2,1)S(1)} %get-tuple-element.40.refs_1_, bf16[192,2048]{1,0:T(8,128)(2,1)S(1)} %collective-permute-done.16.refs_2_, bf16[192,2048]{1,0:T(8,128)(2,1)S(1)} %collective-permute-done.17.refs_3_), custom_call_target="tpu_custom_call" | custom-call | tf_op jit(solution)/shard_map/pallas_call | solution.py:402
  (2 shorter events, 0.1 us)
Async XLA Ops:
  0.0 36.5 %copy-start = (s32[6]{0:T(128)S(1)}, s32[6]{0:T(128)}, u32[]{:S(2)}) copy-start(s32[6]{0:T(128)} %refs_0_.5) | copy-start | bytes 76
  1.1 6.3 %collective-permute-start.5 = (bf16[384,128]{1,0:T(8,128)(2,1)S(1)}, bf16[384,128]{1,0:T(8,128)(2,1)S(1)}, u32[]{:S(2)}, u32[]{:S(2)}) collective-permute-start(bf16[384,128]{1,0:T(8,128)(2,1)S(1)} %get-tuple-element.47), channel_id=1, source_target_pairs={{0,6},{2,4},{4,2},{6,0},{8,14},{10,12},{12,10},{14,8},{16,22},{18,... | collective-permute-start | bytes 294920 | tf_op jit(solution)/shard_map/ppermute | solution.py:356
  2.4 5.5 %collective-permute-start.3 = (bf16[384,128]{1,0:T(8,128)(2,1)S(1)}, bf16[384,128]{1,0:T(8,128)(2,1)S(1)}, u32[]{:S(2)}, u32[]{:S(2)}) collective-permute-start(bf16[384,128]{1,0:T(8,128)(2,1)S(1)} %get-tuple-element.48), channel_id=1, source_target_pairs={{0,2},{2,0},{4,6},{6,4},{8,10},{10,8},{12,14},{14,12},{16,18},{18,... | collective-permute-start | bytes 294920 | tf_op jit(solution)/shard_map/ppermute | solution.py:356
  3.6 4.7 %collective-permute-start.4 = (bf16[384,128]{1,0:T(8,128)(2,1)S(1)}, bf16[384,128]{1,0:T(8,128)(2,1)S(1)}, u32[]{:S(2)}, u32[]{:S(2)}) collective-permute-start(bf16[384,128]{1,0:T(8,128)(2,1)S(1)} %get-tuple-element.50), channel_id=1, source_target_pairs={{0,4},{2,6},{4,0},{6,2},{8,12},{10,14},{12,8},{14,10},{16,20},{18,... | collective-permute-start | bytes 294920 | tf_op jit(solution)/shard_map/ppermute | solution.py:356
  4.9 6.7 %collective-permute-start.2 = (bf16[384,128]{1,0:T(8,128)(2,1)S(1)}, bf16[384,128]{1,0:T(8,128)(2,1)S(1)}, u32[]{:S(2)}, u32[]{:S(2)}) collective-permute-start(bf16[384,128]{1,0:T(8,128)(2,1)S(1)} %get-tuple-element.51), channel_id=1, source_target_pairs={{0,6},{2,4},{4,2},{6,0},{8,14},{10,12},{12,10},{14,8},{16,22},{18,... | collective-permute-start | bytes 294920 | tf_op jit(solution)/shard_map/ppermute | solution.py:356
  6.2 5.5 %collective-permute-start = (bf16[384,128]{1,0:T(8,128)(2,1)S(1)}, bf16[384,128]{1,0:T(8,128)(2,1)S(1)}, u32[]{:S(2)}, u32[]{:S(2)}) collective-permute-start(bf16[384,128]{1,0:T(8,128)(2,1)S(1)} %get-tuple-element.52), channel_id=1, source_target_pairs={{0,2},{2,0},{4,6},{6,4},{8,10},{10,8},{12,14},{14,12},{16,18},{18,... | collective-permute-start | bytes 294920 | tf_op jit(solution)/shard_map/ppermute | solution.py:356
  7.4 5.1 %collective-permute-start.1 = (bf16[384,128]{1,0:T(8,128)(2,1)S(1)}, bf16[384,128]{1,0:T(8,128)(2,1)S(1)}, u32[]{:S(2)}, u32[]{:S(2)}) collective-permute-start(bf16[384,128]{1,0:T(8,128)(2,1)S(1)} %get-tuple-element.54), channel_id=1, source_target_pairs={{0,4},{2,6},{4,0},{6,2},{8,12},{10,14},{12,8},{14,10},{16,20},{18,... | collective-permute-start | bytes 294920 | tf_op jit(solution)/shard_map/ppermute | solution.py:356
  8.4 11.5 %collective-permute-start.9 = (bf16[1536,128]{1,0:T(8,128)(2,1)S(1)}, bf16[1536,128]{1,0:T(8,128)(2,1)S(1)}, u32[]{:S(2)}, u32[]{:S(2)}) collective-permute-start(bf16[1536,128]{1,0:T(8,128)(2,1)S(1)} %shard_map.56.refs_7_.refs_9_), channel_id=1, source_target_pairs={{0,8},{2,10},{4,12},{6,14},{8,16},{10,18},{12,20},{14,22},{16,24},... | collective-permute-start | bytes 1179656 | tf_op jit(solution)/shard_map/ppermute | solution.py:359
  12.5 14.3 %collective-permute-start.8 = (bf16[1536,128]{1,0:T(8,128)(2,1)S(1)}, bf16[1536,128]{1,0:T(8,128)(2,1)S(1)}, u32[]{:S(2)}, u32[]{:S(2)}) collective-permute-start(bf16[1536,128]{1,0:T(8,128)(2,1)S(1)} %shard_map.55.refs_5_.refs_6_.refs_4_), channel_id=1, source_target_pairs={{0,8},{2,10},{4,12},{6,14},{8,16},{10,18},{12,20},{14,22},{16,24},... | collective-permute-start | bytes 1179656 | tf_op jit(solution)/shard_map/ppermute | solution.py:359
  17.2 9.7 %collective-permute-start.10 = (bf16[384,512]{1,0:T(8,128)(2,1)S(1)}, bf16[384,512]{1,0:T(8,128)(2,1)S(1)}, u32[]{:S(2)}, u32[]{:S(2)}) collective-permute-start(bf16[384,512]{1,0:T(8,128)(2,1)S(1)} %get-tuple-element.43), channel_id=1, source_target_pairs={{0,6},{2,4},{4,2},{6,0},{8,14},{10,12},{12,10},{14,8},{16,22},{18,... | collective-permute-start | bytes 1179656 | tf_op jit(solution)/shard_map/ppermute | solution.py:356
  17.6 18.9 %collective-permute-start.7 = (bf16[384,512]{1,0:T(8,128)(2,1)S(1)}, bf16[384,512]{1,0:T(8,128)(2,1)S(1)}, u32[]{:S(2)}, u32[]{:S(2)}) collective-permute-start(bf16[384,512]{1,0:T(8,128)(2,1)S(1)} %get-tuple-element.44), channel_id=1, source_target_pairs={{0,4},{2,6},{4,0},{6,2},{8,12},{10,14},{12,8},{14,10},{16,20},{18,... | collective-permute-start | bytes 1179656 | tf_op jit(solution)/shard_map/ppermute | solution.py:356
  18.6 17.8 %collective-permute-start.6 = (bf16[384,512]{1,0:T(8,128)(2,1)S(1)}, bf16[384,512]{1,0:T(8,128)(2,1)S(1)}, u32[]{:S(2)}, u32[]{:S(2)}) collective-permute-start(bf16[384,512]{1,0:T(8,128)(2,1)S(1)} %get-tuple-element.45), channel_id=1, source_target_pairs={{0,2},{2,0},{4,6},{6,4},{8,10},{10,8},{12,14},{14,12},{16,18},{18,... | collective-permute-start | bytes 1179656 | tf_op jit(solution)/shard_map/ppermute | solution.py:356
  26.9 31.3 %collective-permute-start.11 = (bf16[1536,128]{1,0:T(8,128)(2,1)S(1)}, bf16[1536,128]{1,0:T(8,128)(2,1)S(1)}, u32[]{:S(2)}, u32[]{:S(2)}) collective-permute-start(bf16[1536,128]{1,0:T(8,128)(2,1)S(1)} %collective-permute-done.8.refs_4_.refs_5_.refs_3_), channel_id=1, source_target_pairs={{0,8},{2,10},{4,12},{6,14},{8,16},{10,18},{12,20},{14,22},{16,24},... | collective-permute-start | bytes 1179656 | tf_op jit(solution)/shard_map/ppermute | solution.py:359
  30.0 28.2 %collective-permute-start.12 = (bf16[1536,128]{1,0:T(8,128)(2,1)S(1)}, bf16[1536,128]{1,0:T(8,128)(2,1)S(1)}, u32[]{:S(2)}, u32[]{:S(2)}) collective-permute-start(bf16[1536,128]{1,0:T(8,128)(2,1)S(1)} %collective-permute-done.9.refs_6_.refs_8_), channel_id=1, source_target_pairs={{0,8},{2,10},{4,12},{6,14},{8,16},{10,18},{12,20},{14,22},{16,24},... | collective-permute-start | bytes 1179656 | tf_op jit(solution)/shard_map/ppermute | solution.py:359
  59.1 11.0 %collective-permute-start.15 = (bf16[384,512]{1,0:T(8,128)(2,1)S(1)}, bf16[384,512]{1,0:T(8,128)(2,1)S(1)}, u32[]{:S(2)}, u32[]{:S(2)}) collective-permute-start(bf16[384,512]{1,0:T(8,128)(2,1)S(1)} %get-tuple-element.34), channel_id=1, source_target_pairs={{0,6},{2,4},{4,2},{6,0},{8,14},{10,12},{12,10},{14,8},{16,22},{18,... | collective-permute-start | bytes 1179656 | tf_op jit(solution)/shard_map/ppermute | solution.py:356
  59.6 19.9 %collective-permute-start.14 = (bf16[384,512]{1,0:T(8,128)(2,1)S(1)}, bf16[384,512]{1,0:T(8,128)(2,1)S(1)}, u32[]{:S(2)}, u32[]{:S(2)}) collective-permute-start(bf16[384,512]{1,0:T(8,128)(2,1)S(1)} %get-tuple-element.35), channel_id=1, source_target_pairs={{0,4},{2,6},{4,0},{6,2},{8,12},{10,14},{12,8},{14,10},{16,20},{18,... | collective-permute-start | bytes 1179656 | tf_op jit(solution)/shard_map/ppermute | solution.py:356
  62.8 16.7 %collective-permute-start.13 = (bf16[384,512]{1,0:T(8,128)(2,1)S(1)}, bf16[384,512]{1,0:T(8,128)(2,1)S(1)}, u32[]{:S(2)}, u32[]{:S(2)}) collective-permute-start(bf16[384,512]{1,0:T(8,128)(2,1)S(1)} %get-tuple-element.36), channel_id=1, source_target_pairs={{0,2},{2,0},{4,6},{6,4},{8,10},{10,8},{12,14},{14,12},{16,18},{18,... | collective-permute-start | bytes 1179656 | tf_op jit(solution)/shard_map/ppermute | solution.py:356
  83.8 5.1 %collective-permute-start.17 = (bf16[192,2048]{1,0:T(8,128)(2,1)S(1)}, bf16[192,2048]{1,0:T(8,128)(2,1)S(1)}, u32[]{:S(2)}, u32[]{:S(2)}) collective-permute-start(bf16[192,2048]{1,0:T(8,128)(2,1)S(1)} %get-tuple-element.42), channel_id=1, source_target_pairs={{0,1},{1,0},{2,3},{3,2},{4,5},{5,4},{6,7},{7,6},{8,9},{9,8},{10,11... | collective-permute-start | bytes 2359304 | tf_op jit(solution)/shard_map/ppermute | solution.py:401
  88.9 2.4 %collective-permute-start.16 = (bf16[192,2048]{1,0:T(8,128)(2,1)S(1)}, bf16[192,2048]{1,0:T(8,128)(2,1)S(1)}, u32[]{:S(2)}, u32[]{:S(2)}) collective-permute-start(bf16[192,2048]{1,0:T(8,128)(2,1)S(1)} %get-tuple-element.41), channel_id=1, source_target_pairs={{0,1},{1,0},{2,3},{3,2},{4,5},{5,4},{6,7},{7,6},{8,9},{9,8},{10,11... | collective-permute-start | bytes 2359304 | tf_op jit(solution)/shard_map/ppermute | solution.py:401

commit v3 on v2

--- a/solution.py
+++ b/solution.py
@@ -10,7 +10,7 @@
 
 HD = 128
 UNIT = 128
-CHUNK_UNITS = 4
+CHUNK_UNITS = 6
 LOW = -1e30
 LARGE = 2.0**90
 VMEM_LIMIT = 24 * 1024 * 1024
@@ -19,8 +19,8 @@
 VMEM = pl.BlockSpec(memory_space=pltpu.VMEM)
 
 
-def params():
-    return pltpu.CompilerParams(vmem_limit_bytes=VMEM_LIMIT)
+def params(limit=VMEM_LIMIT):
+    return pltpu.CompilerParams(vmem_limit_bytes=limit)
 
 
 def run_copies(copies):
@@ -284,24 +284,24 @@
     )(*operands)
 
 
-def project_kernel(group, first, tile, *refs):
-    pieces = refs[:group]
-    w_ref, give_ref, keep_ref, a_buf, sem = refs[group:]
+def project_kernel(group, steps, first, tile, resumed, last, *refs):
+    refs = list(refs)
+    pieces = [refs.pop(0) for step in steps]
+    w_ref = refs.pop(0)
+    sums = [refs.pop(0)[:, pl.ds(pl.multiple_of(first + pl.program_id(0) * tile, tile), tile)]] if resumed else []
     width = pieces[0].shape[1]
     member = lax.rem(lax.axis_index("ctx"), group)
-
-    @pl.when(pl.program_id(0) == 0)
-    def _():
-        copies = []
-        for step in range(group):
-            start = pl.multiple_of((member ^ step) * width, width)
-            copies.append(
-                pltpu.make_async_copy(pieces[step], a_buf.at[:, pl.ds(start, width)], sem.at[step])
-            )
-        run_copies(copies)
-
     start = pl.multiple_of(first + pl.program_id(0) * tile, tile)
-    product = jnp.dot(a_buf[...], w_ref[:, pl.ds(start, tile)], preferred_element_type=jnp.float32)
+    weights = jnp.concatenate(
+        [w_ref[pl.ds(pl.multiple_of((member ^ step) * width, width), width), pl.ds(start, tile)] for step in steps],
+        axis=0,
+    )
+    rows = jnp.concatenate([piece[...] for piece in pieces], axis=1)
+    product = sum(sums, jnp.dot(rows, weights, preferred_element_type=jnp.float32))
+    if not last:
+        refs[0][:, pl.ds(start, tile)] = product
+        return
+    give_ref, keep_ref = refs
     product = product.astype(jnp.bfloat16)
     block = product.shape[0] // 2
     low_first = lax.axis_index("head") == 0
@@ -309,24 +309,30 @@
     give_ref[...] = jnp.where(low_first, product[block:], product[:block])
 
 
-def project(pieces, w_out, first, columns, tile):
-    group = len(pieces)
+def project(group, steps, pieces, w_out, first, columns, tile, sums=None, last=True):
     rows, width = pieces[0].shape
-    depth = w_out.shape[0]
-    half = jax.ShapeDtypeStruct((rows // 2, columns), jnp.bfloat16)
-    spec = pl.BlockSpec((rows // 2, tile), lambda step: (0, step))
+    depth = width * len(steps)
+    if last:
+        spec = pl.BlockSpec((rows // 2, tile), lambda step: (0, step))
+        out_specs = [spec, spec]
+        out_shape = [jax.ShapeDtypeStruct((rows // 2, columns), jnp.bfloat16)] * 2
+    else:
+        out_specs = VMEM
+        out_shape = pltpu.VMEM((rows, columns), jnp.float32)
+    operands = [*pieces, w_out]
+    if sums is not None:
+        operands.append(sums)
     return pl.pallas_call(
-        partial(project_kernel, group, first, tile),
-        out_shape=[half, half],
+        partial(project_kernel, group, steps, first, tile, sums is not None, last),
+        out_shape=out_shape,
         grid=(columns // tile,),
-        in_specs=[HBM] * group + [pl.BlockSpec(memory_space=pltpu.VMEM)],
-        out_specs=[spec, spec],
-        scratch_shapes=[pltpu.VMEM((rows, depth), jnp.bfloat16), pltpu.SemaphoreType.DMA((group,))],
-        compiler_params=params(),
+        in_specs=[VMEM] * len(operands),
+        out_specs=out_specs,
+        compiler_params=params(10 * 1024 * 1024),
         cost_estimate=pl.CostEstimate(
             flops=2 * rows * depth * columns, transcendentals=0, bytes_accessed=4 * rows * columns
         ),
-    )(*pieces, w_out)
+    )(*operands)
 
 
 def sum_kernel(*refs):
@@ -393,10 +399,22 @@
     columns = w_out.shape[1]
     if lax.axis_size("head") == 2:
         w_here = pltpu.with_memory_space_constraint(w_here, pltpu.VMEM)
+        soon = (0,) + far[:1]
+        rest = tuple(step for step in range(group) if step not in soon)
+        sums = None
+        if rest:
+            sums = project(
+                group, soon, [attention[step] for step in soon], w_here, 0, columns, 512, last=False
+            )
+            sums = pltpu.with_memory_space_constraint(sums, pltpu.VMEM)
+        else:
+            rest = soon
         size = columns // 2
         keeps, gots = [], []
         for half in range(2):
-            give, keep = project(attention, w_here, half * size, size, 512)
+            give, keep = project(
+                group, rest, [attention[step] for step in rest], w_here, half * size, size, 512, sums=sums
+            )
             keeps.append(keep)
             gots.append(lax.ppermute(give, "head", [(0, 1), (1, 0)]))
         return pl.pallas_call(

time: 94.3 us -> 89.9 us (0.953); the launches traced: 92.7 us -> 89.3 us
  waiting for transfers between devices: 24.7 us -> 23.1 us
  starting transfers between devices: 24.1 us -> 23 us
    pallas_call x3, Pallas kernels: 29.9 us -> 28.1 us  [attend(): pl.pallas_call(partial(attention_kernel, mode, steps, group, regions, hea...]
    ppermute x12, waiting for transfers between devices: 15.6 us -> 13.9 us  [swap(): lax.ppermute(value, 'ctx', [(source, source ^ step) for source in range(c...]
    pallas_call x2 -> x3, Pallas kernels: 8.63 us -> 9.85 us  [project(): pl.pallas_call(partial(project_kernel, group, steps, first, tile, sums is...]
    ppermute x12, starting transfers between devices: 11.9 us -> 10.8 us  [swap(): lax.ppermute(value, 'ctx', [(source, source ^ step) for source in range(c...]
  transfers between devices with their start and end apart: 18 -> 18, of which waited for: 8 -> 11; matrix products, arithmetic and copies ran while one was open for 3% -> 3% of each run, Pallas kernels for 36% -> 39%
where the time goes in v3:
time: 89.9 us; the launch traced here: 89.3 us
  Pallas kernels  39.5 us (44%)
  waiting for transfers between devices  23.1 us (26%)
  starting transfers between devices  23 us (26%)
  local copies, waits for them, and re-layouts  3.63 us (4%)
    pallas_call x3, Pallas kernels, attend(): pl.pallas_call(partial(attention_kernel, mode, steps, group, regions, hea...  28.1 us
    ppermute x12, waiting for transfers between devices, swap(): lax.ppermute(value, 'ctx', [(source, source ^ step) for source in range(c...  13.9 us
    ppermute x4, starting transfers between devices, next_plane(): lax.ppermute(value, 'ctx', [(source, source + group) for source in range(...  11.5 us
    ppermute x12, starting transfers between devices, swap(): lax.ppermute(value, 'ctx', [(source, source ^ step) for source in range(c...  10.8 us
    pallas_call x3, Pallas kernels, project(): pl.pallas_call(partial(project_kernel, group, steps, first, tile, sums is...  9.85 us
    ppermute x4, waiting for transfers between devices, next_plane(): lax.ppermute(value, 'ctx', [(source, source + group) for source in range(...  6.93 us
    dynamic_slice x3, local copies, waits for them, and re-layouts, column_block(): return lax.dynamic_slice(value, (0, (member ^ step) * size), (tokens, size))  3.63 us
    ppermute x2, waiting for transfers between devices, shards(): gots.append(lax.ppermute(give, 'head', [(0, 1), (1, 0)]))  2.23 us
  transfers between devices with their start and end apart: 18, of which 11 were waited for; matrix products, arithmetic and copies ran while one was open for 3% of the time, Pallas kernels for 39%

profile of v3, /device:TPU:19, one launch (start us, length us, event | category | flops | bytes accessed | tf_op | source)
XLA Modules:
  0.0 89.3 jit_solution(10542704394250320209)
XLA Ops:
  0.0 0.0 copy-start
  0.0 1.1 %constant_dynamic-slice_fusion.4 = (bf16[384,128]{1,0:T(8,128)(2,1)S(1)}, bf16[384,128]{1,0:T(8,128)(2,1)S(1)}, bf16[384,128]{1,0:T(8,128)(2,1)S(1)}, bf16[384,128]{1,0:T(8,128)(2,1)S(1)}) fusion(bf16[384,512]{1,0:T(8,128)(2,1)} %param.7, s32[]{:T(128)S(6)} %select_n.31, s32[]{:T(128)S(6)} %select_n.29, s32[]{:T(128)S(6)} %select_n.28, s32[]{:T(128)S(6)} %select_n.30), kind=kLoop, calls=%fused_computation.4 | loop fusion | bytes 786448 | tf_op jit(solution)/shard_map/dynamic_slice | solution.py:357
  1.1 1.3 %collective-permute-start.6 = (bf16[384,128]{1,0:T(8,128)(2,1)S(1)}, bf16[384,128]{1,0:T(8,128)(2,1)S(1)}, u32[]{:S(2)}, u32[]{:S(2)}) collective-permute-start(bf16[384,128]{1,0:T(8,128)(2,1)S(1)} %get-tuple-element.47), channel_id=1, source_target_pairs={{0,6},{2,4},{4,2},{6,0},{8,14},{10,12},{12,10},{14,8},{16,22},{18,... | collective-permute-start | bytes 294920 | tf_op jit(solution)/shard_map/ppermute | solution.py:362
  2.4 1.2 %collective-permute-start.4 = (bf16[384,128]{1,0:T(8,128)(2,1)S(1)}, bf16[384,128]{1,0:T(8,128)(2,1)S(1)}, u32[]{:S(2)}, u32[]{:S(2)}) collective-permute-start(bf16[384,128]{1,0:T(8,128)(2,1)S(1)} %get-tuple-element.48), channel_id=1, source_target_pairs={{0,2},{2,0},{4,6},{6,4},{8,10},{10,8},{12,14},{14,12},{16,18},{18,... | collective-permute-start | bytes 294920 | tf_op jit(solution)/shard_map/ppermute | solution.py:362
  3.6 0.2 collective-permute-start.5
  3.8 1.1 %constant_dynamic-slice_fusion.8 = (bf16[384,128]{1,0:T(8,128)(2,1)S(1)}, bf16[384,128]{1,0:T(8,128)(2,1)S(1)}, bf16[384,128]{1,0:T(8,128)(2,1)S(1)}, bf16[384,128]{1,0:T(8,128)(2,1)S(1)}) fusion(bf16[384,512]{1,0:T(8,128)(2,1)} %param.6, s32[]{:T(128)S(6)} %select_n.31, s32[]{:T(128)S(6)} %select_n.29, s32[]{:T(128)S(6)} %select_n.28, s32[]{:T(128)S(6)} %select_n.30), kind=kLoop, calls=%fused_computation.8 | loop fusion | bytes 786448 | tf_op jit(solution)/shard_map/dynamic_slice | solution.py:357
  4.9 1.3 %collective-permute-start.2 = (bf16[384,128]{1,0:T(8,128)(2,1)S(1)}, bf16[384,128]{1,0:T(8,128)(2,1)S(1)}, u32[]{:S(2)}, u32[]{:S(2)}) collective-permute-start(bf16[384,128]{1,0:T(8,128)(2,1)S(1)} %get-tuple-element.51), channel_id=1, source_target_pairs={{0,6},{2,4},{4,2},{6,0},{8,14},{10,12},{12,10},{14,8},{16,22},{18,... | collective-permute-start | bytes 294920 | tf_op jit(solution)/shard_map/ppermute | solution.py:362
  6.2 1.2 %collective-permute-start = (bf16[384,128]{1,0:T(8,128)(2,1)S(1)}, bf16[384,128]{1,0:T(8,128)(2,1)S(1)}, u32[]{:S(2)}, u32[]{:S(2)}) collective-permute-start(bf16[384,128]{1,0:T(8,128)(2,1)S(1)} %get-tuple-element.52), channel_id=1, source_target_pairs={{0,2},{2,0},{4,6},{6,4},{8,10},{10,8},{12,14},{14,12},{16,18},{18,... | collective-permute-start | bytes 294920 | tf_op jit(solution)/shard_map/ppermute | solution.py:362
  7.4 0.0 collective-permute-done.6.refs_3_
  7.4 0.2 collective-permute-start.1
  7.6 0.3 collective-permute-done.4.refs_1_
  7.9 0.4 collective-permute-done.5.refs_2_
  8.4 3.2 %collective-permute-start.7 = (bf16[1536,128]{1,0:T(8,128)(2,1)S(1)}, bf16[1536,128]{1,0:T(8,128)(2,1)S(1)}, u32[]{:S(2)}, u32[]{:S(2)}) collective-permute-start(bf16[1536,128]{1,0:T(8,128)(2,1)S(1)} %shard_map.56.refs_7_.refs_9_), channel_id=1, source_target_pairs={{0,8},{2,10},{4,12},{6,14},{8,16},{10,18},{12,20},{14,22},{16,24},... | collective-permute-start | bytes 1179656 | tf_op jit(solution)/shard_map/ppermute | solution.py:365
  11.6 0.0 collective-permute-done.2.refs_3_
  11.6 0.0 collective-permute-done.refs_1_
  11.6 0.8 collective-permute-done.1.refs_2_
  12.5 3.2 %collective-permute-start.3 = (bf16[1536,128]{1,0:T(8,128)(2,1)S(1)}, bf16[1536,128]{1,0:T(8,128)(2,1)S(1)}, u32[]{:S(2)}, u32[]{:S(2)}) collective-permute-start(bf16[1536,128]{1,0:T(8,128)(2,1)S(1)} %shard_map.55.refs_5_.refs_6_.refs_4_), channel_id=1, source_target_pairs={{0,8},{2,10},{4,12},{6,14},{8,16},{10,18},{12,20},{14,22},{16,24},... | collective-permute-start | bytes 1179656 | tf_op jit(solution)/shard_map/ppermute | solution.py:365
  15.7 1.5 %constant_dynamic-slice_fusion = (bf16[384,512]{1,0:T(8,128)(2,1)S(1)}, bf16[384,512]{1,0:T(8,128)(2,1)S(1)}, bf16[384,512]{1,0:T(8,128)(2,1)S(1)}, bf16[384,512]{1,0:T(8,128)(2,1)S(1)}) fusion(bf16[384,2048]{1,0:T(8,128)(2,1)} %param.5, s32[]{:T(128)S(6)} %select_n.35, s32[]{:T(128)S(6)} %select_n.34, s32[]{:T(128)S(6)} %select_n.33, s32[]{:T(128)S(6)} %select_n.32), kind=kLoop, calls=%fused_computation | loop fusion | bytes 3145744 | tf_op jit(solution)/shard_map/dynamic_slice | solution.py:357
  17.2 0.4 collective-permute-start.8
  17.6 1.2 %collective-permute-start.10 = (bf16[384,512]{1,0:T(8,128)(2,1)S(1)}, bf16[384,512]{1,0:T(8,128)(2,1)S(1)}, u32[]{:S(2)}, u32[]{:S(2)}) collective-permute-start(bf16[384,512]{1,0:T(8,128)(2,1)S(1)} %get-tuple-element.44), channel_id=1, source_target_pairs={{0,2},{2,0},{4,6},{6,4},{8,10},{10,8},{12,14},{14,12},{16,18},{18,... | collective-permute-start | bytes 1179656 | tf_op jit(solution)/shard_map/ppermute | solution.py:362
  18.8 1.1 %collective-permute-start.9 = (bf16[384,512]{1,0:T(8,128)(2,1)S(1)}, bf16[384,512]{1,0:T(8,128)(2,1)S(1)}, u32[]{:S(2)}, u32[]{:S(2)}) collective-permute-start(bf16[384,512]{1,0:T(8,128)(2,1)S(1)} %get-tuple-element.45), channel_id=1, source_target_pairs={{0,4},{2,6},{4,0},{6,2},{8,12},{10,14},{12,8},{14,10},{16,20},{18,... | collective-permute-start | bytes 1179656 | tf_op jit(solution)/shard_map/ppermute | solution.py:362
  19.9 0.0 collective-permute-done.7.refs_6_.refs_8_
  19.9 6.9 %collective-permute-done.3.refs_4_.refs_5_.refs_3_ = bf16[1536,128]{1,0:T(8,128)(2,1)S(1)} collective-permute-done((bf16[1536,128]{1,0:T(8,128)(2,1)S(1)}, bf16[1536,128]{1,0:T(8,128)(2,1)S(1)}, u32[]{:S(2)}, u32[]{:S(2)}) %collective-permute-start.3) | collective-permute-done | bytes 393248 | tf_op jit(solution)/shard_map/ppermute | solution.py:365
  26.8 0.1 collective-permute-done.8.refs_1_
  26.9 3.1 %collective-permute-start.11 = (bf16[1536,128]{1,0:T(8,128)(2,1)S(1)}, bf16[1536,128]{1,0:T(8,128)(2,1)S(1)}, u32[]{:S(2)}, u32[]{:S(2)}) collective-permute-start(bf16[1536,128]{1,0:T(8,128)(2,1)S(1)} %collective-permute-done.3.refs_4_.refs_5_.refs_3_), channel_id=1, source_target_pairs={{0,8},{2,10},{4,12},{6,14},{8,16},{10,18},{12,20},{14,22},{16,24},... | collective-permute-start | bytes 1179656 | tf_op jit(solution)/shard_map/ppermute | solution.py:365
  30.0 1.9 %collective-permute-start.12 = (bf16[1536,128]{1,0:T(8,128)(2,1)S(1)}, bf16[1536,128]{1,0:T(8,128)(2,1)S(1)}, u32[]{:S(2)}, u32[]{:S(2)}) collective-permute-start(bf16[1536,128]{1,0:T(8,128)(2,1)S(1)} %collective-permute-done.7.refs_6_.refs_8_), channel_id=1, source_target_pairs={{0,8},{2,10},{4,12},{6,14},{8,16},{10,18},{12,20},{14,22},{16,24},... | collective-permute-start | bytes 1179656 | tf_op jit(solution)/shard_map/ppermute | solution.py:365
  31.9 2.2 %collective-permute-done.10.refs_3_ = bf16[384,512]{1,0:T(8,128)(2,1)S(1)} collective-permute-done((bf16[384,512]{1,0:T(8,128)(2,1)S(1)}, bf16[384,512]{1,0:T(8,128)(2,1)S(1)}, u32[]{:S(2)}, u32[]{:S(2)}) %collective-permute-start.10) | collective-permute-done | bytes 393248 | tf_op jit(solution)/shard_map/ppermute | solution.py:362
  34.1 3.5 %collective-permute-done.9.refs_2_ = bf16[384,512]{1,0:T(8,128)(2,1)S(1)} collective-permute-done((bf16[384,512]{1,0:T(8,128)(2,1)S(1)}, bf16[384,512]{1,0:T(8,128)(2,1)S(1)}, u32[]{:S(2)}, u32[]{:S(2)}) %collective-permute-start.9) | collective-permute-done | bytes 393248 | tf_op jit(solution)/shard_map/ppermute | solution.py:362
  37.6 0.0 copy-done
  37.6 20.9 %shard_map.57 = (bf16[384,512]{1,0:T(8,128)(2,1)S(1)}, bf16[384,512]{1,0:T(8,128)(2,1)S(1)}, bf16[384,512]{1,0:T(8,128)(2,1)S(1)}, f32[3,1536,256]{2,1,0:T(8,128)S(1)}, bf16[2048,4096]{1,0:T(8,128)(2,1)S(1)}) custom-call(s32[6]{0:T(128)S(1)} %copy-done, bf16[384,512]{1,0:T(8,128)(2,1)S(1)} %collective-permute-done.8.refs_1_, ...), custom_call_target="tpu_custom_call" | custom-call | flops 3623878656 | bytes 19136512 | tf_op jit(solution)/shard_map/pallas_call | solution.py:268
  58.5 0.0 collective-permute-done.11.refs_4_.refs_2_
  58.5 0.0 collective-permute-done.12.refs_7_.refs_5_
  58.5 0.9 shard_map.58
  59.4 0.1 collective-permute-start.15
  59.4 0.3 collective-permute-start.13
  59.7 2.4 %collective-permute-start.14 = (bf16[384,512]{1,0:T(8,128)(2,1)S(1)}, bf16[384,512]{1,0:T(8,128)(2,1)S(1)}, u32[]{:S(2)}, u32[]{:S(2)}) collective-permute-start(bf16[384,512]{1,0:T(8,128)(2,1)S(1)} %get-tuple-element.35), channel_id=1, source_target_pairs={{0,4},{2,6},{4,0},{6,2},{8,12},{10,14},{12,8},{14,10},{16,20},{18,... | collective-permute-start | bytes 1179656 | tf_op jit(solution)/shard_map/ppermute | solution.py:362
  62.1 6.3 %shard_map.59.refs_0_ = bf16[384,512]{1,0:T(8,128)(2,1)S(1)} custom-call(s32[6]{0:T(128)S(1)} %copy-done, bf16[384,512]{1,0:T(8,128)(2,1)S(1)} %get-tuple-element.38.refs_1_, bf16[1536,128]{1,0:T(8,128)(2,1)S(1)} %collective-permute-done.11.refs_4_.refs_2_, bf16[1536,128]{1,0:T(8,128)(2,1)S(1)} %collective-permute-done.3.refs_4_.refs_5_.refs_3_, ...), custom_call_target="tpu_custom_call" | custom-call | flops 1811939328 | bytes 786432 | tf_op jit(solution)/shard_map/pallas_call | solution.py:268
  68.4 2.1 %collective-permute-done.15.refs_1_ = bf16[384,512]{1,0:T(8,128)(2,1)S(1)} collective-permute-done((bf16[384,512]{1,0:T(8,128)(2,1)S(1)}, bf16[384,512]{1,0:T(8,128)(2,1)S(1)}, u32[]{:S(2)}, u32[]{:S(2)}) %collective-permute-start.15) | collective-permute-done | bytes 393248 | tf_op jit(solution)/shard_map/ppermute | solution.py:362
  70.6 4.7 %shard_map.60.refs_3_ = f32[384,4096]{1,0:T(8,128)S(1)} custom-call(bf16[384,512]{1,0:T(8,128)(2,1)S(1)} %shard_map.59.refs_0_, bf16[384,512]{1,0:T(8,128)(2,1)S(1)} %collective-permute-done.15.refs_1_, bf16[2048,4096]{1,0:T(8,128)(2,1)S(1)} %get-tuple-element.36.refs_2_), custom_call_target="tpu_custom_call" | custom-call | flops 3221225472 | bytes 6291456 | tf_op jit(solution)/shard_map/pallas_call | solution.py:325
  75.3 1.7 %collective-permute-done.13.refs_0_ = bf16[384,512]{1,0:T(8,128)(2,1)S(1)} collective-permute-done((bf16[384,512]{1,0:T(8,128)(2,1)S(1)}, bf16[384,512]{1,0:T(8,128)(2,1)S(1)}, u32[]{:S(2)}, u32[]{:S(2)}) %collective-permute-start.13) | collective-permute-done | bytes 393248 | tf_op jit(solution)/shard_map/ppermute | solution.py:362
  77.0 2.8 %collective-permute-done.14.refs_1_ = bf16[384,512]{1,0:T(8,128)(2,1)S(1)} collective-permute-done((bf16[384,512]{1,0:T(8,128)(2,1)S(1)}, bf16[384,512]{1,0:T(8,128)(2,1)S(1)}, u32[]{:S(2)}, u32[]{:S(2)}) %collective-permute-start.14) | collective-permute-done | bytes 393248 | tf_op jit(solution)/shard_map/ppermute | solution.py:362
  79.8 2.5 %shard_map.62 = (bf16[192,2048]{1,0:T(8,128)(2,1)S(1)}, bf16[192,2048]{1,0:T(8,128)(2,1)S(1)}) custom-call(bf16[384,512]{1,0:T(8,128)(2,1)S(1)} %collective-permute-done.13.refs_0_, bf16[384,512]{1,0:T(8,128)(2,1)S(1)} %collective-permute-done.14.refs_1_, bf16[2048,4096]{1,0:T(8,128)(2,1)S(1)} %get-tuple-element.36.refs_2_, f32[384,4096]{1,0:T(8,128)S(1)} %shard_map.60.refs_3_), custom_call_target="tpu_custom_call" | custom-call | flops 1610612736 | bytes 3145728 | tf_op jit(solution)/shard_map/pallas_call | solution.py:325
  82.3 0.6 collective-permute-start.17
  82.9 2.6 %shard_map.61 = (bf16[192,2048]{1,0:T(8,128)(2,1)S(1)}, bf16[192,2048]{1,0:T(8,128)(2,1)S(1)}) custom-call(bf16[384,512]{1,0:T(8,128)(2,1)S(1)} %collective-permute-done.13.refs_0_, bf16[384,512]{1,0:T(8,128)(2,1)S(1)} %collective-permute-done.14.refs_1_, bf16[2048,4096]{1,0:T(8,128)(2,1)S(1)} %get-tuple-element.36.refs_2_, f32[384,4096]{1,0:T(8,128)S(1)} %shard_map.60.refs_3_), custom_call_target="tpu_custom_call" | custom-call | flops 1610612736 | bytes 3145728 | tf_op jit(solution)/shard_map/pallas_call | solution.py:325
  85.5 0.1 collective-permute-start.16
  85.6 0.0 collective-permute-done.17.refs_3_
  85.6 2.2 %collective-permute-done.16.refs_2_ = bf16[192,2048]{1,0:T(8,128)(2,1)S(1)} collective-permute-done((bf16[192,2048]{1,0:T(8,128)(2,1)S(1)}, bf16[192,2048]{1,0:T(8,128)(2,1)S(1)}, u32[]{:S(2)}, u32[]{:S(2)}) %collective-permute-start.16) | collective-permute-done | bytes 786464 | tf_op jit(solution)/shard_map/ppermute | solution.py:419
  87.8 1.5 %shard_map.63 = bf16[192,4096]{1,0:T(8,128)(2,1)} custom-call(bf16[192,2048]{1,0:T(8,128)(2,1)S(1)} %get-tuple-element.39.refs_0_, bf16[192,2048]{1,0:T(8,128)(2,1)S(1)} %get-tuple-element.40.refs_1_, bf16[192,2048]{1,0:T(8,128)(2,1)S(1)} %collective-permute-done.16.refs_2_, bf16[192,2048]{1,0:T(8,128)(2,1)S(1)} %collective-permute-done.17.refs_3_), custom_call_target="tpu_custom_call" | custom-call | tf_op jit(solution)/shard_map/pallas_call | solution.py:420
  (2 shorter events, 0.1 us)
Async XLA Ops:
  0.0 37.6 %copy-start = (s32[6]{0:T(128)S(1)}, s32[6]{0:T(128)}, u32[]{:S(2)}) copy-start(s32[6]{0:T(128)} %refs_0_.5) | copy-start | bytes 76
  1.1 6.3 %collective-permute-start.6 = (bf16[384,128]{1,0:T(8,128)(2,1)S(1)}, bf16[384,128]{1,0:T(8,128)(2,1)S(1)}, u32[]{:S(2)}, u32[]{:S(2)}) collective-permute-start(bf16[384,128]{1,0:T(8,128)(2,1)S(1)} %get-tuple-element.47), channel_id=1, source_target_pairs={{0,6},{2,4},{4,2},{6,0},{8,14},{10,12},{12,10},{14,8},{16,22},{18,... | collective-permute-start | bytes 294920 | tf_op jit(solution)/shard_map/ppermute | solution.py:362
  2.4 5.5 %collective-permute-start.4 = (bf16[384,128]{1,0:T(8,128)(2,1)S(1)}, bf16[384,128]{1,0:T(8,128)(2,1)S(1)}, u32[]{:S(2)}, u32[]{:S(2)}) collective-permute-start(bf16[384,128]{1,0:T(8,128)(2,1)S(1)} %get-tuple-element.48), channel_id=1, source_target_pairs={{0,2},{2,0},{4,6},{6,4},{8,10},{10,8},{12,14},{14,12},{16,18},{18,... | collective-permute-start | bytes 294920 | tf_op jit(solution)/shard_map/ppermute | solution.py:362
  3.6 4.7 %collective-permute-start.5 = (bf16[384,128]{1,0:T(8,128)(2,1)S(1)}, bf16[384,128]{1,0:T(8,128)(2,1)S(1)}, u32[]{:S(2)}, u32[]{:S(2)}) collective-permute-start(bf16[384,128]{1,0:T(8,128)(2,1)S(1)} %get-tuple-element.50), channel_id=1, source_target_pairs={{0,4},{2,6},{4,0},{6,2},{8,12},{10,14},{12,8},{14,10},{16,20},{18,... | collective-permute-start | bytes 294920 | tf_op jit(solution)/shard_map/ppermute | solution.py:362
  4.9 6.7 %collective-permute-start.2 = (bf16[384,128]{1,0:T(8,128)(2,1)S(1)}, bf16[384,128]{1,0:T(8,128)(2,1)S(1)}, u32[]{:S(2)}, u32[]{:S(2)}) collective-permute-start(bf16[384,128]{1,0:T(8,128)(2,1)S(1)} %get-tuple-element.51), channel_id=1, source_target_pairs={{0,6},{2,4},{4,2},{6,0},{8,14},{10,12},{12,10},{14,8},{16,22},{18,... | collective-permute-start | bytes 294920 | tf_op jit(solution)/shard_map/ppermute | solution.py:362
  6.2 5.5 %collective-permute-start = (bf16[384,128]{1,0:T(8,128)(2,1)S(1)}, bf16[384,128]{1,0:T(8,128)(2,1)S(1)}, u32[]{:S(2)}, u32[]{:S(2)}) collective-permute-start(bf16[384,128]{1,0:T(8,128)(2,1)S(1)} %get-tuple-element.52), channel_id=1, source_target_pairs={{0,2},{2,0},{4,6},{6,4},{8,10},{10,8},{12,14},{14,12},{16,18},{18,... | collective-permute-start | bytes 294920 | tf_op jit(solution)/shard_map/ppermute | solution.py:362
  7.4 5.1 %collective-permute-start.1 = (bf16[384,128]{1,0:T(8,128)(2,1)S(1)}, bf16[384,128]{1,0:T(8,128)(2,1)S(1)}, u32[]{:S(2)}, u32[]{:S(2)}) collective-permute-start(bf16[384,128]{1,0:T(8,128)(2,1)S(1)} %get-tuple-element.54), channel_id=1, source_target_pairs={{0,4},{2,6},{4,0},{6,2},{8,12},{10,14},{12,8},{14,10},{16,20},{18,... | collective-permute-start | bytes 294920 | tf_op jit(solution)/shard_map/ppermute | solution.py:362
  8.4 11.5 %collective-permute-start.7 = (bf16[1536,128]{1,0:T(8,128)(2,1)S(1)}, bf16[1536,128]{1,0:T(8,128)(2,1)S(1)}, u32[]{:S(2)}, u32[]{:S(2)}) collective-permute-start(bf16[1536,128]{1,0:T(8,128)(2,1)S(1)} %shard_map.56.refs_7_.refs_9_), channel_id=1, source_target_pairs={{0,8},{2,10},{4,12},{6,14},{8,16},{10,18},{12,20},{14,22},{16,24},... | collective-permute-start | bytes 1179656 | tf_op jit(solution)/shard_map/ppermute | solution.py:365
  12.5 14.3 %collective-permute-start.3 = (bf16[1536,128]{1,0:T(8,128)(2,1)S(1)}, bf16[1536,128]{1,0:T(8,128)(2,1)S(1)}, u32[]{:S(2)}, u32[]{:S(2)}) collective-permute-start(bf16[1536,128]{1,0:T(8,128)(2,1)S(1)} %shard_map.55.refs_5_.refs_6_.refs_4_), channel_id=1, source_target_pairs={{0,8},{2,10},{4,12},{6,14},{8,16},{10,18},{12,20},{14,22},{16,24},... | collective-permute-start | bytes 1179656 | tf_op jit(solution)/shard_map/ppermute | solution.py:365
  17.2 9.7 %collective-permute-start.8 = (bf16[384,512]{1,0:T(8,128)(2,1)S(1)}, bf16[384,512]{1,0:T(8,128)(2,1)S(1)}, u32[]{:S(2)}, u32[]{:S(2)}) collective-permute-start(bf16[384,512]{1,0:T(8,128)(2,1)S(1)} %get-tuple-element.46), channel_id=1, source_target_pairs={{0,6},{2,4},{4,2},{6,0},{8,14},{10,12},{12,10},{14,8},{16,22},{18,... | collective-permute-start | bytes 1179656 | tf_op jit(solution)/shard_map/ppermute | solution.py:362
  17.6 16.5 %collective-permute-start.10 = (bf16[384,512]{1,0:T(8,128)(2,1)S(1)}, bf16[384,512]{1,0:T(8,128)(2,1)S(1)}, u32[]{:S(2)}, u32[]{:S(2)}) collective-permute-start(bf16[384,512]{1,0:T(8,128)(2,1)S(1)} %get-tuple-element.44), channel_id=1, source_target_pairs={{0,2},{2,0},{4,6},{6,4},{8,10},{10,8},{12,14},{14,12},{16,18},{18,... | collective-permute-start | bytes 1179656 | tf_op jit(solution)/shard_map/ppermute | solution.py:362
  18.8 18.8 %collective-permute-start.9 = (bf16[384,512]{1,0:T(8,128)(2,1)S(1)}, bf16[384,512]{1,0:T(8,128)(2,1)S(1)}, u32[]{:S(2)}, u32[]{:S(2)}) collective-permute-start(bf16[384,512]{1,0:T(8,128)(2,1)S(1)} %get-tuple-element.45), channel_id=1, source_target_pairs={{0,4},{2,6},{4,0},{6,2},{8,12},{10,14},{12,8},{14,10},{16,20},{18,... | collective-permute-start | bytes 1179656 | tf_op jit(solution)/shard_map/ppermute | solution.py:362
  26.9 31.6 %collective-permute-start.11 = (bf16[1536,128]{1,0:T(8,128)(2,1)S(1)}, bf16[1536,128]{1,0:T(8,128)(2,1)S(1)}, u32[]{:S(2)}, u32[]{:S(2)}) collective-permute-start(bf16[1536,128]{1,0:T(8,128)(2,1)S(1)} %collective-permute-done.3.refs_4_.refs_5_.refs_3_), channel_id=1, source_target_pairs={{0,8},{2,10},{4,12},{6,14},{8,16},{10,18},{12,20},{14,22},{16,24},... | collective-permute-start | bytes 1179656 | tf_op jit(solution)/shard_map/ppermute | solution.py:365
  30.0 28.5 %collective-permute-start.12 = (bf16[1536,128]{1,0:T(8,128)(2,1)S(1)}, bf16[1536,128]{1,0:T(8,128)(2,1)S(1)}, u32[]{:S(2)}, u32[]{:S(2)}) collective-permute-start(bf16[1536,128]{1,0:T(8,128)(2,1)S(1)} %collective-permute-done.7.refs_6_.refs_8_), channel_id=1, source_target_pairs={{0,8},{2,10},{4,12},{6,14},{8,16},{10,18},{12,20},{14,22},{16,24},... | collective-permute-start | bytes 1179656 | tf_op jit(solution)/shard_map/ppermute | solution.py:365
  59.4 11.2 %collective-permute-start.15 = (bf16[384,512]{1,0:T(8,128)(2,1)S(1)}, bf16[384,512]{1,0:T(8,128)(2,1)S(1)}, u32[]{:S(2)}, u32[]{:S(2)}) collective-permute-start(bf16[384,512]{1,0:T(8,128)(2,1)S(1)} %get-tuple-element.37), channel_id=1, source_target_pairs={{0,6},{2,4},{4,2},{6,0},{8,14},{10,12},{12,10},{14,8},{16,22},{18,... | collective-permute-start | bytes 1179656 | tf_op jit(solution)/shard_map/ppermute | solution.py:362
  59.4 17.6 %collective-permute-start.13 = (bf16[384,512]{1,0:T(8,128)(2,1)S(1)}, bf16[384,512]{1,0:T(8,128)(2,1)S(1)}, u32[]{:S(2)}, u32[]{:S(2)}) collective-permute-start(bf16[384,512]{1,0:T(8,128)(2,1)S(1)} %get-tuple-element.34), channel_id=1, source_target_pairs={{0,2},{2,0},{4,6},{6,4},{8,10},{10,8},{12,14},{14,12},{16,18},{18,... | collective-permute-start | bytes 1179656 | tf_op jit(solution)/shard_map/ppermute | solution.py:362
  59.7 20.1 %collective-permute-start.14 = (bf16[384,512]{1,0:T(8,128)(2,1)S(1)}, bf16[384,512]{1,0:T(8,128)(2,1)S(1)}, u32[]{:S(2)}, u32[]{:S(2)}) collective-permute-start(bf16[384,512]{1,0:T(8,128)(2,1)S(1)} %get-tuple-element.35), channel_id=1, source_target_pairs={{0,4},{2,6},{4,0},{6,2},{8,12},{10,14},{12,8},{14,10},{16,20},{18,... | collective-permute-start | bytes 1179656 | tf_op jit(solution)/shard_map/ppermute | solution.py:362
  82.3 3.2 %collective-permute-start.17 = (bf16[192,2048]{1,0:T(8,128)(2,1)S(1)}, bf16[192,2048]{1,0:T(8,128)(2,1)S(1)}, u32[]{:S(2)}, u32[]{:S(2)}) collective-permute-start(bf16[192,2048]{1,0:T(8,128)(2,1)S(1)} %get-tuple-element.42), channel_id=1, source_target_pairs={{0,1},{1,0},{2,3},{3,2},{4,5},{5,4},{6,7},{7,6},{8,9},{9,8},{10,11... | collective-permute-start | bytes 2359304 | tf_op jit(solution)/shard_map/ppermute | solution.py:419
  85.5 2.4 %collective-permute-start.16 = (bf16[192,2048]{1,0:T(8,128)(2,1)S(1)}, bf16[192,2048]{1,0:T(8,128)(2,1)S(1)}, u32[]{:S(2)}, u32[]{:S(2)}) collective-permute-start(bf16[192,2048]{1,0:T(8,128)(2,1)S(1)} %get-tuple-element.41), channel_id=1, source_target_pairs={{0,1},{1,0},{2,3},{3,2},{4,5},{5,4},{6,7},{7,6},{8,9},{9,8},{10,11... | collective-permute-start | bytes 2359304 | tf_op jit(solution)/shard_map/ppermute | solution.py:419

commit v4 on v3

--- a/solution.py
+++ b/solution.py
@@ -70,7 +70,7 @@
     outs = take(pieces)
     if early:
         state, w_to = take(2)
-    q_buf, o_buf, shift, total, in_sem, out_sem = refs
+    q_rows, o_buf, shift, total, out_sem = refs
     tokens = queries[0].shape[0]
     units = tokens // UNIT
     sizes = [key.shape[0] // UNIT for key in keys]
@@ -96,18 +96,21 @@
             starts.append(doc_first - first_unit)
         return here - first_unit, starts
 
-    def load():
-        run_copies([
-            pltpu.make_async_copy(queries[piece], q_buf.at[piece], in_sem.at[piece]) for piece in range(pieces)
-        ])
-
     def one_piece(piece):
         ones = jnp.ones((chunk, HD), jnp.bfloat16)
         square = jnp.ones((HD, HD), jnp.bfloat16)
         first_row, starts = place(piece)
         lows = [jnp.maximum(start, 0) for start in starts]
         low, high, stop = lows[0], lows[-1], first_row + units
-        query = jnp.concatenate([q_buf[piece, :, head * HD:(head + 1) * HD] for head in range(heads)], axis=0)
+
+        for number in range(pieces):
+
+            @pl.when(piece == number)
+            def _(number=number):
+                for head in range(heads):
+                    q_rows[head * tokens:(head + 1) * tokens, :] = queries[number][:, head * HD:(head + 1) * HD]
+
+        query = q_rows[...]
 
         def scores_of(region, number, masked, query):
             begin_unit = bases[region] + number * chunk_units
@@ -185,8 +188,7 @@
                 def careful(number, carry, region=region, first=first):
                     head = lax.rem(number, heads)
                     some = pl.ds(pl.multiple_of(head * tokens, tokens), tokens)
-                    query = q_buf[piece, :, pl.ds(pl.multiple_of(head * HD, HD), HD)]
-                    scores, value = scores_of(region, first + number // heads, True, query)
+                    scores, value = scores_of(region, first + number // heads, True, q_rows[some, :])
                     old = shift[some, :]
                     new = jnp.maximum(old, jnp.max(scores, axis=1, keepdims=True))
                     weights = jnp.exp2((scores - new[:, :1]) * scale).astype(jnp.bfloat16)
@@ -208,8 +210,6 @@
 
         @pl.when(sum(needs(jnp.int32(piece)).astype(jnp.int32) for piece in range(pieces)) > 0)
         def _():
-            load()
-
             def maybe(piece, carry):
                 @pl.when(needs(piece))
                 def _():
@@ -227,16 +227,19 @@
         if early:
             w_copy = pltpu.make_async_copy(w_from, w_to, out_sem.at[pieces])
             w_copy.start()
-        load()
-
         def always(piece, carry):
             one_piece(piece)
+            for number in range(pieces):
+
+                @pl.when(piece == number)
+                def _(number=number):
+                    pltpu.make_async_copy(o_buf.at[number], outs[number], out_sem.at[number]).start()
+
             return carry
 
         lax.fori_loop(0, pieces, always, 0)
-        run_copies([
-            pltpu.make_async_copy(o_buf.at[piece], outs[piece], out_sem.at[piece]) for piece in range(pieces)
-        ])
+        for number in range(pieces):
+            pltpu.make_async_copy(o_buf.at[number], outs[number], out_sem.at[number]).wait()
         if early:
             w_copy.wait()
 
@@ -250,7 +253,7 @@
     seen = sum(key.shape[0] for key in (keys[:1] if mode == "late" else keys))
     scores = rows * pieces * seen // 2
     operands = [doc_units, *queries, *keys, *values]
-    in_specs = [SMEM] + [HBM] * pieces + [VMEM] * (2 * regions)
+    in_specs = [SMEM] + [VMEM] * (pieces + 2 * regions)
     out_shape = [jax.ShapeDtypeStruct((tokens, width), jnp.bfloat16)] * pieces
     out_specs = [HBM] * pieces
     aliases = {}
@@ -271,11 +274,10 @@
         in_specs=in_specs,
         out_specs=out_specs,
         scratch_shapes=[
-            pltpu.VMEM((pieces, tokens, width), jnp.bfloat16),
+            pltpu.VMEM((rows, HD), jnp.bfloat16),
             pltpu.VMEM((pieces, tokens, width), jnp.bfloat16),
             pltpu.VMEM((rows, HD), jnp.float32),
             pltpu.VMEM((rows, 2 * HD), jnp.float32),
-            pltpu.SemaphoreType.DMA((pieces,)),
             pltpu.SemaphoreType.DMA((pieces + 1,)),
         ],
         input_output_aliases=aliases,
@@ -369,8 +371,8 @@
         return pack_rows(pieces) if group > 1 else pieces[0]
 
     keys, values = [own_plane(key_heads)], [own_plane(value_heads)]
-    queries = lax.optimization_barrier((queries, keys, values))[0]
-    query_pieces = [swap(column_block(queries, step, width), step) for step in range(group)]
+    blocks = lax.optimization_barrier(([column_block(queries, step, width) for step in range(group)], keys))[0]
+    query_pieces = [swap(blocks[step], step) for step in range(group)]
     keys = [next_plane(keys[0])] + keys
     values = [next_plane(values[0])] + values
     if group > 1:

time: 89.9 us -> 90.2 us (level)
  Pallas kernels: 39.5 us -> 34.3 us
  starting transfers between devices: 23 us -> 27.6 us
    pallas_call x3, Pallas kernels: 28.1 us -> 22.8 us  [attend(): pl.pallas_call(partial(attention_kernel, mode, steps, group, regions, hea...]
    ppermute x4, waiting for transfers between devices: 6.93 us -> 12 us  [next_plane(): lax.ppermute(value, 'ctx', [(source, source + group) for source in range(...]
    ppermute x12, starting transfers between devices: 10.8 us -> 15.6 us  [swap(): lax.ppermute(value, 'ctx', [(source, source ^ step) for source in range(c...]
    ppermute x12, waiting for transfers between devices: 13.9 us -> 9.11 us  [swap(): lax.ppermute(value, 'ctx', [(source, source ^ step) for source in range(c...]
    ppermute x4, starting transfers between devices: 11.5 us -> 10.2 us  [next_plane(): lax.ppermute(value, 'ctx', [(source, source + group) for source in range(...]
    ppermute x2, starting transfers between devices: 0.68 us -> 1.74 us  [shards(): gots.append(lax.ppermute(give, 'head', [(0, 1), (1, 0)]))]
  transfers between devices with their start and end apart: 18 -> 18, of which waited for: 11 -> 8; matrix products, arithmetic and copies ran while one was open for 3% -> 3% of each run, Pallas kernels for 39% -> 30%
where the time goes in v4:
time: 90.2 us; the launch traced here: 89 us
  Pallas kernels  34.3 us (38%)
  starting transfers between devices  27.6 us (31%)
  waiting for transfers between devices  23.3 us (26%)
  local copies, waits for them, and re-layouts  3.62 us (4%)
    pallas_call x3, Pallas kernels, attend(): pl.pallas_call(partial(attention_kernel, mode, steps, group, regions, hea...  22.8 us
    ppermute x12, starting transfers between devices, swap(): lax.ppermute(value, 'ctx', [(source, source ^ step) for source in range(c...  15.6 us
    ppermute x4, waiting for transfers between devices, next_plane(): lax.ppermute(value, 'ctx', [(source, source + group) for source in range(...  12 us
    ppermute x4, starting transfers between devices, next_plane(): lax.ppermute(value, 'ctx', [(source, source + group) for source in range(...  10.2 us
    pallas_call x3, Pallas kernels, project(): pl.pallas_call(partial(project_kernel, group, steps, first, tile, sums is...  9.87 us
    ppermute x12, waiting for transfers between devices, swap(): lax.ppermute(value, 'ctx', [(source, source ^ step) for source in range(c...  9.11 us
    dynamic_slice x3, local copies, waits for them, and re-layouts, column_block(): return lax.dynamic_slice(value, (0, (member ^ step) * size), (tokens, size))  3.62 us
    ppermute x2, waiting for transfers between devices, shards(): gots.append(lax.ppermute(give, 'head', [(0, 1), (1, 0)]))  2.23 us
  transfers between devices with their start and end apart: 18, of which 8 were waited for; matrix products, arithmetic and copies ran while one was open for 3% of the time, Pallas kernels for 30%

profile of v4, /device:TPU:19, one launch (start us, length us, event | category | flops | bytes accessed | tf_op | source)
XLA Modules:
  0.0 89.0 jit_solution(7011682915635357369)
XLA Ops:
  0.0 0.0 copy-start
  0.0 1.1 %constant_dynamic-slice_fusion.4 = (bf16[384,128]{1,0:T(8,128)(2,1)S(1)}, bf16[384,128]{1,0:T(8,128)(2,1)S(1)}, bf16[384,128]{1,0:T(8,128)(2,1)S(1)}, bf16[384,128]{1,0:T(8,128)(2,1)S(1)}) fusion(bf16[384,512]{1,0:T(8,128)(2,1)} %param.7, s32[]{:T(128)S(6)} %select_n.31, s32[]{:T(128)S(6)} %select_n.29, s32[]{:T(128)S(6)} %select_n.28, s32[]{:T(128)S(6)} %select_n.30), kind=kLoop, calls=%fused_computation.4 | loop fusion | bytes 786448 | tf_op jit(solution)/shard_map/dynamic_slice | solution.py:359
  1.1 1.3 %collective-permute-start.6 = (bf16[384,128]{1,0:T(8,128)(2,1)S(1)}, bf16[384,128]{1,0:T(8,128)(2,1)S(1)}, u32[]{:S(2)}, u32[]{:S(2)}) collective-permute-start(bf16[384,128]{1,0:T(8,128)(2,1)S(1)} %get-tuple-element.53), channel_id=1, source_target_pairs={{0,6},{2,4},{4,2},{6,0},{8,14},{10,12},{12,10},{14,8},{16,22},{18,... | collective-permute-start | bytes 294920 | tf_op jit(solution)/shard_map/ppermute | solution.py:364
  2.4 1.1 %constant_dynamic-slice_fusion.8 = (bf16[384,128]{1,0:T(8,128)(2,1)S(1)}, bf16[384,128]{1,0:T(8,128)(2,1)S(1)}, bf16[384,128]{1,0:T(8,128)(2,1)S(1)}, bf16[384,128]{1,0:T(8,128)(2,1)S(1)}) fusion(bf16[384,512]{1,0:T(8,128)(2,1)} %param.6, s32[]{:T(128)S(6)} %select_n.31, s32[]{:T(128)S(6)} %select_n.29, s32[]{:T(128)S(6)} %select_n.28, s32[]{:T(128)S(6)} %select_n.30), kind=kLoop, calls=%fused_computation.8 | loop fusion | bytes 786448 | tf_op jit(solution)/shard_map/dynamic_slice | solution.py:359
  3.4 1.2 %collective-permute-start.2 = (bf16[384,128]{1,0:T(8,128)(2,1)S(1)}, bf16[384,128]{1,0:T(8,128)(2,1)S(1)}, u32[]{:S(2)}, u32[]{:S(2)}) collective-permute-start(bf16[384,128]{1,0:T(8,128)(2,1)S(1)} %get-tuple-element.57), channel_id=1, source_target_pairs={{0,6},{2,4},{4,2},{6,0},{8,14},{10,12},{12,10},{14,8},{16,22},{18,... | collective-permute-start | bytes 294920 | tf_op jit(solution)/shard_map/ppermute | solution.py:364
  4.7 0.3 collective-permute-start
  4.9 1.2 %collective-permute-start.1 = (bf16[384,128]{1,0:T(8,128)(2,1)S(1)}, bf16[384,128]{1,0:T(8,128)(2,1)S(1)}, u32[]{:S(2)}, u32[]{:S(2)}) collective-permute-start(bf16[384,128]{1,0:T(8,128)(2,1)S(1)} %get-tuple-element.60), channel_id=1, source_target_pairs={{0,4},{2,6},{4,0},{6,2},{8,12},{10,14},{12,8},{14,10},{16,20},{18,... | collective-permute-start | bytes 294920 | tf_op jit(solution)/shard_map/ppermute | solution.py:364
  6.2 1.2 %collective-permute-start.4 = (bf16[384,128]{1,0:T(8,128)(2,1)S(1)}, bf16[384,128]{1,0:T(8,128)(2,1)S(1)}, u32[]{:S(2)}, u32[]{:S(2)}) collective-permute-start(bf16[384,128]{1,0:T(8,128)(2,1)S(1)} %get-tuple-element.54), channel_id=1, source_target_pairs={{0,2},{2,0},{4,6},{6,4},{8,10},{10,8},{12,14},{14,12},{16,18},{18,... | collective-permute-start | bytes 294920 | tf_op jit(solution)/shard_map/ppermute | solution.py:364
  7.4 0.0 collective-permute-done.6.refs_3_
  7.4 0.2 collective-permute-start.5
  7.6 1.5 %constant_dynamic-slice_fusion = (bf16[384,512]{1,0:T(8,128)(2,1)S(1)}, bf16[384,512]{1,0:T(8,128)(2,1)S(1)}, bf16[384,512]{1,0:T(8,128)(2,1)S(1)}, bf16[384,512]{1,0:T(8,128)(2,1)S(1)}) fusion(bf16[384,2048]{1,0:T(8,128)(2,1)} %param.5, s32[]{:T(128)S(6)} %select_n.35, s32[]{:T(128)S(6)} %select_n.33, s32[]{:T(128)S(6)} %select_n.32, s32[]{:T(128)S(6)} %select_n.34), kind=kLoop, calls=%fused_computation | loop fusion | bytes 3145744 | tf_op jit(solution)/shard_map/dynamic_slice | solution.py:359
  9.1 3.4 %collective-permute-done.4.refs_1_ = bf16[384,128]{1,0:T(8,128)(2,1)S(1)} collective-permute-done((bf16[384,128]{1,0:T(8,128)(2,1)S(1)}, bf16[384,128]{1,0:T(8,128)(2,1)S(1)}, u32[]{:S(2)}, u32[]{:S(2)}) %collective-permute-start.4) | collective-permute-done | bytes 98336 | tf_op jit(solution)/shard_map/ppermute | solution.py:364
  12.5 0.0 collective-permute-done.5.refs_2_
  12.5 3.2 %collective-permute-start.7 = (bf16[1536,128]{1,0:T(8,128)(2,1)S(1)}, bf16[1536,128]{1,0:T(8,128)(2,1)S(1)}, u32[]{:S(2)}, u32[]{:S(2)}) collective-permute-start(bf16[1536,128]{1,0:T(8,128)(2,1)S(1)} %shard_map.56.refs_7_.refs_9_), channel_id=1, source_target_pairs={{0,8},{2,10},{4,12},{6,14},{8,16},{10,18},{12,20},{14,22},{16,24},... | collective-permute-start | bytes 1179656 | tf_op jit(solution)/shard_map/ppermute | solution.py:367
  15.7 0.0 collective-permute-done.2.refs_3_
  15.7 0.0 collective-permute-done.refs_1_
  15.8 0.0 collective-permute-done.1.refs_2_
  15.8 1.9 %collective-permute-start.3 = (bf16[1536,128]{1,0:T(8,128)(2,1)S(1)}, bf16[1536,128]{1,0:T(8,128)(2,1)S(1)}, u32[]{:S(2)}, u32[]{:S(2)}) collective-permute-start(bf16[1536,128]{1,0:T(8,128)(2,1)S(1)} %shard_map.55.refs_5_.refs_6_.refs_4_), channel_id=1, source_target_pairs={{0,8},{2,10},{4,12},{6,14},{8,16},{10,18},{12,20},{14,22},{16,24},... | collective-permute-start | bytes 1179656 | tf_op jit(solution)/shard_map/ppermute | solution.py:367
  17.7 1.6 %collective-permute-start.8 = (bf16[384,512]{1,0:T(8,128)(2,1)S(1)}, bf16[384,512]{1,0:T(8,128)(2,1)S(1)}, u32[]{:S(2)}, u32[]{:S(2)}) collective-permute-start(bf16[384,512]{1,0:T(8,128)(2,1)S(1)} %get-tuple-element.27), channel_id=1, source_target_pairs={{0,6},{2,4},{4,2},{6,0},{8,14},{10,12},{12,10},{14,8},{16,22},{18,... | collective-permute-start | bytes 1179656 | tf_op jit(solution)/shard_map/ppermute | solution.py:364
  19.3 0.9 collective-permute-start.9
  20.2 0.3 collective-permute-start.10
  20.5 3.0 %collective-permute-done.7.refs_6_.refs_8_ = bf16[1536,128]{1,0:T(8,128)(2,1)S(1)} collective-permute-done((bf16[1536,128]{1,0:T(8,128)(2,1)S(1)}, bf16[1536,128]{1,0:T(8,128)(2,1)S(1)}, u32[]{:S(2)}, u32[]{:S(2)}) %collective-permute-start.7) | collective-permute-done | bytes 393248 | tf_op jit(solution)/shard_map/ppermute | solution.py:367
  23.4 8.4 %collective-permute-done.3.refs_4_.refs_5_.refs_3_ = bf16[1536,128]{1,0:T(8,128)(2,1)S(1)} collective-permute-done((bf16[1536,128]{1,0:T(8,128)(2,1)S(1)}, bf16[1536,128]{1,0:T(8,128)(2,1)S(1)}, u32[]{:S(2)}, u32[]{:S(2)}) %collective-permute-start.3) | collective-permute-done | bytes 393248 | tf_op jit(solution)/shard_map/ppermute | solution.py:367
  31.9 0.0 collective-permute-done.8.refs_1_
  31.9 3.2 %collective-permute-start.11 = (bf16[1536,128]{1,0:T(8,128)(2,1)S(1)}, bf16[1536,128]{1,0:T(8,128)(2,1)S(1)}, u32[]{:S(2)}, u32[]{:S(2)}) collective-permute-start(bf16[1536,128]{1,0:T(8,128)(2,1)S(1)} %collective-permute-done.3.refs_4_.refs_5_.refs_3_), channel_id=1, source_target_pairs={{0,8},{2,10},{4,12},{6,14},{8,16},{10,18},{12,20},{14,22},{16,24},... | collective-permute-start | bytes 1179656 | tf_op jit(solution)/shard_map/ppermute | solution.py:367
  35.1 1.9 %collective-permute-start.12 = (bf16[1536,128]{1,0:T(8,128)(2,1)S(1)}, bf16[1536,128]{1,0:T(8,128)(2,1)S(1)}, u32[]{:S(2)}, u32[]{:S(2)}) collective-permute-start(bf16[1536,128]{1,0:T(8,128)(2,1)S(1)} %collective-permute-done.7.refs_6_.refs_8_), channel_id=1, source_target_pairs={{0,8},{2,10},{4,12},{6,14},{8,16},{10,18},{12,20},{14,22},{16,24},... | collective-permute-start | bytes 1179656 | tf_op jit(solution)/shard_map/ppermute | solution.py:367
  37.0 1.2 %collective-permute-done.9.refs_2_ = bf16[384,512]{1,0:T(8,128)(2,1)S(1)} collective-permute-done((bf16[384,512]{1,0:T(8,128)(2,1)S(1)}, bf16[384,512]{1,0:T(8,128)(2,1)S(1)}, u32[]{:S(2)}, u32[]{:S(2)}) %collective-permute-start.9) | collective-permute-done | bytes 393248 | tf_op jit(solution)/shard_map/ppermute | solution.py:364
  38.2 0.0 collective-permute-done.10.refs_3_
  38.2 0.0 copy-done
  38.2 11.5 %shard_map.57 = (bf16[384,512]{1,0:T(8,128)(2,1)S(1)}, bf16[384,512]{1,0:T(8,128)(2,1)S(1)}, bf16[384,512]{1,0:T(8,128)(2,1)S(1)}, f32[3,1536,256]{2,1,0:T(8,128)S(1)}, bf16[2048,4096]{1,0:T(8,128)(2,1)S(1)}) custom-call(s32[6]{0:T(128)S(1)} %copy-done, bf16[384,512]{1,0:T(8,128)(2,1)S(1)} %collective-permute-done.8.refs_1_, ...), custom_call_target="tpu_custom_call" | custom-call | flops 3623878656 | bytes 19136512 | tf_op jit(solution)/shard_map/pallas_call | solution.py:271
  49.7 0.0 collective-permute-done.11.refs_4_.refs_2_
  49.7 0.6 collective-permute-done.12.refs_7_.refs_5_
  50.3 3.7 %shard_map.58 = (bf16[384,512]{1,0:T(8,128)(2,1)S(1)}, bf16[384,512]{1,0:T(8,128)(2,1)S(1)}, bf16[384,512]{1,0:T(8,128)(2,1)S(1)}) custom-call(s32[6]{0:T(128)S(1)} %copy-done, bf16[384,512]{1,0:T(8,128)(2,1)S(1)} %collective-permute-done.8.refs_1_, ...), custom_call_target="tpu_custom_call", output_to_operand_aliasing={{0}: (11, {}), {1}: (12, {}), {2}: (13, {})} | custom-call | flops 1811939328 | bytes 2359296 | tf_op jit(solution)/shard_map/pallas_call | solution.py:271
  54.0 6.5 %collective-permute-start.15 = (bf16[384,512]{1,0:T(8,128)(2,1)S(1)}, bf16[384,512]{1,0:T(8,128)(2,1)S(1)}, u32[]{:S(2)}, u32[]{:S(2)}) collective-permute-start(bf16[384,512]{1,0:T(8,128)(2,1)S(1)} %get-tuple-element.43), channel_id=1, source_target_pairs={{0,6},{2,4},{4,2},{6,0},{8,14},{10,12},{12,10},{14,8},{16,22},{18,... | collective-permute-start | bytes 1179656 | tf_op jit(solution)/shard_map/ppermute | solution.py:364
  60.5 1.0 %collective-permute-start.13 = (bf16[384,512]{1,0:T(8,128)(2,1)S(1)}, bf16[384,512]{1,0:T(8,128)(2,1)S(1)}, u32[]{:S(2)}, u32[]{:S(2)}) collective-permute-start(bf16[384,512]{1,0:T(8,128)(2,1)S(1)} %get-tuple-element.39), channel_id=1, source_target_pairs={{0,2},{2,0},{4,6},{6,4},{8,10},{10,8},{12,14},{14,12},{16,18},{18,... | collective-permute-start | bytes 1179656 | tf_op jit(solution)/shard_map/ppermute | solution.py:364
  61.5 0.0 collective-permute-start.14
  61.5 7.7 %shard_map.59.refs_0_ = bf16[384,512]{1,0:T(8,128)(2,1)S(1)} custom-call(s32[6]{0:T(128)S(1)} %copy-done, bf16[384,512]{1,0:T(8,128)(2,1)S(1)} %get-tuple-element.44.refs_1_, bf16[1536,128]{1,0:T(8,128)(2,1)S(1)} %collective-permute-done.11.refs_4_.refs_2_, bf16[1536,128]{1,0:T(8,128)(2,1)S(1)} %collective-permute-done.3.refs_4_.refs_5_.refs_3_, ...), custom_call_target="tpu_custom_call" | custom-call | flops 1811939328 | bytes 786432 | tf_op jit(solution)/shard_map/pallas_call | solution.py:271
  69.2 0.0 collective-permute-done.15.refs_1_
  69.2 4.8 %shard_map.60.refs_3_ = f32[384,4096]{1,0:T(8,128)S(1)} custom-call(bf16[384,512]{1,0:T(8,128)(2,1)S(1)} %shard_map.59.refs_0_, bf16[384,512]{1,0:T(8,128)(2,1)S(1)} %collective-permute-done.15.refs_1_, bf16[2048,4096]{1,0:T(8,128)(2,1)S(1)} %get-tuple-element.41.refs_2_), custom_call_target="tpu_custom_call" | custom-call | flops 3221225472 | bytes 6291456 | tf_op jit(solution)/shard_map/pallas_call | solution.py:327
  73.9 3.5 %collective-permute-done.13.refs_0_ = bf16[384,512]{1,0:T(8,128)(2,1)S(1)} collective-permute-done((bf16[384,512]{1,0:T(8,128)(2,1)S(1)}, bf16[384,512]{1,0:T(8,128)(2,1)S(1)}, u32[]{:S(2)}, u32[]{:S(2)}) %collective-permute-start.13) | collective-permute-done | bytes 393248 | tf_op jit(solution)/shard_map/ppermute | solution.py:364
  77.5 1.0 %collective-permute-done.14.refs_1_ = bf16[384,512]{1,0:T(8,128)(2,1)S(1)} collective-permute-done((bf16[384,512]{1,0:T(8,128)(2,1)S(1)}, bf16[384,512]{1,0:T(8,128)(2,1)S(1)}, u32[]{:S(2)}, u32[]{:S(2)}) %collective-permute-start.14) | collective-permute-done | bytes 393248 | tf_op jit(solution)/shard_map/ppermute | solution.py:364
  78.5 2.5 %shard_map.62 = (bf16[192,2048]{1,0:T(8,128)(2,1)S(1)}, bf16[192,2048]{1,0:T(8,128)(2,1)S(1)}) custom-call(bf16[384,512]{1,0:T(8,128)(2,1)S(1)} %collective-permute-done.13.refs_0_, bf16[384,512]{1,0:T(8,128)(2,1)S(1)} %collective-permute-done.14.refs_1_, bf16[2048,4096]{1,0:T(8,128)(2,1)S(1)} %get-tuple-element.41.refs_2_, f32[384,4096]{1,0:T(8,128)S(1)} %shard_map.60.refs_3_), custom_call_target="tpu_custom_call" | custom-call | flops 1610612736 | bytes 3145728 | tf_op jit(solution)/shard_map/pallas_call | solution.py:327
  81.0 1.6 %collective-permute-start.17 = (bf16[192,2048]{1,0:T(8,128)(2,1)S(1)}, bf16[192,2048]{1,0:T(8,128)(2,1)S(1)}, u32[]{:S(2)}, u32[]{:S(2)}) collective-permute-start(bf16[192,2048]{1,0:T(8,128)(2,1)S(1)} %get-tuple-element.48), channel_id=1, source_target_pairs={{0,1},{1,0},{2,3},{3,2},{4,5},{5,4},{6,7},{7,6},{8,9},{9,8},{10,11... | collective-permute-start | bytes 2359304 | tf_op jit(solution)/shard_map/ppermute | solution.py:421
  82.6 2.5 %shard_map.61 = (bf16[192,2048]{1,0:T(8,128)(2,1)S(1)}, bf16[192,2048]{1,0:T(8,128)(2,1)S(1)}) custom-call(bf16[384,512]{1,0:T(8,128)(2,1)S(1)} %collective-permute-done.13.refs_0_, bf16[384,512]{1,0:T(8,128)(2,1)S(1)} %collective-permute-done.14.refs_1_, bf16[2048,4096]{1,0:T(8,128)(2,1)S(1)} %get-tuple-element.41.refs_2_, f32[384,4096]{1,0:T(8,128)S(1)} %shard_map.60.refs_3_), custom_call_target="tpu_custom_call" | custom-call | flops 1610612736 | bytes 3145728 | tf_op jit(solution)/shard_map/pallas_call | solution.py:327
  85.2 0.1 collective-permute-start.16
  85.3 0.0 collective-permute-done.17.refs_3_
  85.3 2.2 %collective-permute-done.16.refs_2_ = bf16[192,2048]{1,0:T(8,128)(2,1)S(1)} collective-permute-done((bf16[192,2048]{1,0:T(8,128)(2,1)S(1)}, bf16[192,2048]{1,0:T(8,128)(2,1)S(1)}, u32[]{:S(2)}, u32[]{:S(2)}) %collective-permute-start.16) | collective-permute-done | bytes 786464 | tf_op jit(solution)/shard_map/ppermute | solution.py:421
  87.5 1.5 %shard_map.63 = bf16[192,4096]{1,0:T(8,128)(2,1)} custom-call(bf16[192,2048]{1,0:T(8,128)(2,1)S(1)} %get-tuple-element.45.refs_0_, bf16[192,2048]{1,0:T(8,128)(2,1)S(1)} %get-tuple-element.46.refs_1_, bf16[192,2048]{1,0:T(8,128)(2,1)S(1)} %collective-permute-done.16.refs_2_, bf16[192,2048]{1,0:T(8,128)(2,1)S(1)} %collective-permute-done.17.refs_3_), custom_call_target="tpu_custom_call" | custom-call | tf_op jit(solution)/shard_map/pallas_call | solution.py:422
  (2 shorter events, 0.1 us)
Async XLA Ops:
  0.0 38.2 %copy-start = (s32[6]{0:T(128)S(1)}, s32[6]{0:T(128)}, u32[]{:S(2)}) copy-start(s32[6]{0:T(128)} %refs_0_.5) | copy-start | bytes 76
  1.1 6.3 %collective-permute-start.6 = (bf16[384,128]{1,0:T(8,128)(2,1)S(1)}, bf16[384,128]{1,0:T(8,128)(2,1)S(1)}, u32[]{:S(2)}, u32[]{:S(2)}) collective-permute-start(bf16[384,128]{1,0:T(8,128)(2,1)S(1)} %get-tuple-element.53), channel_id=1, source_target_pairs={{0,6},{2,4},{4,2},{6,0},{8,14},{10,12},{12,10},{14,8},{16,22},{18,... | collective-permute-start | bytes 294920 | tf_op jit(solution)/shard_map/ppermute | solution.py:364
  3.4 12.3 %collective-permute-start.2 = (bf16[384,128]{1,0:T(8,128)(2,1)S(1)}, bf16[384,128]{1,0:T(8,128)(2,1)S(1)}, u32[]{:S(2)}, u32[]{:S(2)}) collective-permute-start(bf16[384,128]{1,0:T(8,128)(2,1)S(1)} %get-tuple-element.57), channel_id=1, source_target_pairs={{0,6},{2,4},{4,2},{6,0},{8,14},{10,12},{12,10},{14,8},{16,22},{18,... | collective-permute-start | bytes 294920 | tf_op jit(solution)/shard_map/ppermute | solution.py:364
  4.7 11.1 %collective-permute-start = (bf16[384,128]{1,0:T(8,128)(2,1)S(1)}, bf16[384,128]{1,0:T(8,128)(2,1)S(1)}, u32[]{:S(2)}, u32[]{:S(2)}) collective-permute-start(bf16[384,128]{1,0:T(8,128)(2,1)S(1)} %get-tuple-element.58), channel_id=1, source_target_pairs={{0,2},{2,0},{4,6},{6,4},{8,10},{10,8},{12,14},{14,12},{16,18},{18,... | collective-permute-start | bytes 294920 | tf_op jit(solution)/shard_map/ppermute | solution.py:364
  4.9 10.8 %collective-permute-start.1 = (bf16[384,128]{1,0:T(8,128)(2,1)S(1)}, bf16[384,128]{1,0:T(8,128)(2,1)S(1)}, u32[]{:S(2)}, u32[]{:S(2)}) collective-permute-start(bf16[384,128]{1,0:T(8,128)(2,1)S(1)} %get-tuple-element.60), channel_id=1, source_target_pairs={{0,4},{2,6},{4,0},{6,2},{8,12},{10,14},{12,8},{14,10},{16,20},{18,... | collective-permute-start | bytes 294920 | tf_op jit(solution)/shard_map/ppermute | solution.py:364
  6.2 6.3 %collective-permute-start.4 = (bf16[384,128]{1,0:T(8,128)(2,1)S(1)}, bf16[384,128]{1,0:T(8,128)(2,1)S(1)}, u32[]{:S(2)}, u32[]{:S(2)}) collective-permute-start(bf16[384,128]{1,0:T(8,128)(2,1)S(1)} %get-tuple-element.54), channel_id=1, source_target_pairs={{0,2},{2,0},{4,6},{6,4},{8,10},{10,8},{12,14},{14,12},{16,18},{18,... | collective-permute-start | bytes 294920 | tf_op jit(solution)/shard_map/ppermute | solution.py:364
  7.4 5.1 %collective-permute-start.5 = (bf16[384,128]{1,0:T(8,128)(2,1)S(1)}, bf16[384,128]{1,0:T(8,128)(2,1)S(1)}, u32[]{:S(2)}, u32[]{:S(2)}) collective-permute-start(bf16[384,128]{1,0:T(8,128)(2,1)S(1)} %get-tuple-element.56), channel_id=1, source_target_pairs={{0,4},{2,6},{4,0},{6,2},{8,12},{10,14},{12,8},{14,10},{16,20},{18,... | collective-permute-start | bytes 294920 | tf_op jit(solution)/shard_map/ppermute | solution.py:364
  12.5 10.9 %collective-permute-start.7 = (bf16[1536,128]{1,0:T(8,128)(2,1)S(1)}, bf16[1536,128]{1,0:T(8,128)(2,1)S(1)}, u32[]{:S(2)}, u32[]{:S(2)}) collective-permute-start(bf16[1536,128]{1,0:T(8,128)(2,1)S(1)} %shard_map.56.refs_7_.refs_9_), channel_id=1, source_target_pairs={{0,8},{2,10},{4,12},{6,14},{8,16},{10,18},{12,20},{14,22},{16,24},... | collective-permute-start | bytes 1179656 | tf_op jit(solution)/shard_map/ppermute | solution.py:367
  15.8 16.0 %collective-permute-start.3 = (bf16[1536,128]{1,0:T(8,128)(2,1)S(1)}, bf16[1536,128]{1,0:T(8,128)(2,1)S(1)}, u32[]{:S(2)}, u32[]{:S(2)}) collective-permute-start(bf16[1536,128]{1,0:T(8,128)(2,1)S(1)} %shard_map.55.refs_5_.refs_6_.refs_4_), channel_id=1, source_target_pairs={{0,8},{2,10},{4,12},{6,14},{8,16},{10,18},{12,20},{14,22},{16,24},... | collective-permute-start | bytes 1179656 | tf_op jit(solution)/shard_map/ppermute | solution.py:367
  17.7 14.1 %collective-permute-start.8 = (bf16[384,512]{1,0:T(8,128)(2,1)S(1)}, bf16[384,512]{1,0:T(8,128)(2,1)S(1)}, u32[]{:S(2)}, u32[]{:S(2)}) collective-permute-start(bf16[384,512]{1,0:T(8,128)(2,1)S(1)} %get-tuple-element.27), channel_id=1, source_target_pairs={{0,6},{2,4},{4,2},{6,0},{8,14},{10,12},{12,10},{14,8},{16,22},{18,... | collective-permute-start | bytes 1179656 | tf_op jit(solution)/shard_map/ppermute | solution.py:364
  19.3 18.9 %collective-permute-start.9 = (bf16[384,512]{1,0:T(8,128)(2,1)S(1)}, bf16[384,512]{1,0:T(8,128)(2,1)S(1)}, u32[]{:S(2)}, u32[]{:S(2)}) collective-permute-start(bf16[384,512]{1,0:T(8,128)(2,1)S(1)} %get-tuple-element.29), channel_id=1, source_target_pairs={{0,4},{2,6},{4,0},{6,2},{8,12},{10,14},{12,8},{14,10},{16,20},{18,... | collective-permute-start | bytes 1179656 | tf_op jit(solution)/shard_map/ppermute | solution.py:364
  20.2 18.0 %collective-permute-start.10 = (bf16[384,512]{1,0:T(8,128)(2,1)S(1)}, bf16[384,512]{1,0:T(8,128)(2,1)S(1)}, u32[]{:S(2)}, u32[]{:S(2)}) collective-permute-start(bf16[384,512]{1,0:T(8,128)(2,1)S(1)} %get-tuple-element.30), channel_id=1, source_target_pairs={{0,2},{2,0},{4,6},{6,4},{8,10},{10,8},{12,14},{14,12},{16,18},{18,... | collective-permute-start | bytes 1179656 | tf_op jit(solution)/shard_map/ppermute | solution.py:364
  31.9 17.8 %collective-permute-start.11 = (bf16[1536,128]{1,0:T(8,128)(2,1)S(1)}, bf16[1536,128]{1,0:T(8,128)(2,1)S(1)}, u32[]{:S(2)}, u32[]{:S(2)}) collective-permute-start(bf16[1536,128]{1,0:T(8,128)(2,1)S(1)} %collective-permute-done.3.refs_4_.refs_5_.refs_3_), channel_id=1, source_target_pairs={{0,8},{2,10},{4,12},{6,14},{8,16},{10,18},{12,20},{14,22},{16,24},... | collective-permute-start | bytes 1179656 | tf_op jit(solution)/shard_map/ppermute | solution.py:367
  35.1 15.2 %collective-permute-start.12 = (bf16[1536,128]{1,0:T(8,128)(2,1)S(1)}, bf16[1536,128]{1,0:T(8,128)(2,1)S(1)}, u32[]{:S(2)}, u32[]{:S(2)}) collective-permute-start(bf16[1536,128]{1,0:T(8,128)(2,1)S(1)} %collective-permute-done.7.refs_6_.refs_8_), channel_id=1, source_target_pairs={{0,8},{2,10},{4,12},{6,14},{8,16},{10,18},{12,20},{14,22},{16,24},... | collective-permute-start | bytes 1179656 | tf_op jit(solution)/shard_map/ppermute | solution.py:367
  54.0 15.2 %collective-permute-start.15 = (bf16[384,512]{1,0:T(8,128)(2,1)S(1)}, bf16[384,512]{1,0:T(8,128)(2,1)S(1)}, u32[]{:S(2)}, u32[]{:S(2)}) collective-permute-start(bf16[384,512]{1,0:T(8,128)(2,1)S(1)} %get-tuple-element.43), channel_id=1, source_target_pairs={{0,6},{2,4},{4,2},{6,0},{8,14},{10,12},{12,10},{14,8},{16,22},{18,... | collective-permute-start | bytes 1179656 | tf_op jit(solution)/shard_map/ppermute | solution.py:364
  60.5 17.0 %collective-permute-start.13 = (bf16[384,512]{1,0:T(8,128)(2,1)S(1)}, bf16[384,512]{1,0:T(8,128)(2,1)S(1)}, u32[]{:S(2)}, u32[]{:S(2)}) collective-permute-start(bf16[384,512]{1,0:T(8,128)(2,1)S(1)} %get-tuple-element.39), channel_id=1, source_target_pairs={{0,2},{2,0},{4,6},{6,4},{8,10},{10,8},{12,14},{14,12},{16,18},{18,... | collective-permute-start | bytes 1179656 | tf_op jit(solution)/shard_map/ppermute | solution.py:364
  61.5 17.0 %collective-permute-start.14 = (bf16[384,512]{1,0:T(8,128)(2,1)S(1)}, bf16[384,512]{1,0:T(8,128)(2,1)S(1)}, u32[]{:S(2)}, u32[]{:S(2)}) collective-permute-start(bf16[384,512]{1,0:T(8,128)(2,1)S(1)} %get-tuple-element.40), channel_id=1, source_target_pairs={{0,4},{2,6},{4,0},{6,2},{8,12},{10,14},{12,8},{14,10},{16,20},{18,... | collective-permute-start | bytes 1179656 | tf_op jit(solution)/shard_map/ppermute | solution.py:364
  81.0 4.3 %collective-permute-start.17 = (bf16[192,2048]{1,0:T(8,128)(2,1)S(1)}, bf16[192,2048]{1,0:T(8,128)(2,1)S(1)}, u32[]{:S(2)}, u32[]{:S(2)}) collective-permute-start(bf16[192,2048]{1,0:T(8,128)(2,1)S(1)} %get-tuple-element.48), channel_id=1, source_target_pairs={{0,1},{1,0},{2,3},{3,2},{4,5},{5,4},{6,7},{7,6},{8,9},{9,8},{10,11... | collective-permute-start | bytes 2359304 | tf_op jit(solution)/shard_map/ppermute | solution.py:421
  85.2 2.4 %collective-permute-start.16 = (bf16[192,2048]{1,0:T(8,128)(2,1)S(1)}, bf16[192,2048]{1,0:T(8,128)(2,1)S(1)}, u32[]{:S(2)}, u32[]{:S(2)}) collective-permute-start(bf16[192,2048]{1,0:T(8,128)(2,1)S(1)} %get-tuple-element.47), channel_id=1, source_target_pairs={{0,1},{1,0},{2,3},{3,2},{4,5},{5,4},{6,7},{7,6},{8,9},{9,8},{10,11... | collective-permute-start | bytes 2359304 | tf_op jit(solution)/shard_map/ppermute | solution.py:421
